TPU v7x, 32 devices: a whole 2x2x4 slice. The times are simulated.
32 devices in a mesh: gx: 4 (over z), gy: 4 (over y, x), gz: 2 (over core).
Axes of the slice: x: 2, y: 2, z: 4, core: 2. Of those that a mesh axis runs over, the one named last changes fastest.
Arguments:
- phi: bfloat16 [64, 128, 8, 512], P('gx', None, 'gy', 'gz'), may hold values from -6 to 6
- pot: float32 [64, 8, 512], P('gx', 'gy', 'gz'), may hold values from -1 to 1
- kern: bfloat16 [64, 16, 128, 128], P('gx'), may hold values from -0.06982422 to 0.06982422
- kern_hk: bfloat16 [64, 16, 128, 128], P('gx'), may hold values from -0.119628906 to 0.119628906
- slot_of: int32 [64, 16], P('gx'), may hold values from 0 to 31, as said below
- req_cols: int32 [128], P('gx'), may hold values from 0 to 63, as said below
Outputs:
- grad: bfloat16 [64, 128, 8, 512], P('gx', None, 'gy', 'gz')
Inputs may be any that keep to these rules, and one draw needn't show every extreme that they name: `slot_of`: each row's entries are distinct. `req_cols`: the 32 entries of group d are distinct, name columns of exactly 2 groups (d itself among them), exactly 16 of each, listed by increasing owning group; column c belongs to group c // 16.
All inputs are finite; a program needn't handle non-finite values.
Results may differ from a plain program's by a relative error of at most 0.011.
Values may be sent and summed in bfloat16 or wider, within the bound.
No kernel may reach another device: no remote copies, remote signals or barrier semaphores. Data moves between devices by JAX's collectives and lax.ppermute only.
A program may use at most 192 MiB of HBM per device.

v0:
```python
import jax
import jax.numpy as jnp
from jax import lax
from jax.sharding import PartitionSpec as P


def with_halo(block, sides, width):
    for axis, dim in sides:
        count = lax.axis_size(axis)
        forward = [(i, i + 1) for i in range(count - 1)]
        backward = [(target, source) for source, target in forward]
        low = lax.ppermute(
            lax.slice_in_dim(block, block.shape[dim] - width, None, axis=dim), axis, forward
        )
        high = lax.ppermute(lax.slice_in_dim(block, 0, width, axis=dim), axis, backward)
        block = jnp.concatenate([low, block, high], axis=dim)
    return block


def per_device(phi, pot, kern, kern_hk, slot_of, req_cols):
    padded = with_halo(phi, (("gy", 2), ("gz", 3)), 1).astype(jnp.float32)
    field = padded[:, :, 1:-1, 1:-1]
    beside_all = (
        padded[:, :, 2:, 1:-1]
        + padded[:, :, :-2, 1:-1]
        + padded[:, :, 1:-1, 2:]
        + padded[:, :, 1:-1, :-2]
    )
    action = (-0.5 * (beside_all - 4.0 * field) + pot[:, None, :, :] * field).astype(jnp.bfloat16)
    group_rows = kern.shape[0]
    listed = req_cols.shape[0]
    placed = (slot_of[:, :, None] == jnp.arange(listed, dtype=jnp.int32)[None, None, :]).astype(
        jnp.bfloat16
    )
    dense_kern = jnp.einsum(
        "iku,ikab->uiab", placed, kern, preferred_element_type=jnp.float32
    ).astype(jnp.bfloat16)
    dense_hk = jnp.einsum(
        "iku,ikab->uiab", placed, kern_hk, preferred_element_type=jnp.float32
    ).astype(jnp.bfloat16)
    partial_value = jnp.einsum(
        "uiab,iayz->ubyz", dense_kern, action, preferred_element_type=jnp.float32
    )
    partial_value = partial_value - jnp.einsum(
        "uiab,iayz->ubyz", dense_hk, phi, preferred_element_type=jnp.float32
    )
    partial_bf = partial_value.astype(jnp.bfloat16)
    select = (
        req_cols[:, None] == jnp.arange(group_rows * lax.axis_size("gx"), dtype=jnp.int32)[None, :]
    ).astype(jnp.bfloat16)
    total = lax.psum_scatter(
        jnp.einsum("ur,ubyz->rbyz", select, partial_bf, preferred_element_type=jnp.float32).astype(
            jnp.bfloat16
        ),
        "gx",
        scatter_dimension=0,
        tiled=True,
    ).astype(jnp.float32)
    return (2.0 * total).astype(jnp.bfloat16)


def solution(mesh):
    placed = (
        P("gx", None, "gy", "gz"),
        P("gx", "gy", "gz"),
        P("gx", None, None, None),
        P("gx", None, None, None),
        P("gx", None),
        P("gx"),
    )
    return jax.shard_map(
        per_device, mesh=mesh, in_specs=placed, out_specs=P("gx", None, "gy", "gz"), check_vma=False
    )
```

profile of v0, /device:TPU:0, one launch (start us, length us, event | category | flops | bytes accessed | tf_op | source)
XLA Modules:
  0.0 360.8 jit_solution(4260982954226969708)
XLA Ops:
  6.5 0.0 reduce-scatter.2.cloned.1.call-start
  6.5 5.6 %fusion.27 = (bf16[16,128,1,256]{3,2,1,0:T(2,128)(2,1)S(1)}, bf16[16,128,1,256]{3,2,1,0:T(2,128)(2,1)S(1)}) fusion(bf16[16,128,2,256]{3,2,1,0:T(2,128)(2,1)} %param.6), kind=kLoop, calls=%fused_computation.35 | loop fusion | bytes 4194304 | tf_op jit(solution)/shard_map/slice | solution.py:13
  12.2 0.0 copy-start
  12.2 0.2 copy.28
  12.4 0.0 copy-start.1
  12.4 1.4 collective-permute-start.1
  13.9 1.2 copy.27
  15.1 6.5 %collective-permute-start = (bf16[16,128,1,256]{3,1,2,0:T(8,128)(2,1)}, bf16[16,128,1,256]{3,1,2,0:T(8,128)(2,1)}, u32[]{:S(2)}, u32[]{:S(2)}) collective-permute-start(bf16[16,128,1,256]{3,1,2,0:T(8,128)(2,1)} %copy.27), channel_id=1, source_target_pairs={{0,2},{2,4},{4,6},{1,3},{3,5},{5,7},{8,10},{10,12},{12,14},{9,11},... | collective-permute-start | bytes 3145736 | tf_op jit(solution)/shard_map/ppermute | solution.py:12
  21.5 0.0 copy-done
  21.5 3.7 %copy.11 = bf16[16,128,2,256]{1,0,3,2:T(8,128)(2,1)} copy(bf16[16,128,2,256]{3,2,1,0:T(2,128)(2,1)S(1)} %copy-done) | data formatting | bytes 4194304 | tf_op args[0]
  25.2 0.0 copy-done.1
  25.2 12.9 %fusion.5 = bf16[16,32,128,128]{3,1,2,0:T(8,128)(2,1)} fusion(bf16[16,16,128,128]{3,2,1,0:T(8,128)(2,1)} %param.8, s32[16,16]{1,0:T(8,128)S(1)} %copy-done.1), kind=kOutput, calls=%fused_computation.8 | convolution fusion | flops 268443648 | bytes 25166848 | tf_op jit(solution)/shard_map/iku,ikab->uiab/dot_general | solution.py:35
  38.1 3.4 collective-permute-done.1
  41.5 1.9 copy.12
  43.4 0.0 collective-permute-done
  43.5 2.7 copy.10
  46.1 0.7 pad_maximum_fusion.2
  46.9 1.3 collective-permute-start.2
  48.1 0.0 copy-start.2
  48.2 1.5 collective-permute-start.3
  49.6 12.9 %fusion.3 = bf16[16,32,128,128]{3,1,2,0:T(8,128)(2,1)} fusion(bf16[16,16,128,128]{3,2,1,0:T(8,128)(2,1)} %param.9, s32[16,16]{1,0:T(8,128)S(1)} %copy-done.1), kind=kOutput, calls=%fused_computation.6 | convolution fusion | flops 268443648 | bytes 25166848 | tf_op jit(solution)/shard_map/iku,ikab->uiab/dot_general | solution.py:38
  62.5 0.0 copy-done.2
  62.6 0.1 copy.13
  62.7 17.5 %copy.44 = bf16[16,32,128,128]{3,2,1,0:T(8,128)(2,1)} copy(bf16[16,32,128,128]{3,1,2,0:T(8,128)(2,1)} %fusion.5) | data formatting | bytes 33554432 | tf_op jit(solution)/shard_map/iku,ikab->uiab/dot_general | solution.py:35
  80.2 23.7 %copy.18 = bf16[32,16,128,128,1]{2,0,1,4,3:T(8,128)(2,1)} copy(bf16[32,16,128,128,1]{3,2,0,1,4:T(8,128)(2,1)} %bitcast.36) | data formatting | bytes 33554432 | tf_op jit(solution)/shard_map/convert_element_type | solution.py:37
  103.9 17.5 %copy.45 = bf16[16,32,128,128]{3,2,1,0:T(8,128)(2,1)} copy(bf16[16,32,128,128]{3,1,2,0:T(8,128)(2,1)} %fusion.3) | data formatting | bytes 33554432 | tf_op jit(solution)/shard_map/iku,ikab->uiab/dot_general | solution.py:38
  121.4 23.4 %copy.23 = bf16[32,16,128,128,1]{2,0,1,4,3:T(8,128)(2,1)} copy(bf16[32,16,128,128,1]{3,2,0,1,4:T(8,128)(2,1)} %bitcast.37) | data formatting | bytes 33554432 | tf_op jit(solution)/shard_map/convert_element_type | solution.py:40
  144.8 0.0 collective-permute-done.2
  144.8 0.0 collective-permute-done.3
  144.8 0.0 slice-start
  144.8 0.0 slice-start.1
  144.8 2.6 maximum_convert_fusion
  147.3 0.0 slice-start.2
  147.4 0.0 slice-start.3
  147.4 3.4 fusion.18
  150.8 0.0 slice-done
  150.8 0.0 slice-done.1
  150.8 0.4 slice-done.2
  151.1 1.4 slice-done.3
  152.5 0.0 copy-start.3
  152.5 13.0 %fusion.16 = f32[32,128,2,256,1]{3,0,4,2,1:T(8,128)} fusion(bf16[32,16,128,128,1]{2,0,1,4,3:T(8,128)(2,1)S(1)} %bitcast.40, bf16[16,128,2,256,1]{1,0,3,2,4:T(8,128)(2,1)} %fusion.18), kind=kOutput, calls=%fused_computation.22 | convolution fusion | flops 8589934592 | bytes 27262976 | tf_op jit(solution)/shard_map/uiab,iayz->ubyz/dot_general | solution.py:41
  165.5 0.0 copy-done.3
  165.5 16.6 %convolution_convert_fusion = bf16[64,128,2,256]{3,0,2,1:T(8,128)(2,1)} fusion(f32[32,128,2,256,1]{3,0,4,2,1:T(8,128)} %fusion.16, bf16[32,16,128,128,1]{2,0,1,4,3:T(8,128)(2,1)} %copy.23, bf16[16,128,2,256,1]{3,2,1,0,4:T(2,128)(2,1)S(1)} %bitcast.38, s32[32]{0:T(128)S(1)} %copy-done.3), kind=kOutput, calls=%fused_computation.10 | convolution fusion | flops 8866760704 | bytes 35651712 | tf_op jit(solution)/shard_map/ur,ubyz->rbyz/dot_general | solution.py:52
  182.1 0.0 reduce-scatter.2.cloned.1.call-update
  182.1 166.5 %reduce-scatter.2.cloned.1.call-done = bf16[16,128,2,256]{3,0,2,1:T(8,128)(2,1)} async-done(((bf16[64,128,2,256]{3,0,2,1:T(8,128)(2,1)}), bf16[16,128,2,256]{3,0,2,1:T(8,128)(2,1)}) %reduce-scatter.2.cloned.1.call-update) | async-done | bytes 2097168 | tf_op jit(solution)/shard_map/reduce_scatter | solution.py:51
  348.6 2.1 multiply_convert_fusion
  350.7 3.2 copy.14
  (1 shorter events, 0.0 us)
Async XLA Ops:
  6.5 342.1 %reduce-scatter.2.cloned.1.call-start = ((), (), s32[]{:S(2)}) async-start(), calls=%async_computation.1 | async-start | bytes 10485760 | tf_op jit(solution)/shard_map/reduce_scatter | solution.py:51
  12.2 9.4 %copy-start = (bf16[16,128,2,256]{3,2,1,0:T(2,128)(2,1)S(1)}, bf16[16,128,2,256]{3,2,1,0:T(2,128)(2,1)}, u32[]{:S(2)}) copy-start(bf16[16,128,2,256]{3,2,1,0:T(2,128)(2,1)} %param.6) | copy-start | bytes 6291460
  12.4 12.8 %copy-start.1 = (s32[16,16]{1,0:T(8,128)S(1)}, s32[16,16]{1,0:T(8,128)}, u32[]{:S(2)}) copy-start(s32[16,16]{1,0:T(8,128)} %param.10) | copy-start | bytes 3076
  12.4 29.1 %collective-permute-start.1 = (bf16[16,128,1,256]{3,1,2,0:T(8,128)(2,1)S(1)}, bf16[16,128,1,256]{3,1,2,0:T(8,128)(2,1)}, u32[]{:S(2)}, u32[]{:S(2)}) collective-permute-start(bf16[16,128,1,256]{3,1,2,0:T(8,128)(2,1)S(1)} %copy.28), channel_id=1, source_target_pairs={{2,0},{4,2},{6,4},{3,1},{5,3},{7,5},{10,8},{12,10},{14,12},{11,9},... | collective-permute-start | bytes 3145736 | tf_op jit(solution)/shard_map/ppermute | solution.py:15
  15.1 28.4 %collective-permute-start = (bf16[16,128,1,256]{3,1,2,0:T(8,128)(2,1)}, bf16[16,128,1,256]{3,1,2,0:T(8,128)(2,1)}, u32[]{:S(2)}, u32[]{:S(2)}) collective-permute-start(bf16[16,128,1,256]{3,1,2,0:T(8,128)(2,1)} %copy.27), channel_id=1, source_target_pairs={{0,2},{2,4},{4,6},{1,3},{3,5},{5,7},{8,10},{10,12},{12,14},{9,11},... | collective-permute-start | bytes 3145736 | tf_op jit(solution)/shard_map/ppermute | solution.py:12
  46.9 97.9 %collective-permute-start.2 = (bf16[16,128,4,1]{1,0,3,2:T(8,128)(2,1)S(1)}, bf16[16,128,4,1]{1,0,3,2:T(8,128)(2,1)S(1)}, u32[]{:S(2)}, u32[]{:S(2)}) collective-permute-start(bf16[16,128,4,1]{1,0,3,2:T(8,128)(2,1)S(1)} %get-tuple-element.5), channel_id=1, source_target_pairs={{0,1},{2,3},{4,5},{6,7},{8,9},{10,11},{12,13},{14,15},{16,17},{18,... | collective-permute-start | bytes 49160 | tf_op jit(solution)/shard_map/ppermute | solution.py:12
  48.1 14.4 %copy-start.2 = (f32[16,2,256]{2,1,0:T(2,128)S(1)}, f32[16,2,256]{2,1,0:T(2,128)}, u32[]{:S(2)}) copy-start(f32[16,2,256]{2,1,0:T(2,128)} %param.7) | copy-start | bytes 98308
  48.2 96.6 %collective-permute-start.3 = (bf16[16,128,4,1]{1,0,3,2:T(8,128)(2,1)S(1)}, bf16[16,128,4,1]{1,0,3,2:T(8,128)(2,1)S(1)}, u32[]{:S(2)}, u32[]{:S(2)}) collective-permute-start(bf16[16,128,4,1]{1,0,3,2:T(8,128)(2,1)S(1)} %get-tuple-element.6), channel_id=1, source_target_pairs={{1,0},{3,2},{5,4},{7,6},{9,8},{11,10},{13,12},{15,14},{17,16},{19,... | collective-permute-start | bytes 49160 | tf_op jit(solution)/shard_map/ppermute | solution.py:15
  144.8 6.0 %slice-start = ((s8[16777216]{0:T(1024)(128)(4,1)}), s8[4194304]{0:T(1024)(128)(4,1)S(1)}, s32[]{:S(2)}) async-start(s8[16777216]{0:T(1024)(128)(4,1)} %bitcast.39), calls=%async_computation.2 | async-start | bytes 8388608
  144.8 6.0 %slice-start.1 = ((s8[16777216]{0:T(1024)(128)(4,1)}), s8[4194304]{0:T(1024)(128)(4,1)S(1)}, s32[]{:S(2)}) async-start(s8[16777216]{0:T(1024)(128)(4,1)} %bitcast.39), calls=%async_computation.3 | async-start | bytes 8388608
  147.3 3.8 %slice-start.2 = ((s8[16777216]{0:T(1024)(128)(4,1)}), s8[4194304]{0:T(1024)(128)(4,1)S(1)}, s32[]{:S(2)}) async-start(s8[16777216]{0:T(1024)(128)(4,1)} %bitcast.39), calls=%async_computation.4 | async-start | bytes 8388608
  147.4 5.2 %slice-start.3 = ((s8[16777216]{0:T(1024)(128)(4,1)}), s8[4194304]{0:T(1024)(128)(4,1)S(1)}, s32[]{:S(2)}) async-start(s8[16777216]{0:T(1024)(128)(4,1)} %bitcast.39), calls=%async_computation.5 | async-start | bytes 8388608
  152.5 13.0 %copy-start.3 = (s32[32]{0:T(128)S(1)}, s32[32]{0:T(128)}, u32[]{:S(2)}) copy-start(s32[32]{0:T(128)} %param.11) | copy-start | bytes 388
Sparse Core Ops, SparseCore 0:
  182.2 166.3 reduce-scatter.1
where the time goes:
time: 363 us; the launch traced here: 361 us
  waiting for transfers between devices  170 us (47%)
  local copies, waits for them, and re-layouts  103 us (28%)
  matrix products  55.4 us (15%)
  between operations  13.5 us (4%)
  starting transfers between devices  10.6 us (3%)
  other arithmetic  8.81 us (2%)
    reduce_scatter x1, waiting for transfers between devices, per_device(): lax.psum_scatter(jnp.einsum('ur,ubyz->rbyz', select, partial_bf, preferre...  167 us
    convert_element_type x1, local copies, waits for them, and re-layouts, per_device(): dense_kern = jnp.einsum('iku,ikab->uiab', placed, kern, preferred_element...  23.7 us
    convert_element_type x1, local copies, waits for them, and re-layouts, per_device(): dense_hk = jnp.einsum('iku,ikab->uiab', placed, kern_hk, preferred_elemen...  23.4 us
    dot_general x1, local copies, waits for them, and re-layouts, per_device(): jnp.einsum('iku,ikab->uiab', placed, kern, preferred_element_type=jnp.flo...  17.5 us
    dot_general x1, local copies, waits for them, and re-layouts, per_device(): jnp.einsum('iku,ikab->uiab', placed, kern_hk, preferred_element_type=jnp....  17.5 us
    dot_general x1, matrix products, per_device(): jnp.einsum('ur,ubyz->rbyz', select, partial_bf, preferred_element_type=jn...  16.6 us
    dot_general x1, matrix products, per_device(): jnp.einsum('uiab,iayz->ubyz', dense_kern, action, preferred_element_type=...  13 us
    dot_general x1, matrix products, per_device(): jnp.einsum('iku,ikab->uiab', placed, kern_hk, preferred_element_type=jnp....  12.9 us
  transfers between devices with their start and end apart: 5, of which 2 were waited for; matrix products, arithmetic and copies ran while one was open for 32% of the time, Pallas kernels for 0%

commit v1 on v0

v1 whole, which is shorter than its diff:
```python
import functools

import jax
import jax.numpy as jnp
import numpy as np
from jax import lax
from jax.experimental import pallas as pl
from jax.experimental.pallas import tpu as pltpu
from jax.sharding import PartitionSpec as P

CHUNKS = 2
LANES = 128
MIB = 1 << 20


def regroup_matrix(block, parts):
    rows = np.arange(block * parts)
    out = np.zeros((block * parts, block * parts), np.float32)
    out[rows, (rows % parts) * block + rows // parts] = 1.0
    return jnp.asarray(out, jnp.bfloat16)


def prepare_kernel(per_step, chunks, rows_y, tiles, phi_ref, mix_ref, *out_refs):
    block = mix_ref.shape[0]
    size = block // (tiles * rows_y)
    zc = tiles * LANES // chunks
    for step in range(per_step):
        part = phi_ref[step * block : (step + 1) * block, :]
        turned = lax.dot_general(
            part, mix_ref[...], (((0,), (0,)), ((), ())), preferred_element_type=jnp.float32
        ).astype(jnp.bfloat16)
        for chunk in range(chunks):
            tile, low = divmod(chunk * zc, LANES)
            for y in range(rows_y):
                at = (tile * rows_y + y) * size
                for more in range(max(1, zc // LANES)):
                    lane = at + more * rows_y * size
                    rows = min(zc, LANES)
                    out_refs[chunk * rows_y + y][step, more * LANES : more * LANES + rows, :] = turned[
                        low : low + rows, lane : lane + size
                    ]


def prepare(phi, chunks):
    groups, block, rows_y, rows_z = phi.shape
    tiles = rows_z // LANES
    flat = (
        phi.reshape(groups, block, rows_y, tiles, LANES)
        .transpose(0, 1, 3, 2, 4)
        .reshape(groups * block * tiles * rows_y, LANES)
    )
    parts = tiles * rows_y
    zc = rows_z // chunks
    per_step = 4
    outs = pl.pallas_call(
        functools.partial(prepare_kernel, per_step, chunks, rows_y, tiles),
        grid=(groups // per_step,),
        in_specs=[
            pl.BlockSpec((per_step * block * parts, LANES), lambda s: (s, 0)),
            pl.BlockSpec((block * parts, block * parts), lambda s: (0, 0)),
        ],
        out_specs=[pl.BlockSpec((per_step, zc, block), lambda s: (s, 0, 0))] * (chunks * rows_y),
        out_shape=[jax.ShapeDtypeStruct((groups, zc, block), jnp.bfloat16)] * (chunks * rows_y),
        name="prepare",
    )(flat, regroup_matrix(block, parts))
    return [[outs[c * rows_y + y] for y in range(rows_y)] for c in range(chunks)]


def gather_kernel(cols, groups, which_ref, kern_ref, hk_ref, out_ref, zero_ref, sem):
    zero_ref[...] = jnp.zeros_like(zero_ref)

    @pl.loop(0, cols)
    def _(col):
        for row in range(groups):
            at = which_ref[col * groups + row]

            @pl.when(at >= 0)
            def _():
                pltpu.make_async_copy(kern_ref.at[row, at], out_ref.at[col, row, 0], sem).start()
                pltpu.make_async_copy(hk_ref.at[row, at], out_ref.at[col, row, 1], sem).start()

            @pl.when(at < 0)
            def _():
                pltpu.make_async_copy(zero_ref, out_ref.at[col, row, 0], sem).start()
                pltpu.make_async_copy(zero_ref, out_ref.at[col, row, 1], sem).start()

    pltpu.make_async_copy(out_ref, out_ref, sem).wait()


def gather_blocks(kern, kern_hk, which):
    cols, groups = which.shape
    block = kern.shape[-1]
    shape = (cols, groups, 2, block, block)
    return pl.pallas_call(
        functools.partial(gather_kernel, cols, groups),
        grid_spec=pltpu.PrefetchScalarGridSpec(
            num_scalar_prefetch=1,
            grid=(1,),
            in_specs=[pl.BlockSpec(memory_space=pl.ANY)] * 2,
            out_specs=pl.BlockSpec(memory_space=pl.ANY),
            scratch_shapes=[pltpu.VMEM((block, block), jnp.bfloat16), pltpu.SemaphoreType.DMA(())],
        ),
        out_shape=jax.ShapeDtypeStruct(shape, jnp.bfloat16),
        cost_estimate=pl.CostEstimate(flops=0, transcendentals=0, bytes_accessed=4 * int(np.prod(shape))),
        name="gather_blocks",
    )(which.reshape(-1), kern, kern_hk)


def fill_operand(groups, rows_y, x_ref, y_refs, prev_ref, next_ref, low_ref, high_ref, pot_ref):
    zc, block = y_refs[0].shape[1:]
    z = lax.broadcasted_iota(jnp.int32, (zc, block), 0)
    for row in range(groups):
        fields = [ref[row].astype(jnp.float32) for ref in y_refs]
        above = [prev_ref[row].astype(jnp.float32)] + fields[:-1]
        below = fields[1:] + [next_ref[row].astype(jnp.float32)]
        for y, field in enumerate(fields):
            low = low_ref[y, row : row + 1, :].astype(jnp.float32)
            high = high_ref[y, row : row + 1, :].astype(jnp.float32)
            left = jnp.where(z == 0, low, pltpu.roll(field, 1, 0))
            right = jnp.where(z == zc - 1, high, pltpu.roll(field, zc - 1, 0))
            beside = below[y] + above[y] + right + left
            pot = pot_ref[y * zc : (y + 1) * zc, row : row + 1]
            action = -0.5 * (beside - 4.0 * field) + pot * field
            x_ref[y * zc : (y + 1) * zc, row * 2 * block : row * 2 * block + block] = action.astype(jnp.bfloat16)
            x_ref[y * zc : (y + 1) * zc, row * 2 * block + block : (row + 1) * 2 * block] = -y_refs[y][row]


def columns_of(x, w_ref):
    pair = [w_ref[j].reshape(-1, w_ref.shape[-1]) for j in range(2)]
    return jnp.dot(x, jnp.concatenate(pair, axis=1), preferred_element_type=jnp.float32)


def store_pair(out_ref, value):
    block = out_ref.shape[-1]
    for j in range(2):
        out_ref[j] = value[:, j * block : (j + 1) * block].astype(jnp.bfloat16)


def first_kernel(groups, rows_y, split, *refs):
    y_refs = refs[:rows_y]
    prev_ref, next_ref, low_ref, high_ref, pot_ref, w_ref, x_ref = refs[rows_y : rows_y + 7]
    outs = refs[rows_y + 7 :]
    pair = pl.program_id(0)

    @pl.when(pair == 0)
    def _():
        fill_operand(groups, rows_y, x_ref, y_refs, prev_ref, next_ref, low_ref, high_ref, pot_ref)

    value = columns_of(x_ref[...], w_ref)
    if len(outs) == 1:
        store_pair(outs[0], value)
    else:

        @pl.when(pair < split)
        def _():
            store_pair(outs[0], value)

        @pl.when(pair >= split)
        def _():
            store_pair(outs[1], value)


def first_columns(fields, prev, after, low, high, pot, blocks, halves):
    rows_y = len(fields)
    groups, zc, block = fields[0].shape
    cols = blocks.shape[0]
    pairs = cols // 2
    n = rows_y * zc
    depth = groups * 2 * block
    whole = lambda *shape: pl.BlockSpec(shape, lambda p: (0,) * len(shape))
    split = pairs // 2
    if halves == 2:
        out_specs = [
            pl.BlockSpec((2, n, block), lambda p: (jnp.minimum(p, split - 1), 0, 0)),
            pl.BlockSpec((2, n, block), lambda p: (jnp.maximum(p - split, 0), 0, 0)),
        ]
    else:
        out_specs = [pl.BlockSpec((2, n, block), lambda p: (p, 0, 0))]
    return pl.pallas_call(
        functools.partial(first_kernel, groups, rows_y, split),
        grid=(pairs,),
        in_specs=[whole(groups, zc, block)] * (rows_y + 2)
        + [whole(rows_y, groups, block)] * 2
        + [whole(n, groups), pl.BlockSpec((2, groups, 2, block, block), lambda p: (p, 0, 0, 0, 0))],
        out_specs=[whole(n, depth)] + out_specs,
        out_shape=[jax.ShapeDtypeStruct((n, depth), jnp.bfloat16)]
        + [jax.ShapeDtypeStruct((cols // halves, n, block), jnp.bfloat16)] * halves,
        compiler_params=pltpu.CompilerParams(vmem_limit_bytes=40 * MIB),
        cost_estimate=pl.CostEstimate(
            flops=2 * n * depth * cols * block, transcendentals=0, bytes_accessed=2 * depth * cols * block
        ),
        name="first_columns",
    )(*fields, prev, after, low, high, pot, blocks)


def local_kernel(chunks, *refs):
    x_refs, w_ref, out_refs = refs[:chunks], refs[chunks], refs[chunks + 1 :]
    for x_ref, out_ref in zip(x_refs, out_refs):
        store_pair(out_ref, columns_of(x_ref[...], w_ref))


def local_columns(xs, blocks):
    cols, groups, _, block, _ = blocks.shape
    n, depth = xs[0].shape
    return pl.pallas_call(
        functools.partial(local_kernel, len(xs)),
        grid=(cols // 2,),
        in_specs=[pl.BlockSpec((n, depth), lambda p: (0, 0))] * len(xs)
        + [pl.BlockSpec((2, groups, 2, block, block), lambda p: (p, 0, 0, 0, 0))],
        out_specs=[pl.BlockSpec((2, n, block), lambda p: (p, 0, 0))] * len(xs),
        out_shape=[jax.ShapeDtypeStruct((cols, n, block), jnp.bfloat16)] * len(xs),
        compiler_params=pltpu.CompilerParams(vmem_limit_bytes=40 * MIB),
        cost_estimate=pl.CostEstimate(
            flops=2 * n * len(xs) * depth * cols * block, transcendentals=0, bytes_accessed=2 * depth * cols * block
        ),
        name="local_columns",
    )(*xs, blocks)


def write_columns(rows_y, tiles, values, mix_ref, out_ref, at):
    chunks = len(values)
    zc = values[0].shape[0] // rows_y
    parts = []
    for tile in range(tiles):
        for y in range(rows_y):
            pieces = []
            for chunk in range(chunks):
                first, last = chunk * zc, (chunk + 1) * zc
                lo, hi = max(first, tile * LANES), min(last, (tile + 1) * LANES)
                if lo < hi:
                    pieces.append(values[chunk][y * zc + lo - first : y * zc + hi - first, :])
            parts.append(jnp.concatenate(pieces, axis=0) if len(pieces) > 1 else pieces[0])
    turned = jnp.concatenate([(2.0 * part).astype(jnp.bfloat16) for part in parts], axis=1)
    rows = mix_ref.shape[0]
    out_ref[at * rows : (at + 1) * rows, :] = lax.dot_general(
        mix_ref[...], turned, (((1,), (1,)), ((), ())), preferred_element_type=jnp.float32
    ).astype(jnp.bfloat16)


def final_kernel(per_step, chunks, rows_y, tiles, flags_ref, mix_ref, *refs):
    own, right2, left1, left2, right1 = (refs[k * chunks : (k + 1) * chunks] for k in range(5))
    out_ref = refs[5 * chunks]
    step = pl.program_id(0)
    half = pl.num_programs(0) // 2

    def emit(added, maybe, flag):
        for col in range(per_step):
            values = []
            for chunk in range(chunks):
                extra = jnp.where(flag == 1, maybe[chunk][col].astype(jnp.float32), 0.0)
                values.append(
                    own[chunk][col].astype(jnp.float32) + added[chunk][col].astype(jnp.float32) + extra
                )
            write_columns(rows_y, tiles, values, mix_ref, out_ref, col)

    @pl.when(step < half)
    def _():
        emit(right2, left1, flags_ref[0])

    @pl.when(step >= half)
    def _():
        emit(left2, right1, flags_ref[1])


def finish(flags, own, right2, left1, left2, right1, rows_y, rows_z):
    chunks = len(own)
    cols, n, block = own[0].shape
    tiles = rows_z // LANES
    rows = block * tiles * rows_y
    per_step = 2
    steps = cols // per_step
    half = steps // 2
    all_cols = pl.BlockSpec((per_step, n, block), lambda s, f: (s, 0, 0))
    low_cols = pl.BlockSpec((per_step, n, block), lambda s, f: (jnp.minimum(s, half - 1), 0, 0))
    high_cols = pl.BlockSpec((per_step, n, block), lambda s, f: (jnp.maximum(s - half, 0), 0, 0))
    flat = pl.pallas_call(
        functools.partial(final_kernel, per_step, chunks, rows_y, tiles),
        grid_spec=pltpu.PrefetchScalarGridSpec(
            num_scalar_prefetch=1,
            grid=(steps,),
            in_specs=[pl.BlockSpec((rows, rows), lambda s, f: (0, 0))]
            + [all_cols] * chunks
            + [low_cols] * (2 * chunks)
            + [high_cols] * (2 * chunks),
            out_specs=pl.BlockSpec((per_step * rows, LANES), lambda s, f: (s, 0)),
        ),
        out_shape=jax.ShapeDtypeStruct((cols * rows, LANES), jnp.bfloat16),
        name="finish",
    )(flags, regroup_matrix(block, tiles * rows_y), *own, *right2, *left1, *left2, *right1)
    return unflatten(flat, cols, block, rows_y, tiles)


def unflatten(flat, cols, block, rows_y, tiles):
    return (
        flat.reshape(cols, block, tiles, rows_y, LANES)
        .transpose(0, 1, 3, 2, 4)
        .reshape(cols, block, rows_y, tiles * LANES)
    )


def plain_kernel(per_step, chunks, rows_y, tiles, mix_ref, *refs):
    for col in range(per_step):
        values = [refs[chunk][col].astype(jnp.float32) for chunk in range(chunks)]
        write_columns(rows_y, tiles, values, mix_ref, refs[chunks], col)


def finish_plain(totals, rows_y, rows_z):
    chunks = len(totals)
    cols, n, block = totals[0].shape
    tiles = rows_z // LANES
    rows = block * tiles * rows_y
    per_step = 2
    flat = pl.pallas_call(
        functools.partial(plain_kernel, per_step, chunks, rows_y, tiles),
        grid=(cols // per_step,),
        in_specs=[pl.BlockSpec((rows, rows), lambda s: (0, 0))]
        + [pl.BlockSpec((per_step, n, block), lambda s: (s, 0, 0))] * chunks,
        out_specs=pl.BlockSpec((per_step * rows, LANES), lambda s: (s, 0)),
        out_shape=jax.ShapeDtypeStruct((cols * rows, LANES), jnp.bfloat16),
        name="finish",
    )(regroup_matrix(block, tiles * rows_y), *totals)
    return unflatten(flat, cols, block, rows_y, tiles)


def block_of_column(slot_of, slots):
    hit = slot_of[None, :, :] == slots[:, None, None]
    index = jnp.arange(1, slot_of.shape[1] + 1, dtype=jnp.int32)
    return jnp.sum(jnp.where(hit, index, 0), axis=2) - 1


def shifts(axis, by):
    count = lax.axis_size(axis)
    return [(i, i + by) for i in range(count) if 0 <= i + by < count]


def per_device(phi, pot, kern, kern_hk, slot_of, req_cols):
    groups, block, rows_y, rows_z = phi.shape
    listed = req_cols.shape[0]
    ring = lax.axis_size("gx")
    chunks = CHUNKS
    zc = rows_z // chunks

    fields = prepare(phi, chunks)
    edge_low = jnp.stack([fields[0][y][:, 0, :] for y in range(rows_y)])
    edge_high = jnp.stack([fields[-1][y][:, -1, :] for y in range(rows_y)])
    from_low = lax.ppermute(edge_high, "gz", shifts("gz", 1))
    from_high = lax.ppermute(edge_low, "gz", shifts("gz", -1))
    halo = [
        (
            lax.ppermute(fields[c][-1], "gy", shifts("gy", 1)),
            lax.ppermute(fields[c][0], "gy", shifts("gy", -1)),
        )
        for c in range(chunks)
    ]
    lows = [from_low] + [
        jnp.stack([fields[c - 1][y][:, -1, :] for y in range(rows_y)]) for c in range(1, chunks)
    ]
    highs = [
        jnp.stack([fields[c + 1][y][:, 0, :] for y in range(rows_y)]) for c in range(chunks - 1)
    ] + [from_high]
    pots = [
        pot[:, :, c * zc : (c + 1) * zc].reshape(groups, rows_y * zc).T for c in range(chunks)
    ]

    if ring != 4:
        which = block_of_column(slot_of, jnp.arange(listed, dtype=jnp.int32))
        blocks = gather_blocks(kern, kern_hk, which)
        hit = req_cols[None, :] == jnp.arange(groups * ring, dtype=jnp.int32)[:, None]
        named = jnp.any(hit, axis=1)
        source = jnp.sum(jnp.where(hit, jnp.arange(listed, dtype=jnp.int32), 0), axis=1)
        totals = []
        for c in range(chunks):
            _, part = first_columns(fields[c], *halo[c], lows[c], highs[c], pots[c], blocks, 1)
            spread = jnp.where(named[:, None, None], part[source], 0)
            totals.append(lax.psum_scatter(spread, "gx", scatter_dimension=0, tiled=True))
        return finish_plain(totals, rows_y, rows_z)

    me = lax.axis_index("gx")
    owners = req_cols // groups
    other = jnp.where(owners[0] == me, owners[listed - 1], owners[0])
    away = (other - me) % ring
    ahead = [(i, (i + 1) % ring) for i in range(ring)]
    behind = [(i, (i - 1) % ring) for i in range(ring)]
    left_away = lax.ppermute(away.reshape(1), "gx", ahead)[0]
    right_away = lax.ppermute(away.reshape(1), "gx", behind)[0]

    half = groups // 2
    column = jnp.arange(groups, dtype=jnp.int32)
    swapped = jnp.where(away == 2, column, (column + half) % groups)
    wanted = jnp.concatenate([other * groups + swapped, me * groups + column])
    slots = jnp.sum(
        jnp.where(wanted[:, None] == req_cols[None, :], jnp.arange(listed, dtype=jnp.int32), 0), axis=1
    )
    which = block_of_column(slot_of, slots)
    far_blocks = gather_blocks(kern, kern_hk, which[:groups])
    near_blocks = gather_blocks(kern, kern_hk, which[groups:])

    xs, sent, right1, left1, right2, left2 = [], [], [], [], [], []
    for c in range(chunks):
        x, q0, q1 = first_columns(fields[c], *halo[c], lows[c], highs[c], pots[c], far_blocks, 2)
        xs.append(x)
        sent.append((q0, q1))
        right1.append(lax.ppermute(q0, "gx", ahead))
        left1.append(lax.ppermute(q1, "gx", behind))
    own = local_columns(xs, near_blocks)
    for c in range(chunks):
        q0, q1 = sent[c]

        def onward(mine, is_mine, arrived, is_through):
            kept = jnp.where(is_mine, mine.astype(jnp.float32), 0.0)
            through = jnp.where(is_through, arrived.astype(jnp.float32), 0.0)
            return (kept + through).astype(jnp.bfloat16)

        right2.append(lax.ppermute(onward(q1, away == 1, right1[c], left_away == 2), "gx", ahead))
        left2.append(lax.ppermute(onward(q0, away == ring - 1, left1[c], right_away == 2), "gx", behind))
    flags = jnp.stack([right_away == ring - 1, left_away == 1]).astype(jnp.int32)
    return finish(flags, own, right2, left1, left2, right1, rows_y, rows_z)


def solution(mesh):
    placed = (
        P("gx", None, "gy", "gz"),
        P("gx", "gy", "gz"),
        P("gx", None, None, None),
        P("gx", None, None, None),
        P("gx", None),
        P("gx"),
    )
    return jax.shard_map(
        per_device, mesh=mesh, in_specs=placed, out_specs=P("gx", None, "gy", "gz"), check_vma=False
    )
```

time: 363 us -> 694 us (1.91); the launches traced: 361 us -> 705 us
  Pallas kernels: 0 us -> 565 us
  waiting for transfers between devices: 170 us -> 34.1 us
  local copies, waits for them, and re-layouts: 103 us -> 18.4 us
  starting transfers between devices: 10.6 us -> 78 us
  matrix products: 55.4 us -> 0 us
  between operations: 13.5 us -> 4.57 us
    pallas_call x0 -> x7, Pallas kernels: none -> 565 us  [the longest x2 512 us: gather_blocks(): pl.pallas_call(functools.partial(gather_kernel, cols, groups), grid_spec=...]
    reduce_scatter x1 -> x0, waiting for transfers between devices: 167 us -> none  [per_device(): lax.psum_scatter(jnp.einsum('ur,ubyz->rbyz', select, partial_bf, preferre...]
    ppermute x4 -> x16, starting transfers between devices: 10.6 us -> 78 us  [the longest x2 35.1 us: per_device(): left1.append(lax.ppermute(q1, 'gx', behind))]
    dot_general x4 -> x0, matrix products: 55.4 us -> none  [the longest x1 16.6 us: per_device(): jnp.einsum('ur,ubyz->rbyz', select, partial_bf, preferred_element_type=jn...]
    convert_element_type x3 -> x0, local copies, waits for them, and re-layouts: 50.2 us -> none  [the longest x1 23.7 us: per_device(): dense_kern = jnp.einsum('iku,ikab->uiab', placed, kern, preferred_element...]
    dot_general x2 -> x0, local copies, waits for them, and re-layouts: 35.1 us -> none  [the longest x1 17.5 us: per_device(): jnp.einsum('iku,ikab->uiab', placed, kern, preferred_element_type=jnp.flo...]
    ppermute x4 -> x16, waiting for transfers between devices: 3.39 us -> 34.1 us  [the longest x2 18.9 us: per_device(): lax.ppermute(onward(q0, away == ring - 1, left1[c], right_away == 2), 'gx...]
  transfers between devices with their start and end apart: 5 -> 16, of which waited for: 2 -> 4; matrix products, arithmetic and copies ran while one was open for 32% -> 2% of each run, Pallas kernels for 0% -> 78%
where the time goes in v1:
time: 694 us; the launch traced here: 705 us
  Pallas kernels  565 us (81%)
  starting transfers between devices  78 us (11%)
  waiting for transfers between devices  34.1 us (5%)
  local copies, waits for them, and re-layouts  18.4 us (3%)
    pallas_call x2, Pallas kernels, gather_blocks(): pl.pallas_call(functools.partial(gather_kernel, cols, groups), grid_spec=...  512 us
    ppermute x2, starting transfers between devices, per_device(): left1.append(lax.ppermute(q1, 'gx', behind))  35.1 us
    pallas_call x2, Pallas kernels, first_columns(): pl.pallas_call(functools.partial(first_kernel, groups, rows_y, split), gr...  25.5 us
    ppermute x2, waiting for transfers between devices, per_device(): lax.ppermute(onward(q0, away == ring - 1, left1[c], right_away == 2), 'gx...  18.9 us
    ppermute x2, waiting for transfers between devices, per_device(): left1.append(lax.ppermute(q1, 'gx', behind))  15.2 us
  transfers between devices with their start and end apart: 16, of which 4 were waited for; matrix products, arithmetic and copies ran while one was open for 2% of the time, Pallas kernels for 78%

profile of v1, /device:TPU:0, one launch (start us, length us, event | category | flops | bytes accessed | tf_op | source)
XLA Modules:
  0.0 704.9 jit_solution(7381809205620702215)
XLA Ops:
  0.0 4.8 prepare.1
  4.8 4.9 collective-permute-start.2
  9.7 1.3 collective-permute-start.3
  11.0 4.6 collective-permute-start.5
  15.6 1.3 collective-permute-start.6
  16.9 1.4 copy.35
  18.2 1.4 copy.34
  19.7 1.3 collective-permute-start.4
  21.0 0.7 and_select_fusion.1
  21.6 0.6 fusion.4
  24.1 1.4 copy.41
  25.5 1.4 copy.40
  27.0 0.8 select_reduce_fusion.1
  27.8 0.8 select_reduce_fusion
  28.7 0.7 fusion.2
  29.7 0.7 reshape.46.which_ref
  30.5 270.0 %gather_blocks.2.refs_7_ = bf16[16,16,2,128,128]{4,3,2,1,0:T(8,128)(2,1)} custom-call(s32[256]{0:T(256)} %reshape.46.which_ref, bf16[16,16,128,128]{3,2,1,0:T(8,128)(2,1)} %kern_ref.3, bf16[16,16,128,128]{3,2,1,0:T(8,128)(2,1)} %hk_ref.3), custom_call_target="tpu_custom_call" | custom-call | bytes 33554432 | tf_op jit(solution)/shard_map/gather_blocks/pallas_call | solution.py:94
  300.5 1.3 collective-permute-start.7
  301.8 12.8 %first_columns.2 = (bf16[256,4096]{1,0:T(8,128)(2,1)S(1)}, bf16[8,256,128]{2,1,0:T(8,128)(2,1)}, bf16[8,256,128]{2,1,0:T(8,128)(2,1)S(1)}) custom-call(bf16[16,128,128]{2,1,0:T(8,128)(2,1)S(1)} %copy-done.2, bf16[16,128,128]{2,1,0:T(8,128)(2,1)S(1)} %copy-done.3, bf16[16,128,128]{2,1,0:T(8,128)(2,1)S(1)} %collective-permute-done.2.refs_2_, ...), custom_call_target="tpu_custom_call" | custom-call | flops 4294967296 | bytes 16777216 | tf_op jit(solution)/shard_map/first_columns/pallas_call | solution.py:179
  314.6 0.8 copy-done.6
  315.4 12.7 %first_columns.3 = (bf16[256,4096]{1,0:T(8,128)(2,1)S(1)}, bf16[8,256,128]{2,1,0:T(8,128)(2,1)S(1)}, bf16[8,256,128]{2,1,0:T(8,128)(2,1)S(1)}) custom-call(bf16[16,128,128]{2,1,0:T(8,128)(2,1)S(1)} %copy-done, bf16[16,128,128]{2,1,0:T(8,128)(2,1)S(1)} %copy-done.1, bf16[16,128,128]{2,1,0:T(8,128)(2,1)S(1)} %collective-permute-done.5.refs_2_, ...), custom_call_target="tpu_custom_call" | custom-call | flops 4294967296 | bytes 16777216 | tf_op jit(solution)/shard_map/first_columns/pallas_call | solution.py:179
  328.2 1.3 copy-done.10
  329.5 12.0 %collective-permute-start.1 = (s32[1]{0:T(128)}, s32[1]{0:T(128)}, u32[]{:S(2)}, u32[]{:S(2)}) collective-permute-start(s32[1]{0:T(128)} %bitcast.2), channel_id=1, source_target_pairs={{0,8},{8,16},{16,24},{24,0},{1,9},{9,17},{17,25},{25,1},{2,10},{10... | collective-permute-start | bytes 20 | tf_op jit(solution)/shard_map/ppermute | solution.py:384
  341.5 5.3 collective-permute-start
  346.9 0.7 reshape.48.which_ref
  347.6 242.2 %gather_blocks.3.refs_2_ = bf16[16,16,2,128,128]{4,3,2,1,0:T(8,128)(2,1)} custom-call(s32[256]{0:T(256)} %reshape.48.which_ref, bf16[16,16,128,128]{3,2,1,0:T(8,128)(2,1)} %kern_ref.3, bf16[16,16,128,128]{3,2,1,0:T(8,128)(2,1)} %hk_ref.3), custom_call_target="tpu_custom_call" | custom-call | bytes 33554432 | tf_op jit(solution)/shard_map/gather_blocks/pallas_call | solution.py:94
  592.2 0.6 add_convert_fusion.4.flags_ref
  592.8 35.1 %collective-permute-start.12 = (bf16[8,256,128]{2,1,0:T(8,128)(2,1)S(1)}, bf16[8,256,128]{2,1,0:T(8,128)(2,1)S(1)}, u32[]{:S(2)}, u32[]{:S(2)}) collective-permute-start(bf16[8,256,128]{2,1,0:T(8,128)(2,1)S(1)} %copy-done.7), channel_id=1, source_target_pairs={{0,24},{8,0},{16,8},{24,16},{1,25},{9,1},{17,9},{25,17},{2,26},{10... | collective-permute-start | bytes 1572872 | tf_op jit(solution)/shard_map/ppermute | solution.py:404
  627.9 0.2 add_convert_fusion.3
  628.1 2.0 collective-permute-start.9
  630.2 0.2 add_convert_fusion.2
  630.5 9.8 %collective-permute-done.12.refs_4_ = bf16[8,256,128]{2,1,0:T(8,128)(2,1)S(1)} collective-permute-done((bf16[8,256,128]{2,1,0:T(8,128)(2,1)S(1)}, bf16[8,256,128]{2,1,0:T(8,128)(2,1)S(1)}, u32[]{:S(2)}, u32[]{:S(2)}) %collective-permute-start.12) | collective-permute-done | bytes 524320 | tf_op jit(solution)/shard_map/ppermute | solution.py:404
  640.3 1.4 add_convert_fusion.1
  641.7 4.4 collective-permute-start.14
  646.2 5.4 collective-permute-done.13.refs_5_
  651.5 0.2 add_convert_fusion
  651.7 4.3 collective-permute-start.15
  656.1 1.6 copy-done.9
  657.7 1.6 copy-done.11
  659.3 12.8 %local_columns.1 = (bf16[16,256,128]{2,1,0:T(8,128)(2,1)S(1)}, bf16[16,256,128]{2,1,0:T(8,128)(2,1)S(1)}) custom-call(bf16[256,4096]{1,0:T(8,128)(2,1)S(1)} %copy-done.9, bf16[256,4096]{1,0:T(8,128)(2,1)S(1)} %copy-done.11, bf16[16,16,2,128,128]{4,3,2,1,0:T(8,128)(2,1)} %gather_blocks.3.refs_2_), custom_call_target="tpu_custom_call" | custom-call | flops 8589934592 | bytes 16777216 | tf_op jit(solution)/shard_map/local_columns/pallas_call | solution.py:205
  672.2 1.0 copy-done.4
  673.1 1.0 copy-done.5
  674.1 0.8 copy-done.16
  674.9 0.8 copy-done.17
  675.7 9.5 %collective-permute-done.14.refs_6_ = bf16[8,256,128]{2,1,0:T(8,128)(2,1)S(1)} collective-permute-done((bf16[8,256,128]{2,1,0:T(8,128)(2,1)S(1)}, bf16[8,256,128]{2,1,0:T(8,128)(2,1)S(1)}, u32[]{:S(2)}, u32[]{:S(2)}) %collective-permute-start.14) | collective-permute-done | bytes 524320 | tf_op jit(solution)/shard_map/ppermute | solution.py:415
  685.2 9.3 %collective-permute-done.15.refs_7_ = bf16[8,256,128]{2,1,0:T(8,128)(2,1)S(1)} collective-permute-done((bf16[8,256,128]{2,1,0:T(8,128)(2,1)S(1)}, bf16[8,256,128]{2,1,0:T(8,128)(2,1)S(1)}, u32[]{:S(2)}, u32[]{:S(2)}) %collective-permute-start.15) | collective-permute-done | bytes 524320 | tf_op jit(solution)/shard_map/ppermute | solution.py:415
  694.6 0.8 copy-done.19
  695.4 9.5 %finish.1 = bf16[8192,128]{1,0:T(8,128)(2,1)} custom-call(s32[2]{0:T(128)} %add_convert_fusion.4.flags_ref, bf16[512,512]{1,0:T(8,128)(2,1)} %constant.65.clone.mix_ref, bf16[16,256,128]{2,1,0:T(8,128)(2,1)} %copy-done.4, bf16[16,256,128]{2,1,0:T(8,128)(2,1)} %copy-done.5, bf16[8,256,128]{2,1,0:T(8,128)(2,1)} %copy-done.16, bf16[8,256,128]{2,1,0:T(8,128)(2,1)} %copy-done.17, ...), custom_call_target="tpu_custom_call" | custom-call | tf_op jit(solution)/shard_map/finish/pallas_call | solution.py:276
  (65 shorter events, 0.8 us)
Async XLA Ops:
  4.8 297.0 %collective-permute-start.2 = (bf16[16,128,128]{2,1,0:T(8,128)(2,1)}, bf16[16,128,128]{2,1,0:T(8,128)(2,1)S(1)}, u32[]{:S(2)}, u32[]{:S(2)}) collective-permute-start(bf16[16,128,128]{2,1,0:T(8,128)(2,1)} %get-tuple-element.18.refs_1_), channel_id=1, source_target_pairs={{0,2},{2,4},{4,6},{1,3},{3,5},{5,7},{8,10},{10,12},{12,14},{9,11},... | collective-permute-start | bytes 1572872 | tf_op jit(solution)/shard_map/ppermute | solution.py:350
  9.7 292.1 %collective-permute-start.3 = (bf16[16,128,128]{2,1,0:T(8,128)(2,1)}, bf16[16,128,128]{2,1,0:T(8,128)(2,1)S(1)}, u32[]{:S(2)}, u32[]{:S(2)}) collective-permute-start(bf16[16,128,128]{2,1,0:T(8,128)(2,1)} %get-tuple-element.17.refs_0_), channel_id=1, source_target_pairs={{2,0},{4,2},{6,4},{3,1},{5,3},{7,5},{10,8},{12,10},{14,12},{11,9},... | collective-permute-start | bytes 1572872 | tf_op jit(solution)/shard_map/ppermute | solution.py:351
  11.0 304.4 %collective-permute-start.5 = (bf16[16,128,128]{2,1,0:T(8,128)(2,1)}, bf16[16,128,128]{2,1,0:T(8,128)(2,1)S(1)}, u32[]{:S(2)}, u32[]{:S(2)}) collective-permute-start(bf16[16,128,128]{2,1,0:T(8,128)(2,1)} %get-tuple-element.20.refs_1_), channel_id=1, source_target_pairs={{0,2},{2,4},{4,6},{1,3},{3,5},{5,7},{8,10},{10,12},{12,14},{9,11},... | collective-permute-start | bytes 1572872 | tf_op jit(solution)/shard_map/ppermute | solution.py:350
  15.6 299.8 %collective-permute-start.6 = (bf16[16,128,128]{2,1,0:T(8,128)(2,1)}, bf16[16,128,128]{2,1,0:T(8,128)(2,1)S(1)}, u32[]{:S(2)}, u32[]{:S(2)}) collective-permute-start(bf16[16,128,128]{2,1,0:T(8,128)(2,1)} %get-tuple-element.19.refs_0_), channel_id=1, source_target_pairs={{2,0},{4,2},{6,4},{3,1},{5,3},{7,5},{10,8},{12,10},{14,12},{11,9},... | collective-permute-start | bytes 1572872 | tf_op jit(solution)/shard_map/ppermute | solution.py:351
  19.7 280.8 %collective-permute-start.4 = (bf16[2,16,128]{2,1,0:T(8,128)(2,1)S(1)}, bf16[2,16,128]{2,1,0:T(8,128)(2,1)S(1)}, u32[]{:S(2)}, u32[]{:S(2)}) collective-permute-start(bf16[2,16,128]{2,1,0:T(8,128)(2,1)S(1)} %pad_maximum_fusion), channel_id=1, source_target_pairs={{0,1},{2,3},{4,5},{6,7},{8,9},{10,11},{12,13},{14,15},{16,17},{18,... | collective-permute-start | bytes 24584 | tf_op jit(solution)/shard_map/ppermute | solution.py:346
  30.4 271.3 %copy-start.2 = (bf16[16,128,128]{2,1,0:T(8,128)(2,1)S(1)}, bf16[16,128,128]{2,1,0:T(8,128)(2,1)}, u32[]{:S(2)}) copy-start(bf16[16,128,128]{2,1,0:T(8,128)(2,1)} %get-tuple-element.17.refs_0_) | copy-start | bytes 1572868
  30.5 271.3 %copy-start.3 = (bf16[16,128,128]{2,1,0:T(8,128)(2,1)S(1)}, bf16[16,128,128]{2,1,0:T(8,128)(2,1)}, u32[]{:S(2)}) copy-start(bf16[16,128,128]{2,1,0:T(8,128)(2,1)} %get-tuple-element.18.refs_1_) | copy-start | bytes 1572868
  300.5 14.9 %collective-permute-start.7 = (bf16[2,16,128]{2,1,0:T(8,128)(2,1)S(1)}, bf16[2,16,128]{2,1,0:T(8,128)(2,1)S(1)}, u32[]{:S(2)}, u32[]{:S(2)}) collective-permute-start(bf16[2,16,128]{2,1,0:T(8,128)(2,1)S(1)} %pad_maximum_fusion.3), channel_id=1, source_target_pairs={{1,0},{3,2},{5,4},{7,6},{9,8},{11,10},{13,12},{15,14},{17,16},{19,... | collective-permute-start | bytes 24584 | tf_op jit(solution)/shard_map/ppermute | solution.py:347
  301.8 13.6 %copy-start = (bf16[16,128,128]{2,1,0:T(8,128)(2,1)S(1)}, bf16[16,128,128]{2,1,0:T(8,128)(2,1)}, u32[]{:S(2)}) copy-start(bf16[16,128,128]{2,1,0:T(8,128)(2,1)} %get-tuple-element.19.refs_0_) | copy-start | bytes 1572868
  301.8 13.6 %copy-start.1 = (bf16[16,128,128]{2,1,0:T(8,128)(2,1)S(1)}, bf16[16,128,128]{2,1,0:T(8,128)(2,1)}, u32[]{:S(2)}) copy-start(bf16[16,128,128]{2,1,0:T(8,128)(2,1)} %get-tuple-element.20.refs_1_) | copy-start | bytes 1572868
  314.6 0.8 copy-start.6
  315.4 12.8 %copy-start.8 = (bf16[256,4096]{1,0:T(8,128)(2,1)}, bf16[256,4096]{1,0:T(8,128)(2,1)S(1)}, u32[]{:S(2)}) copy-start(bf16[256,4096]{1,0:T(8,128)(2,1)S(1)} %get-tuple-element.21.refs_0_) | copy-start | bytes 6291460
  315.4 312.5 %collective-permute-start.8 = (bf16[8,256,128]{2,1,0:T(8,128)(2,1)}, bf16[8,256,128]{2,1,0:T(8,128)(2,1)S(1)}, u32[]{:S(2)}, u32[]{:S(2)}) collective-permute-start(bf16[8,256,128]{2,1,0:T(8,128)(2,1)} %get-tuple-element.26), channel_id=1, source_target_pairs={{0,8},{8,16},{16,24},{24,0},{1,9},{9,17},{17,25},{25,1},{2,10},{10... | collective-permute-start | bytes 1572872 | tf_op jit(solution)/shard_map/ppermute | solution.py:403
  328.2 1.4 copy-start.10
  329.5 300.7 %collective-permute-start.10 = (bf16[8,256,128]{2,1,0:T(8,128)(2,1)S(1)}, bf16[8,256,128]{2,1,0:T(8,128)(2,1)S(1)}, u32[]{:S(2)}, u32[]{:S(2)}) collective-permute-start(bf16[8,256,128]{2,1,0:T(8,128)(2,1)S(1)} %get-tuple-element.28), channel_id=1, source_target_pairs={{0,8},{8,16},{16,24},{24,0},{1,9},{9,17},{17,25},{25,1},{2,10},{10... | collective-permute-start | bytes 1572872 | tf_op jit(solution)/shard_map/ppermute | solution.py:403
  329.5 260.3 %collective-permute-start.1 = (s32[1]{0:T(128)}, s32[1]{0:T(128)}, u32[]{:S(2)}, u32[]{:S(2)}) collective-permute-start(s32[1]{0:T(128)} %bitcast.2), channel_id=1, source_target_pairs={{0,8},{8,16},{16,24},{24,0},{1,9},{9,17},{17,25},{25,1},{2,10},{10... | collective-permute-start | bytes 20 | tf_op jit(solution)/shard_map/ppermute | solution.py:384
  341.5 249.5 %collective-permute-start = (s32[1]{0:T(128)}, s32[1]{0:T(128)}, u32[]{:S(2)}, u32[]{:S(2)}) collective-permute-start(s32[1]{0:T(128)} %bitcast.2), channel_id=1, source_target_pairs={{0,24},{8,0},{16,8},{24,16},{1,25},{9,1},{17,9},{25,17},{2,26},{10... | collective-permute-start | bytes 20 | tf_op jit(solution)/shard_map/ppermute | solution.py:385
  347.6 245.2 %copy-start.7 = (bf16[8,256,128]{2,1,0:T(8,128)(2,1)S(1)}, bf16[8,256,128]{2,1,0:T(8,128)(2,1)}, u32[]{:S(2)}) copy-start(bf16[8,256,128]{2,1,0:T(8,128)(2,1)} %copy-done.6) | copy-start | bytes 1572868
  592.8 47.5 %collective-permute-start.12 = (bf16[8,256,128]{2,1,0:T(8,128)(2,1)S(1)}, bf16[8,256,128]{2,1,0:T(8,128)(2,1)S(1)}, u32[]{:S(2)}, u32[]{:S(2)}) collective-permute-start(bf16[8,256,128]{2,1,0:T(8,128)(2,1)S(1)} %copy-done.7), channel_id=1, source_target_pairs={{0,24},{8,0},{16,8},{24,16},{1,25},{9,1},{17,9},{25,17},{2,26},{10... | collective-permute-start | bytes 1572872 | tf_op jit(solution)/shard_map/ppermute | solution.py:404
  627.9 23.7 %collective-permute-start.13 = (bf16[8,256,128]{2,1,0:T(8,128)(2,1)S(1)}, bf16[8,256,128]{2,1,0:T(8,128)(2,1)S(1)}, u32[]{:S(2)}, u32[]{:S(2)}) collective-permute-start(bf16[8,256,128]{2,1,0:T(8,128)(2,1)S(1)} %get-tuple-element.27), channel_id=1, source_target_pairs={{0,24},{8,0},{16,8},{24,16},{1,25},{9,1},{17,9},{25,17},{2,26},{10... | collective-permute-start | bytes 1572872 | tf_op jit(solution)/shard_map/ppermute | solution.py:404
  627.9 44.2 %copy-start.12 = (bf16[8,256,128]{2,1,0:T(8,128)(2,1)}, bf16[8,256,128]{2,1,0:T(8,128)(2,1)S(1)}, u32[]{:S(2)}) copy-start(bf16[8,256,128]{2,1,0:T(8,128)(2,1)S(1)} %collective-permute-done.8.refs_8_) | copy-start | bytes 1572868
  628.1 46.0 %collective-permute-start.9 = (bf16[8,256,128]{2,1,0:T(8,128)(2,1)S(1)}, bf16[8,256,128]{2,1,0:T(8,128)(2,1)S(1)}, u32[]{:S(2)}, u32[]{:S(2)}) collective-permute-start(bf16[8,256,128]{2,1,0:T(8,128)(2,1)S(1)} %add_convert_fusion.3), channel_id=1, source_target_pairs={{0,8},{8,16},{16,24},{24,0},{1,9},{9,17},{17,25},{25,1},{2,10},{10... | collective-permute-start | bytes 1572872 | tf_op jit(solution)/shard_map/ppermute | solution.py:414
  630.2 42.0 %copy-start.13 = (bf16[8,256,128]{2,1,0:T(8,128)(2,1)}, bf16[8,256,128]{2,1,0:T(8,128)(2,1)S(1)}, u32[]{:S(2)}) copy-start(bf16[8,256,128]{2,1,0:T(8,128)(2,1)S(1)} %collective-permute-done.10.refs_9_) | copy-start | bytes 1572868
  630.4 44.5 %collective-permute-start.11 = (bf16[8,256,128]{2,1,0:T(8,128)(2,1)S(1)}, bf16[8,256,128]{2,1,0:T(8,128)(2,1)S(1)}, u32[]{:S(2)}, u32[]{:S(2)}) collective-permute-start(bf16[8,256,128]{2,1,0:T(8,128)(2,1)S(1)} %add_convert_fusion.2), channel_id=1, source_target_pairs={{0,8},{8,16},{16,24},{24,0},{1,9},{9,17},{17,25},{25,1},{2,10},{10... | collective-permute-start | bytes 1572872 | tf_op jit(solution)/shard_map/ppermute | solution.py:414
  640.3 31.8 %copy-start.14 = (bf16[8,256,128]{2,1,0:T(8,128)(2,1)}, bf16[8,256,128]{2,1,0:T(8,128)(2,1)S(1)}, u32[]{:S(2)}) copy-start(bf16[8,256,128]{2,1,0:T(8,128)(2,1)S(1)} %collective-permute-done.12.refs_4_) | copy-start | bytes 1572868
  641.7 43.5 %collective-permute-start.14 = (bf16[8,256,128]{2,1,0:T(8,128)(2,1)S(1)}, bf16[8,256,128]{2,1,0:T(8,128)(2,1)S(1)}, u32[]{:S(2)}, u32[]{:S(2)}) collective-permute-start(bf16[8,256,128]{2,1,0:T(8,128)(2,1)S(1)} %add_convert_fusion.1), channel_id=1, source_target_pairs={{0,24},{8,0},{16,8},{24,16},{1,25},{9,1},{17,9},{25,17},{2,26},{10... | collective-permute-start | bytes 1572872 | tf_op jit(solution)/shard_map/ppermute | solution.py:415
  651.5 4.5 copy-start.15
  651.7 42.8 %collective-permute-start.15 = (bf16[8,256,128]{2,1,0:T(8,128)(2,1)S(1)}, bf16[8,256,128]{2,1,0:T(8,128)(2,1)S(1)}, u32[]{:S(2)}, u32[]{:S(2)}) collective-permute-start(bf16[8,256,128]{2,1,0:T(8,128)(2,1)S(1)} %add_convert_fusion), channel_id=1, source_target_pairs={{0,24},{8,0},{16,8},{24,16},{1,25},{9,1},{17,9},{25,17},{2,26},{10... | collective-permute-start | bytes 1572872 | tf_op jit(solution)/shard_map/ppermute | solution.py:415
  656.1 1.6 copy-start.9
  657.7 1.6 copy-start.11
  672.2 1.0 copy-start.4
  673.1 1.0 copy-start.5
  674.1 0.8 copy-start.16
  674.9 0.8 copy-start.17
  685.2 9.3 %copy-start.18 = (bf16[8,256,128]{2,1,0:T(8,128)(2,1)}, bf16[8,256,128]{2,1,0:T(8,128)(2,1)S(1)}, u32[]{:S(2)}) copy-start(bf16[8,256,128]{2,1,0:T(8,128)(2,1)S(1)} %collective-permute-done.14.refs_6_) | copy-start | bytes 1572868
  694.6 0.8 copy-start.19

commit v2 on v0

v2 whole, which is shorter than its diff:
```python
import functools

import jax
import jax.numpy as jnp
import numpy as np
from jax import lax
from jax.experimental import pallas as pl
from jax.experimental.pallas import tpu as pltpu
from jax.sharding import PartitionSpec as P

CUTS = (0, 128, 256)
RIGHT, ACROSS, LEFT = 1, 2, 3
LANES = 128
SCOPED = 14 << 20
VMEM = pl.BlockSpec(memory_space=pltpu.VMEM)


def in_hbm(*arrays):
    return [pltpu.with_memory_space_constraint(array, pltpu.HBM) for array in arrays]


def after(value, *before):
    return lax.optimization_barrier((value, *before))[0]


def regroup_matrix(block, parts):
    rows = np.arange(block * parts)
    out = np.zeros((block * parts, block * parts), np.float32)
    out[rows, (rows % parts) * block + rows // parts] = 1.0
    return jnp.asarray(out, jnp.bfloat16)


def stencil_matrix(zc, rows_y):
    out = np.zeros((rows_y, zc, rows_y + 2, zc), np.float32)
    z = np.arange(zc)
    for y in range(rows_y):
        out[y, z, y, z] = 0.5
        out[y, z, y + 2, z] = 0.5
        out[y, z, y + 1, z] = -2.0
        out[y, z[1:], y + 1, z[:-1]] = 0.5
        out[y, z[:-1], y + 1, z[1:]] = 0.5
    return jnp.asarray(out.reshape(rows_y * zc, (rows_y + 2) * zc), jnp.bfloat16)


def prepare_kernel(per_step, cuts, rows_y, tiles, phi_ref, mix_ref, pot_ref, *out_refs):
    block = mix_ref.shape[0]
    size = block // (tiles * rows_y)
    spans = list(zip(cuts, cuts[1:]))
    singles = [0, cuts[-1] - 1] + [z for cut in cuts[1:-1] for z in (cut - 1, cut)]
    field_refs = out_refs[: len(spans) * rows_y]
    edge_ref, inner_ref = out_refs[len(spans) * rows_y : len(spans) * rows_y + 2]
    turned_pot_refs = out_refs[len(spans) * rows_y + 2 :]

    @pl.when(pl.program_id(0) == 0)
    def _():
        for y in range(rows_y):
            turned = pot_ref[:, y, :].T
            for ref, (first, last) in zip(turned_pot_refs, spans):
                ref[y * (last - first) : (y + 1) * (last - first), :] = turned[first:last]

    for step in range(per_step):
        part = phi_ref[step * block : (step + 1) * block, :]
        turned = lax.dot_general(
            part, mix_ref[...], (((0,), (0,)), ((), ())), preferred_element_type=jnp.float32
        ).astype(jnp.bfloat16)
        lanes = slice(step * size, (step + 1) * size)
        for y in range(rows_y):
            for chunk, (first, last) in enumerate(spans):
                for tile in range(tiles):
                    lo, hi = max(first, tile * LANES), min(last, (tile + 1) * LANES)
                    if lo < hi:
                        lane = (tile * rows_y + y) * size
                        field_refs[chunk * rows_y + y][lo - first : hi - first, lanes] = turned[
                            lo - tile * LANES : hi - tile * LANES, lane : lane + size
                        ]
            for k, z in enumerate(singles):
                tile, row = divmod(z, LANES)
                lane = (tile * rows_y + y) * size
                ref, at = (edge_ref, k * rows_y + y) if k < 2 else (inner_ref, (k - 2) * rows_y + y)
                ref[at : at + 1, lanes] = turned[row : row + 1, lane : lane + size]


def prepare(phi, pot, cuts):
    groups, block, rows_y, rows_z = phi.shape
    tiles = rows_z // LANES
    flat = (
        phi.reshape(groups, block, rows_y, tiles, LANES)
        .transpose(0, 1, 3, 2, 4)
        .reshape(groups * block * tiles * rows_y, LANES)
    )
    parts = tiles * rows_y
    per_step = 4
    width = per_step * block
    chunks = len(cuts) - 1
    spans = [last - first for first, last in zip(cuts, cuts[1:])]
    sizes = [span for span in spans for _ in range(rows_y)] + [2 * rows_y, 2 * rows_y * max(1, chunks - 1)]
    outs = pl.pallas_call(
        functools.partial(prepare_kernel, per_step, cuts, rows_y, tiles),
        grid=(groups // per_step,),
        in_specs=[
            pl.BlockSpec((per_step * block * parts, LANES), lambda s: (s, 0)),
            pl.BlockSpec((block * parts, block * parts), lambda s: (0, 0)),
            pl.BlockSpec((groups, rows_y, rows_z), lambda s: (0, 0, 0)),
        ],
        out_specs=[pl.BlockSpec((size, width), lambda s: (0, s)) for size in sizes]
        + [pl.BlockSpec((rows_y * span, groups), lambda s: (0, 0)) for span in spans],
        out_shape=[jax.ShapeDtypeStruct((size, groups * block), jnp.bfloat16) for size in sizes]
        + [jax.ShapeDtypeStruct((rows_y * span, groups), jnp.float32) for span in spans],
        compiler_params=pltpu.CompilerParams(vmem_limit_bytes=SCOPED),
        name="prepare",
    )(*in_hbm(flat, regroup_matrix(block, parts), pot))
    fields = [[outs[c * rows_y + y] for y in range(rows_y)] for c in range(chunks)]
    return fields, outs[chunks * rows_y], outs[chunks * rows_y + 1], outs[chunks * rows_y + 2 :]


def stacked_blocks(ref, which_ref, pair, groups):
    return jnp.concatenate(
        [
            jnp.concatenate([ref[which_ref[(2 * pair + j) * groups + row]] for j in range(2)], axis=1)
            for row in range(groups)
        ],
        axis=0,
    )


def phi_kernel(groups, rows_y, loads, which_ref, *refs):
    y_refs, refs = refs[:rows_y], refs[rows_y:]
    if loads:
        (kern_hbm, hk_hbm), (rows_ref, sum_ref, kern_ref, hk_ref, sems) = refs[:2], refs[2:]
    else:
        hk_ref, rows_ref, sum_ref = refs
    zc = y_refs[0].shape[0]
    pair = pl.program_id(0)

    def copies():
        count = kern_hbm.shape[0]
        return [
            pltpu.make_async_copy(source, target.at[:count], sems.at[k])
            for k, (source, target) in enumerate(((hk_hbm, hk_ref), (kern_hbm, kern_ref)))
        ]

    @pl.when(pair == 0)
    def _():
        if loads:
            for copy in copies():
                copy.start()
            for ref in (kern_ref, hk_ref):
                ref[ref.shape[0] - 1] = jnp.zeros(ref.shape[1:], ref.dtype)
        for y, ref in enumerate(y_refs):
            rows_ref[y * zc : (y + 1) * zc, :] = ref[...]
        if loads:
            copies()[0].wait()

    sum_ref[pair] = jnp.dot(
        rows_ref[...], stacked_blocks(hk_ref, which_ref, pair, groups), preferred_element_type=jnp.float32
    )
    if loads:

        @pl.when(pair == pl.num_programs(0) - 1)
        def _():
            copies()[1].wait()


def phi_part(fields, groups, which, kern_hk, kern=None):
    zc, width = fields[0].shape
    n = len(fields) * zc
    block = width // groups
    pairs = which.shape[0] // groups // 2
    loads = kern is not None
    hbm = pl.BlockSpec(memory_space=pltpu.HBM)
    out_shape = [pltpu.VMEM((n, width), jnp.bfloat16), pltpu.VMEM((pairs, n, 2 * block), jnp.float32)]
    if loads:
        out_shape += [pltpu.VMEM((part.shape[0] + 1, *part.shape[1:]), part.dtype) for part in (kern, kern_hk)]
    return pl.pallas_call(
        functools.partial(phi_kernel, groups, len(fields), loads),
        grid_spec=pltpu.PrefetchScalarGridSpec(
            num_scalar_prefetch=1,
            grid=(pairs,),
            in_specs=[VMEM] * len(fields) + ([hbm] * 2 if loads else [VMEM]),
            out_specs=[VMEM] * len(out_shape),
            scratch_shapes=[pltpu.SemaphoreType.DMA((2,))] if loads else [],
        ),
        out_shape=out_shape,
        compiler_params=pltpu.CompilerParams(vmem_limit_bytes=SCOPED),
        cost_estimate=pl.CostEstimate(
            flops=4 * n * width * pairs * block, transcendentals=0, bytes_accessed=2 * n * width
        ),
        name="phi_part",
    )(which, *fields, *(in_hbm(kern, kern_hk) if loads else [kern_hk]))


def fill_action(rows_y, groups, act_ref, rows, prev_ref, next_ref, low_ref, high_ref, low_at, high_at, flags, pot_ref, mix_ref):
    depth = act_ref.shape[1]
    zc = act_ref.shape[0] // rows_y
    block = depth // groups
    wide = 4
    scales = [0.5 if flag is None else 0.5 * flag.astype(jnp.float32) for flag in flags]
    for first in range(0, groups, wide):
        lanes = slice(first * block, (first + wide) * block)
        around = jnp.concatenate([prev_ref[:, lanes], rows[:, lanes], next_ref[:, lanes]], axis=0)
        beside = jnp.dot(mix_ref[...], around, preferred_element_type=jnp.float32)
        for y in range(rows_y):
            at = slice(y * zc, (y + 1) * zc)
            field = rows[at, lanes]
            pots = jnp.concatenate(
                [jnp.broadcast_to(pot_ref[at, row : row + 1], (zc, block)) for row in range(first, first + wide)],
                axis=1,
            )
            value = beside[at] - pots * field.astype(jnp.float32)
            low = scales[0] * low_ref[low_at + y : low_at + y + 1, lanes].astype(jnp.float32)
            high = scales[1] * high_ref[high_at + y : high_at + y + 1, lanes].astype(jnp.float32)
            z = lax.broadcasted_iota(jnp.int32, (8, wide * block), 0)
            head = value[:8] + jnp.where(z == 0, low, 0.0)
            tail = value[zc - 8 :] + jnp.where(z == 7, high, 0.0)
            act_ref[at, lanes] = jnp.concatenate([head, value[8 : zc - 8], tail], axis=0).astype(jnp.bfloat16)


def action_kernel(groups, rows_y, cols, low_at, high_at, masked, which_ref, *refs):
    rows_ref, sum_ref, prev_ref, next_ref, low_ref, high_ref, pot_ref, mix_ref, kern_ref, act_ref = refs[:10]
    outs = refs[10:]
    pair = pl.program_id(0)
    n = rows_ref.shape[0]
    extra = cols * groups

    @pl.when(pair == 0)
    def _():
        flags = [which_ref[extra + k] if masked[k] else None for k in range(2)]
        fill_action(
            rows_y, groups, act_ref, rows_ref, prev_ref, next_ref, low_ref, high_ref, low_at, high_at, flags, pot_ref, mix_ref
        )
        if len(outs) == 2:
            code = jnp.full((16, outs[0].shape[1]), which_ref[extra + 2].astype(jnp.float32)).astype(jnp.bfloat16)
            for ref in outs:
                ref[ref.shape[0] - 16 :, :] = code

    value = sum_ref[pair] + jnp.dot(
        act_ref[...], stacked_blocks(kern_ref, which_ref, pair, groups), preferred_element_type=jnp.float32
    )
    block = value.shape[1] // 2
    split = cols // 2 // len(outs)

    def store(ref, first):
        for j in range(2):
            at = pl.multiple_of((2 * (pair - first) + j) * n, 16)
            ref[pl.ds(at, n), :] = value[:, j * block : (j + 1) * block].astype(jnp.bfloat16)

    if len(outs) == 1:
        store(outs[0], 0)
    else:

        @pl.when(pair < split)
        def _():
            store(outs[0], 0)

        @pl.when(pair >= split)
        def _():
            store(outs[1], split)


def action_part(rows, partial, prev, below, low, low_at, high, high_at, masked, pot, groups, rows_y, cols, which, kern, halves):
    n, width = rows.shape
    zc = n // rows_y
    block = width // groups
    out_rows = [cols // halves * n + (16 if halves == 2 else 0)] * halves
    return pl.pallas_call(
        functools.partial(action_kernel, groups, rows_y, cols, low_at, high_at, masked),
        grid_spec=pltpu.PrefetchScalarGridSpec(
            num_scalar_prefetch=1,
            grid=(cols // 2,),
            in_specs=[VMEM] * 9,
            out_specs=[VMEM] * (1 + halves),
        ),
        out_shape=[pltpu.VMEM((n, width), jnp.bfloat16)]
        + [pltpu.VMEM((rows_out, block), jnp.bfloat16) for rows_out in out_rows],
        compiler_params=pltpu.CompilerParams(vmem_limit_bytes=SCOPED),
        cost_estimate=pl.CostEstimate(
            flops=2 * n * width * cols * block, transcendentals=0, bytes_accessed=2 * n * width
        ),
        name="action_part",
    )(which, rows, partial, prev, below, low, high, pot, stencil_matrix(zc, rows_y), kern)


def onward_kernel(away_ref, q0_ref, q1_ref, right_ref, right_code, left_ref, left_code, to_right, to_left):
    for mine, direction, arrived, code, out in (
        (q1_ref, RIGHT, right_ref, right_code, to_right),
        (q0_ref, LEFT, left_ref, left_code, to_left),
    ):
        kept = jnp.where(away_ref[0] == direction, mine[...].astype(jnp.float32), 0.0)
        through = code[:1, :].astype(jnp.float32) == ACROSS
        out[...] = (kept + jnp.where(through, arrived[...].astype(jnp.float32), 0.0)).astype(jnp.bfloat16)


def send_onward(away, q0, q1, right1, left1):
    rows, block = q0.shape
    steps = 4
    size = (rows - 16) // steps
    part = pl.BlockSpec((size, block), lambda s, a: (s, 0))
    code = pl.BlockSpec((16, block), lambda s, a: ((rows - 16) // 16, 0))
    return pl.pallas_call(
        onward_kernel,
        grid_spec=pltpu.PrefetchScalarGridSpec(
            num_scalar_prefetch=1,
            grid=(steps,),
            in_specs=[part, part, part, code, part, code],
            out_specs=[part, part],
        ),
        out_shape=[jax.ShapeDtypeStruct((rows - 16, block), jnp.bfloat16)] * 2,
        compiler_params=pltpu.CompilerParams(vmem_limit_bytes=SCOPED),
        cost_estimate=pl.CostEstimate(flops=0, transcendentals=0, bytes_accessed=12 * rows * block),
        name="send_onward",
    )(away, q0, q1, right1, right1, left1, left1)


def local_kernel(groups, which_ref, act_ref, rows_ref, kern_ref, hk_ref, left_ref, left_code, right_ref, right_code, out_ref):
    pair = pl.program_id(0)
    value = jnp.dot(
        act_ref[...], stacked_blocks(kern_ref, which_ref, pair, groups), preferred_element_type=jnp.float32
    ) + jnp.dot(rows_ref[...], stacked_blocks(hk_ref, which_ref, pair, groups), preferred_element_type=jnp.float32)
    n = rows_ref.shape[0]
    block = value.shape[1] // 2

    def store(arrived, code, wanted):
        mine = code[:1, :].astype(jnp.float32) == wanted
        for j in range(2):
            at = slice(j * n, (j + 1) * n)
            more = jnp.where(mine, arrived[at, :].astype(jnp.float32), 0.0)
            out_ref[at, :] = (value[:, j * block : (j + 1) * block] + more).astype(jnp.bfloat16)

    half = pl.num_programs(0) // 2

    @pl.when(pair < half)
    def _():
        store(left_ref, left_code, LEFT)

    @pl.when(pair >= half)
    def _():
        store(right_ref, right_code, RIGHT)


def local_columns(act, rows, groups, which, kern, kern_hk, left1, right1):
    cols = which.shape[0] // groups
    n, width = rows.shape
    block = width // groups
    half = cols // 4
    code = pl.BlockSpec((16, block), lambda p, w: (cols // 2 * n // 16, 0))
    return pl.pallas_call(
        functools.partial(local_kernel, groups),
        grid_spec=pltpu.PrefetchScalarGridSpec(
            num_scalar_prefetch=1,
            grid=(cols // 2,),
            in_specs=[VMEM] * 4
            + [pl.BlockSpec((2 * n, block), lambda p, w: (jnp.minimum(p, half - 1), 0)), code]
            + [pl.BlockSpec((2 * n, block), lambda p, w: (jnp.maximum(p - half, 0), 0)), code],
            out_specs=pl.BlockSpec((2 * n, block), lambda p, w: (p, 0)),
        ),
        out_shape=jax.ShapeDtypeStruct((cols * n, block), jnp.bfloat16),
        compiler_params=pltpu.CompilerParams(vmem_limit_bytes=SCOPED),
        cost_estimate=pl.CostEstimate(
            flops=4 * n * width * cols * block, transcendentals=0, bytes_accessed=2 * n * width
        ),
        name="local_columns",
    )(which, act, rows, kern, kern_hk, left1, left1, right1, right1)


def write_columns(rows_y, tiles, columns, mix_ref, out_ref):
    sizes = [value.shape[0] // rows_y for value in columns[0]]
    rows = mix_ref.shape[0]
    turned = []
    for values in columns:
        parts = []
        for tile in range(tiles):
            for y in range(rows_y):
                pieces = []
                for chunk, zc in enumerate(sizes):
                    first = sum(sizes[:chunk])
                    lo, hi = max(first, tile * LANES), min(first + zc, (tile + 1) * LANES)
                    if lo < hi:
                        pieces.append(values[chunk][y * zc + lo - first : y * zc + hi - first, :])
                part = jnp.concatenate(pieces, axis=0) if len(pieces) > 1 else pieces[0]
                parts.append((-2.0 * part).astype(jnp.bfloat16))
        turned.append(jnp.concatenate(parts, axis=1))
    wide = 2
    for first in range(0, len(turned), wide):
        both = jnp.concatenate(turned[first : first + wide], axis=0)
        out = lax.dot_general(mix_ref[...], both, (((1,), (1,)), ((), ())), preferred_element_type=jnp.float32)
        for j in range(wide):
            out_ref[(first + j) * rows : (first + j + 1) * rows, :] = out[:, j * LANES : (j + 1) * LANES].astype(
                jnp.bfloat16
            )


def final_kernel(per_step, chunks, rows_y, tiles, mix_ref, *refs):
    own, rest, out_ref = refs[:chunks], refs[chunks:-1], refs[-1]
    step = pl.program_id(0)
    half = pl.num_programs(0) // 2

    def emit(added):
        columns = []
        for col in range(per_step):
            values = []
            for chunk, mine in enumerate(own):
                n = mine.shape[0] // per_step
                at = slice(col * n, (col + 1) * n)
                value = mine[at, :].astype(jnp.float32)
                values.append(value + added[chunk][at, :].astype(jnp.float32) if added else value)
            columns.append(values)
        write_columns(rows_y, tiles, columns, mix_ref, out_ref)

    if not rest:
        emit(())
        return

    @pl.when(step < half)
    def _():
        emit(rest[:chunks])

    @pl.when(step >= half)
    def _():
        emit(rest[chunks:])


def finish(own, low, high, cols, rows_y, rows_z):
    chunks = len(own)
    block = own[0].shape[1]
    tiles = rows_z // LANES
    rows = block * tiles * rows_y
    per_step = 4
    steps = cols // per_step
    half = steps // 2

    def specs(place):
        return [pl.BlockSpec((part.shape[0] // steps, block), lambda s: (place(s), 0)) for part in own]

    in_specs = [pl.BlockSpec((rows, rows), lambda s: (0, 0))] + specs(lambda s: s)
    arrays = list(own)
    if low is not None:
        in_specs += specs(lambda s: jnp.minimum(s, half - 1)) + specs(lambda s: jnp.maximum(s - half, 0))
        arrays += [*low, *high]
    flat = pl.pallas_call(
        functools.partial(final_kernel, per_step, chunks, rows_y, tiles),
        grid=(steps,),
        in_specs=in_specs,
        out_specs=pl.BlockSpec((per_step * rows, LANES), lambda s: (s, 0)),
        out_shape=jax.ShapeDtypeStruct((cols * rows, LANES), jnp.bfloat16),
        compiler_params=pltpu.CompilerParams(vmem_limit_bytes=SCOPED),
        name="finish",
    )(*in_hbm(regroup_matrix(block, tiles * rows_y), *arrays))
    return unflatten(flat, cols, block, rows_y, tiles)


def unflatten(flat, cols, block, rows_y, tiles):
    return (
        flat.reshape(cols, block, tiles, rows_y, LANES)
        .transpose(0, 1, 3, 2, 4)
        .reshape(cols, block, rows_y, tiles * LANES)
    )


def block_of_column(slot_of, slots):
    hit = slot_of[None, :, :] == slots[:, None, None]
    zero = slot_of.size
    place = jnp.arange(zero, dtype=jnp.int32).reshape(slot_of.shape) - zero
    return zero + jnp.sum(jnp.where(hit, place, 0), axis=2)


def shifts(axis, by):
    count = lax.axis_size(axis)
    return [(i, i + by) for i in range(count) if 0 <= i + by < count]


def outer_rows(edges, rows_y):
    if lax.axis_size("gz") == 2:
        return lax.ppermute(edges, "gz", [(0, 1), (1, 0)])
    after_last = lax.ppermute(edges[:rows_y], "gz", shifts("gz", -1))
    before_first = lax.ppermute(edges[rows_y:], "gz", shifts("gz", 1))
    return jnp.concatenate([after_last, before_first], axis=0)


def per_device(phi, pot, kern, kern_hk, slot_of, req_cols):
    groups, block, rows_y, rows_z = phi.shape
    listed = req_cols.shape[0]
    ring = lax.axis_size("gx")
    cuts = CUTS if CUTS[-1] == rows_z else (0, rows_z)
    chunks = len(cuts) - 1

    fields, edges, inner, pots = prepare(phi, pot, cuts)
    halo = []

    def send_halo(c, *before):
        up, down = after(fields[c][-1], *before), after(fields[c][0], *before)
        halo.append((lax.ppermute(up, "gy", shifts("gy", 1)), lax.ppermute(down, "gy", shifts("gy", -1))))

    send_halo(0)
    outer = outer_rows(edges, rows_y)
    req_cols, slot_of, _ = lax.optimization_barrier((req_cols, slot_of, edges))
    kern = kern.reshape(-1, block, block)
    kern_hk = kern_hk.reshape(-1, block, block)
    place = lax.axis_index("gz")
    marks = [place > 0, place < lax.axis_size("gz") - 1]

    def sides(c):
        low = (outer, rows_y) if c == 0 else (inner, (2 * c - 2) * rows_y)
        high = (outer, 0) if c == chunks - 1 else (inner, (2 * c + 1) * rows_y)
        return *low, *high, (c == 0, c == chunks - 1)

    blocks = []

    def phi_columns(c, names):
        if blocks:
            return phi_part(fields[c], groups, names, blocks[1])
        mine, partial, *loaded = phi_part(fields[c], groups, names, kern_hk, kern)
        blocks.extend(loaded)
        return mine, partial

    def all_columns(c, mine, partial, table, cols, halves):
        return action_part(
            mine, partial, *halo[c], *sides(c), pots[c], groups, rows_y, cols, table, blocks[0], halves
        )

    if ring != 4:
        which = block_of_column(slot_of, jnp.arange(listed, dtype=jnp.int32)).reshape(-1)
        table = jnp.concatenate([which, jnp.stack(marks).astype(jnp.int32)])
        hit = req_cols[None, :] == jnp.arange(groups * ring, dtype=jnp.int32)[:, None]
        named = jnp.any(hit, axis=1)
        source = jnp.sum(jnp.where(hit, jnp.arange(listed, dtype=jnp.int32), 0), axis=1)
        parts = []
        for c in range(chunks):
            if c:
                send_halo(c, table)
            _, sums = all_columns(c, *phi_columns(c, which), table, listed, 1)
            spread = jnp.where(named[:, None, None], sums.reshape(listed, -1, block)[source], 0)
            total = lax.psum_scatter(spread, "gx", scatter_dimension=0, tiled=True)
            parts.append(total.reshape(-1, block))
        return finish(parts, None, None, groups, rows_y, rows_z)

    me = lax.axis_index("gx")
    owners = req_cols // groups
    other = jnp.where(owners[0] == me, owners[listed - 1], owners[0])
    away = (other - me) % ring
    ahead = [(i, (i + 1) % ring) for i in range(ring)]
    behind = [(i, (i - 1) % ring) for i in range(ring)]

    half = groups // 2
    column = jnp.arange(groups, dtype=jnp.int32)
    swapped = jnp.where(away == ACROSS, column, (column + half) % groups)
    wanted = jnp.concatenate([other * groups + swapped, me * groups + column])
    slots = jnp.sum(
        jnp.where(wanted[:, None] == req_cols[None, :], jnp.arange(listed, dtype=jnp.int32), 0), axis=1
    )
    which = block_of_column(slot_of, slots).reshape(-1)
    far, near = which[: groups * groups], which[groups * groups :]
    table = jnp.concatenate([far, jnp.stack([*marks, away]).astype(jnp.int32)])
    away = away.reshape(1)
    for c in range(1, chunks):
        send_halo(c, table)

    rows, acts, sent, own, right1, left1, right2, left2 = [], [], [], [], [], [], [], []

    def send_first(c, *before):
        mine, partial = phi_columns(c, after(far, *before))
        act, q0, q1 = all_columns(c, mine, partial, after(table, *before), groups, 2)
        rows.append(mine)
        acts.append(act)
        sent.append((q0, q1))
        right1.append(lax.ppermute(q0, "gx", ahead))
        left1.append(lax.ppermute(q1, "gx", behind))

    def send_second(c, *before):
        arrived = lax.optimization_barrier((right1[c], left1[c], *before))
        right1[c], left1[c] = arrived[:2]
        to_right, to_left = send_onward(away, *sent[c], right1[c], left1[c])
        right2.append(lax.ppermute(to_right, "gx", ahead))
        left2.append(lax.ppermute(to_left, "gx", behind))
        own.append(
            local_columns(acts[c], rows[c], groups, after(near, to_right, *right2[:c], *left2[:c]), *blocks, left1[c], right1[c])
        )

    send_first(0)
    for c in range(1, chunks):
        send_first(c, *sent[c - 1])
        send_second(c - 1, *sent[c])
    send_second(chunks - 1, own[-1])
    return finish(own, right2, left2, groups, rows_y, rows_z)


def solution(mesh):
    placed = (
        P("gx", None, "gy", "gz"),
        P("gx", "gy", "gz"),
        P("gx", None, None, None),
        P("gx", None, None, None),
        P("gx", None),
        P("gx"),
    )
    return jax.shard_map(
        per_device, mesh=mesh, in_specs=placed, out_specs=P("gx", None, "gy", "gz"), check_vma=False
    )
```

time: 363 us -> 143 us (0.39)
  waiting for transfers between devices: 170 us -> 42.8 us
  local copies, waits for them, and re-layouts: 103 us -> 13 us
  matrix products: 55.4 us -> 0 us
  Pallas kernels: 0 us -> 54 us
  starting transfers between devices: 10.6 us -> 27.4 us
  between operations: 13.5 us -> 2.31 us
  other arithmetic: 8.81 us -> 2.52 us
    reduce_scatter x1 -> x0, waiting for transfers between devices: 167 us -> none  [per_device(): lax.psum_scatter(jnp.einsum('ur,ubyz->rbyz', select, partial_bf, preferre...]
    dot_general x4 -> x0, matrix products: 55.4 us -> none  [the longest x1 16.6 us: per_device(): jnp.einsum('ur,ubyz->rbyz', select, partial_bf, preferred_element_type=jn...]
    pallas_call x0 -> x10, Pallas kernels: none -> 54 us  [the longest x2 13.5 us: local_columns(): pl.pallas_call(functools.partial(local_kernel, groups), grid_spec=pltpu.P...]
    convert_element_type x3 -> x0, local copies, waits for them, and re-layouts: 50.2 us -> none  [the longest x1 23.7 us: per_device(): dense_kern = jnp.einsum('iku,ikab->uiab', placed, kern, preferred_element...]
    ppermute x4 -> x13, waiting for transfers between devices: 3.39 us -> 42.8 us  [the longest x2 25.5 us: send_second(): left2.append(lax.ppermute(to_left, 'gx', behind))]
    dot_general x2 -> x0, local copies, waits for them, and re-layouts: 35.1 us -> none  [the longest x1 17.5 us: per_device(): jnp.einsum('iku,ikab->uiab', placed, kern, preferred_element_type=jnp.flo...]
    ppermute x4 -> x13, starting transfers between devices: 10.6 us -> 27.4 us  [the longest x2 8.97 us: send_halo(): lax.ppermute(up, 'gy', shifts('gy', 1))]
    convert_element_type x3 -> x0, other arithmetic: 8.09 us -> none  [the longest x1 3.42 us: per_device(): (-0.5 * (beside_all - 4.0 * field) + pot[:, None, :, :] * field).astype(j...]
  transfers between devices with their start and end apart: 5 -> 13, of which waited for: 2 -> 6; matrix products, arithmetic and copies ran while one was open for 32% -> 2% of each run, Pallas kernels for 0% -> 31%
where the time goes in v2:
time: 143 us; the launch traced here: 142 us
  Pallas kernels  54 us (38%)
  waiting for transfers between devices  42.8 us (30%)
  starting transfers between devices  27.4 us (19%)
  local copies, waits for them, and re-layouts  13 us (9%)
  other arithmetic  2.52 us (2%)
  between operations  2.31 us (2%)
    ppermute x2, waiting for transfers between devices, send_second(): left2.append(lax.ppermute(to_left, 'gx', behind))  25.5 us
    pallas_call x2, Pallas kernels, local_columns(): pl.pallas_call(functools.partial(local_kernel, groups), grid_spec=pltpu.P...  13.5 us
    pallas_call x2, Pallas kernels, phi_part(): pl.pallas_call(functools.partial(phi_kernel, groups, len(fields), loads),...  13.2 us
    pallas_call x2, Pallas kernels, action_part(): pl.pallas_call(functools.partial(action_kernel, groups, rows_y, cols, low...  12.2 us
    unnamed x38, local copies, waits for them, and re-layouts  12 us
    ppermute x2, waiting for transfers between devices, send_halo(): lax.ppermute(down, 'gy', shifts('gy', -1))  11.6 us
    ppermute x2, starting transfers between devices, send_halo(): lax.ppermute(up, 'gy', shifts('gy', 1))  8.97 us
    ppermute x2, starting transfers between devices, send_second(): left2.append(lax.ppermute(to_left, 'gx', behind))  7.07 us
  transfers between devices with their start and end apart: 13, of which 6 were waited for; matrix products, arithmetic and copies ran while one was open for 2% of the time, Pallas kernels for 31%

profile of v2, /device:TPU:0, one launch (start us, length us, event | category | flops | bytes accessed | tf_op | source)
XLA Modules:
  0.0 142.1 jit_solution(5500363420662880953)
XLA Ops:
  0.0 4.8 %prepare.1 = (bf16[128,2048]{1,0:T(8,128)(2,1)S(1)}, bf16[128,2048]{1,0:T(8,128)(2,1)S(1)}, bf16[128,2048]{1,0:T(8,128)(2,1)S(1)}, bf16[128,2048]{1,0:T(8,128)(2...) custom-call(bf16[8192,128]{1,0:T(8,128)(2,1)} %bitcast.19, ...), custom_call_target="tpu_custom_call" | custom-call | tf_op jit(solution)/shard_map/prepare/pallas_call | solution.py:97
  4.8 0.5 collective-permute-start.2
  5.2 4.4 %collective-permute-start = (bf16[128,2048]{1,0:T(8,128)(2,1)S(1)}, bf16[128,2048]{1,0:T(8,128)(2,1)S(1)}, u32[]{:S(2)}, u32[]{:S(2)}) collective-permute-start(bf16[128,2048]{1,0:T(8,128)(2,1)S(1)} %get-tuple-element.45.refs_1_), channel_id=1, source_target_pairs={{0,2},{2,4},{4,6},{1,3},{3,5},{5,7},{8,10},{10,12},{12,14},{9,11},... | collective-permute-start | bytes 1572872 | tf_op jit(solution)/shard_map/ppermute | solution.py:491
  9.6 1.3 collective-permute-start.1
  11.0 0.7 and_select_fusion.1
  11.6 0.6 fusion.3
  14.3 0.1 pad_add_fusion.1
  14.3 0.8 select_reduce_fusion.1
  15.2 0.8 select_reduce_fusion
  16.0 0.1 fusion.2
  16.1 0.1 copy.17
  16.2 0.1 slice.24.which_ref
  16.3 0.1 pad_add_fusion.which_ref
  16.3 4.6 %collective-permute-start.5 = (bf16[128,2048]{1,0:T(8,128)(2,1)}, bf16[128,2048]{1,0:T(8,128)(2,1)S(1)}, u32[]{:S(2)}, u32[]{:S(2)}) collective-permute-start(bf16[128,2048]{1,0:T(8,128)(2,1)} %get-tuple-element.60.refs_1_), channel_id=1, source_target_pairs={{0,2},{2,4},{4,6},{1,3},{3,5},{5,7},{8,10},{10,12},{12,14},{9,11},... | collective-permute-start | bytes 1572872 | tf_op jit(solution)/shard_map/ppermute | solution.py:491
  20.9 1.3 collective-permute-start.6
  22.2 0.0 copy-start.14
  22.2 7.7 %phi_part.2 = (bf16[256,2048]{1,0:T(8,128)(2,1)S(1)}, f32[8,256,256]{2,1,0:T(8,128)S(1)}, bf16[257,128,128]{2,1,0:T(8,128)(2,1)S(1)}, bf16[257,128,128]{2,1,0:T(8,128)(2,1)S(1)}) custom-call(s32[256]{0:T(256)S(1)} %slice.24.which_ref, bf16[128,2048]{1,0:T(8,128)(2,1)S(1)} %get-tuple-element.44.refs_0_, bf16[128,2048]{1,0:T(8,128)(2,1)S(1)} %get-tuple-element.45.refs_1_, ...), custom_call_target="tpu_custom_call" | custom-call | flops 2147483648 | bytes 1048576 | tf_op jit(solution)/shard_map/phi_part/pallas_call | solution.py:174
  30.0 5.0 %collective-permute-done.1.refs_3_ = bf16[128,2048]{1,0:T(8,128)(2,1)S(1)} collective-permute-done((bf16[128,2048]{1,0:T(8,128)(2,1)S(1)}, bf16[128,2048]{1,0:T(8,128)(2,1)S(1)}, u32[]{:S(2)}, u32[]{:S(2)}) %collective-permute-start.1) | collective-permute-done | bytes 524320 | tf_op jit(solution)/shard_map/ppermute | solution.py:491
  35.0 6.2 %action_part.2 = (bf16[256,2048]{1,0:T(8,128)(2,1)S(1)}, bf16[2064,128]{1,0:T(8,128)(2,1)}, bf16[2064,128]{1,0:T(8,128)(2,1)}) custom-call(s32[259]{0:T(512)S(1)} %pad_add_fusion.which_ref, bf16[256,2048]{1,0:T(8,128)(2,1)S(1)} %get-tuple-element.46.refs_0_.rows_ref, f32[8,256,256]{2,1,0:T(8,128)S(1)} %get-tuple-element.47.refs_1_, ...), custom_call_target="tpu_custom_call" | custom-call | flops 2147483648 | bytes 1048576 | tf_op jit(solution)/shard_map/action_part/pallas_call | solution.py:265
  41.2 1.6 %collective-permute-start.3 = (bf16[2064,128]{1,0:T(8,128)(2,1)}, bf16[2064,128]{1,0:T(8,128)(2,1)S(1)}, u32[]{:S(2)}, u32[]{:S(2)}) collective-permute-start(bf16[2064,128]{1,0:T(8,128)(2,1)} %get-tuple-element.51.q0_ref), channel_id=1, source_target_pairs={{0,8},{8,16},{16,24},{24,0},{1,9},{9,17},{17,25},{25,1},{2,10},{10... | collective-permute-start | bytes 1585160 | tf_op jit(solution)/shard_map/ppermute | solution.py:565
  42.8 2.2 %collective-permute-start.4 = (bf16[2064,128]{1,0:T(8,128)(2,1)}, bf16[2064,128]{1,0:T(8,128)(2,1)S(1)}, u32[]{:S(2)}, u32[]{:S(2)}) collective-permute-start(bf16[2064,128]{1,0:T(8,128)(2,1)} %get-tuple-element.52.q1_ref), channel_id=1, source_target_pairs={{0,24},{8,0},{16,8},{24,16},{1,25},{9,1},{17,9},{25,17},{2,26},{10... | collective-permute-start | bytes 1585160 | tf_op jit(solution)/shard_map/ppermute | solution.py:566
  45.0 5.5 %phi_part.3 = (bf16[256,2048]{1,0:T(8,128)(2,1)S(1)}, f32[8,256,256]{2,1,0:T(8,128)S(1)}) custom-call(s32[256]{0:T(256)S(1)} %slice.24.which_ref, bf16[128,2048]{1,0:T(8,128)(2,1)S(1)} %get-tuple-element.61.refs_0_, bf16[128,2048]{1,0:T(8,128)(2,1)} %get-tuple-element.60.refs_1_, bf16[257,128,128]{2,1,0:T(8,128)(2,1)S(1)} %get-tuple-element.57.refs_2_.hk_ref), custom_call_target="tpu_custom_call" | custom-call | flops 2147483648 | bytes 1048576 | tf_op jit(solution)/shard_map/phi_part/pallas_call | solution.py:174
  50.5 6.6 %collective-permute-done.6.refs_3_ = bf16[128,2048]{1,0:T(8,128)(2,1)S(1)} collective-permute-done((bf16[128,2048]{1,0:T(8,128)(2,1)S(1)}, bf16[128,2048]{1,0:T(8,128)(2,1)S(1)}, u32[]{:S(2)}, u32[]{:S(2)}) %collective-permute-start.6) | collective-permute-done | bytes 524320 | tf_op jit(solution)/shard_map/ppermute | solution.py:491
  57.1 6.1 %action_part.3 = (bf16[256,2048]{1,0:T(8,128)(2,1)S(1)}, bf16[2064,128]{1,0:T(8,128)(2,1)}, bf16[2064,128]{1,0:T(8,128)(2,1)}) custom-call(s32[259]{0:T(512)S(1)} %pad_add_fusion.which_ref, bf16[256,2048]{1,0:T(8,128)(2,1)S(1)} %get-tuple-element.58.refs_0_.rows_ref, f32[8,256,256]{2,1,0:T(8,128)S(1)} %get-tuple-element.59.refs_1_, ...), custom_call_target="tpu_custom_call" | custom-call | flops 2147483648 | bytes 1048576 | tf_op jit(solution)/shard_map/action_part/pallas_call | solution.py:265
  63.2 1.0 copy-done.10
  64.2 1.6 %collective-permute-start.7 = (bf16[2064,128]{1,0:T(8,128)(2,1)}, bf16[2064,128]{1,0:T(8,128)(2,1)S(1)}, u32[]{:S(2)}, u32[]{:S(2)}) collective-permute-start(bf16[2064,128]{1,0:T(8,128)(2,1)} %get-tuple-element.63.q0_ref), channel_id=1, source_target_pairs={{0,8},{8,16},{16,24},{24,0},{1,9},{9,17},{17,25},{25,1},{2,10},{10... | collective-permute-start | bytes 1585160 | tf_op jit(solution)/shard_map/ppermute | solution.py:565
  65.8 2.2 %collective-permute-start.8 = (bf16[2064,128]{1,0:T(8,128)(2,1)}, bf16[2064,128]{1,0:T(8,128)(2,1)S(1)}, u32[]{:S(2)}, u32[]{:S(2)}) collective-permute-start(bf16[2064,128]{1,0:T(8,128)(2,1)} %get-tuple-element.64.q1_ref), channel_id=1, source_target_pairs={{0,24},{8,0},{16,8},{24,16},{1,25},{9,1},{17,9},{25,17},{2,26},{10... | collective-permute-start | bytes 1585160 | tf_op jit(solution)/shard_map/ppermute | solution.py:566
  68.0 0.1 copy.16
  68.1 0.1 slice.22.which_ref
  68.2 2.3 %send_onward.2 = (bf16[2048,128]{1,0:T(8,128)(2,1)S(1)}, bf16[2048,128]{1,0:T(8,128)(2,1)S(1)}) custom-call(s32[1]{0:T(128)} %bitcast.5.away_ref, bf16[2064,128]{1,0:T(8,128)(2,1)} %get-tuple-element.51.q0_ref, bf16[2064,128]{1,0:T(8,128)(2,1)} %get-tuple-element.52.q1_ref, bf16[2064,128]{1,0:T(8,128)(2,1)S(1)} %collective-permute-done.3.right_ref.right_code, ...), custom_call_target="tpu_custom_call" | custom-call | bytes 3170304 | tf_op jit(solution)/shard_map/send_onward/pallas_call | solution.py:299
  70.5 0.3 collective-permute-start.9
  70.8 3.6 %collective-permute-start.10 = (bf16[2048,128]{1,0:T(8,128)(2,1)S(1)}, bf16[2048,128]{1,0:T(8,128)(2,1)S(1)}, u32[]{:S(2)}, u32[]{:S(2)}) collective-permute-start(bf16[2048,128]{1,0:T(8,128)(2,1)S(1)} %get-tuple-element.73), channel_id=1, source_target_pairs={{0,24},{8,0},{16,8},{24,16},{1,25},{9,1},{17,9},{25,17},{2,26},{10... | collective-permute-start | bytes 1572872 | tf_op jit(solution)/shard_map/ppermute | solution.py:573
  74.4 3.4 %copy-done.1 = bf16[257,128,128]{2,1,0:T(8,128)(2,1)S(1)} copy-done((bf16[257,128,128]{2,1,0:T(8,128)(2,1)S(1)}, bf16[257,128,128]{2,1,0:T(8,128)(2,1)}, u32[]{:S(2)}) %copy-start.1) | copy-done | bytes 8421400
  77.8 3.4 %copy-done.4 = bf16[257,128,128]{2,1,0:T(8,128)(2,1)S(1)} copy-done((bf16[257,128,128]{2,1,0:T(8,128)(2,1)S(1)}, bf16[257,128,128]{2,1,0:T(8,128)(2,1)}, u32[]{:S(2)}) %copy-start.4) | copy-done | bytes 8421400
  81.2 1.2 copy-done.9
  82.4 1.2 copy-done.13
  83.6 6.7 %local_columns.2.refs_0_ = bf16[4096,128]{1,0:T(8,128)(2,1)S(1)} custom-call(s32[256]{0:T(256)S(1)} %slice.22.which_ref, bf16[256,2048]{1,0:T(8,128)(2,1)S(1)} %copy-done.13, bf16[256,2048]{1,0:T(8,128)(2,1)S(1)} %copy-done.9, bf16[257,128,128]{2,1,0:T(8,128)(2,1)S(1)} %copy-done.1, bf16[257,128,128]{2,1,0:T(8,128)(2,1)S(1)} %copy-done.4, ...), custom_call_target="tpu_custom_call" | custom-call | flops 4294967296 | bytes 1048576 | tf_op jit(solution)/shard_map/local_columns/pallas_call | solution.py:346
  90.3 2.4 %collective-permute-done.8.left_ref.left_code = bf16[2064,128]{1,0:T(8,128)(2,1)S(1)} collective-permute-done((bf16[2064,128]{1,0:T(8,128)(2,1)}, bf16[2064,128]{1,0:T(8,128)(2,1)S(1)}, u32[]{:S(2)}, u32[]{:S(2)}) %collective-permute-start.8) | collective-permute-done | bytes 528416 | tf_op jit(solution)/shard_map/ppermute | solution.py:566
  92.7 2.3 %send_onward.3 = (bf16[2048,128]{1,0:T(8,128)(2,1)S(1)}, bf16[2048,128]{1,0:T(8,128)(2,1)S(1)}) custom-call(s32[1]{0:T(128)} %bitcast.5.away_ref, bf16[2064,128]{1,0:T(8,128)(2,1)} %get-tuple-element.63.q0_ref, bf16[2064,128]{1,0:T(8,128)(2,1)} %get-tuple-element.64.q1_ref, bf16[2064,128]{1,0:T(8,128)(2,1)S(1)} %collective-permute-done.7.right_ref.right_code, ...), custom_call_target="tpu_custom_call" | custom-call | bytes 3170304 | tf_op jit(solution)/shard_map/send_onward/pallas_call | solution.py:299
  95.1 0.4 collective-permute-start.11
  95.5 3.5 %collective-permute-start.12 = (bf16[2048,128]{1,0:T(8,128)(2,1)S(1)}, bf16[2048,128]{1,0:T(8,128)(2,1)S(1)}, u32[]{:S(2)}, u32[]{:S(2)}) collective-permute-start(bf16[2048,128]{1,0:T(8,128)(2,1)S(1)} %get-tuple-element.76), channel_id=1, source_target_pairs={{0,24},{8,0},{16,8},{24,16},{1,25},{9,1},{17,9},{25,17},{2,26},{10... | collective-permute-start | bytes 1572872 | tf_op jit(solution)/shard_map/ppermute | solution.py:573
  98.9 16.1 %collective-permute-done.10.refs_4_ = bf16[2048,128]{1,0:T(8,128)(2,1)S(1)} collective-permute-done((bf16[2048,128]{1,0:T(8,128)(2,1)S(1)}, bf16[2048,128]{1,0:T(8,128)(2,1)S(1)}, u32[]{:S(2)}, u32[]{:S(2)}) %collective-permute-start.10) | collective-permute-done | bytes 524320 | tf_op jit(solution)/shard_map/ppermute | solution.py:573
  115.1 6.9 %local_columns.3.refs_1_ = bf16[4096,128]{1,0:T(8,128)(2,1)S(1)} custom-call(s32[256]{0:T(256)S(1)} %slice.22.which_ref, bf16[256,2048]{1,0:T(8,128)(2,1)S(1)} %copy-done.11, bf16[256,2048]{1,0:T(8,128)(2,1)S(1)} %get-tuple-element.58.refs_0_.rows_ref, bf16[257,128,128]{2,1,0:T(8,128)(2,1)S(1)} %copy-done.2, bf16[257,128,128]{2,1,0:T(8,128)(2,1)S(1)} %copy-done.5, ...), custom_call_target="tpu_custom_call" | custom-call | flops 4294967296 | bytes 1048576 | tf_op jit(solution)/shard_map/local_columns/pallas_call | solution.py:346
  122.0 1.0 copy-done.7
  123.0 3.3 %collective-permute-done.11.refs_3_ = bf16[2048,128]{1,0:T(8,128)(2,1)S(1)} collective-permute-done((bf16[2048,128]{1,0:T(8,128)(2,1)S(1)}, bf16[2048,128]{1,0:T(8,128)(2,1)S(1)}, u32[]{:S(2)}, u32[]{:S(2)}) %collective-permute-start.11) | collective-permute-done | bytes 524320 | tf_op jit(solution)/shard_map/ppermute | solution.py:572
  126.3 9.4 %collective-permute-done.12.refs_5_ = bf16[2048,128]{1,0:T(8,128)(2,1)S(1)} collective-permute-done((bf16[2048,128]{1,0:T(8,128)(2,1)S(1)}, bf16[2048,128]{1,0:T(8,128)(2,1)S(1)}, u32[]{:S(2)}, u32[]{:S(2)}) %collective-permute-start.12) | collective-permute-done | bytes 524320 | tf_op jit(solution)/shard_map/ppermute | solution.py:573
  135.6 0.8 copy-done.18
  136.4 5.7 %finish.1 = bf16[8192,128]{1,0:T(8,128)(2,1)} custom-call(bf16[512,512]{1,0:T(8,128)(2,1)} %constant.64.clone.mix_ref, bf16[4096,128]{1,0:T(8,128)(2,1)} %copy-done.6, bf16[4096,128]{1,0:T(8,128)(2,1)} %copy-done.7, bf16[2048,128]{1,0:T(8,128)(2,1)} %copy-done.15, bf16[2048,128]{1,0:T(8,128)(2,1)} %copy-done.17, bf16[2048,128]{1,0:T(8,128)(2,1)} %copy-done.16, ...), custom_call_target="tpu_custom_call" | custom-call | tf_op jit(solution)/shard_map/finish/pallas_call | solution.py:439
  (40 shorter events, 0.1 us)
Async XLA Ops:
  4.8 25.2 %collective-permute-start.2 = (bf16[4,2048]{1,0:T(4,128)(2,1)S(1)}, bf16[4,2048]{1,0:T(4,128)(2,1)S(1)}, u32[]{:S(2)}, u32[]{:S(2)}) collective-permute-start(bf16[4,2048]{1,0:T(4,128)(2,1)S(1)} %get-tuple-element.41), channel_id=1, source_target_pairs={{0,1},{1,0},{2,3},{3,2},{4,5},{5,4},{6,7},{7,6},{8,9},{9,8},{10,11... | collective-permute-start | bytes 49160 | tf_op jit(solution)/shard_map/ppermute | solution.py:473
  5.2 24.7 %collective-permute-start = (bf16[128,2048]{1,0:T(8,128)(2,1)S(1)}, bf16[128,2048]{1,0:T(8,128)(2,1)S(1)}, u32[]{:S(2)}, u32[]{:S(2)}) collective-permute-start(bf16[128,2048]{1,0:T(8,128)(2,1)S(1)} %get-tuple-element.45.refs_1_), channel_id=1, source_target_pairs={{0,2},{2,4},{4,6},{1,3},{3,5},{5,7},{8,10},{10,12},{12,14},{9,11},... | collective-permute-start | bytes 1572872 | tf_op jit(solution)/shard_map/ppermute | solution.py:491
  9.6 25.4 %collective-permute-start.1 = (bf16[128,2048]{1,0:T(8,128)(2,1)S(1)}, bf16[128,2048]{1,0:T(8,128)(2,1)S(1)}, u32[]{:S(2)}, u32[]{:S(2)}) collective-permute-start(bf16[128,2048]{1,0:T(8,128)(2,1)S(1)} %get-tuple-element.44.refs_0_), channel_id=1, source_target_pairs={{2,0},{4,2},{6,4},{3,1},{5,3},{7,5},{10,8},{12,10},{14,12},{11,9},... | collective-permute-start | bytes 1572872 | tf_op jit(solution)/shard_map/ppermute | solution.py:491
  16.3 34.1 %collective-permute-start.5 = (bf16[128,2048]{1,0:T(8,128)(2,1)}, bf16[128,2048]{1,0:T(8,128)(2,1)S(1)}, u32[]{:S(2)}, u32[]{:S(2)}) collective-permute-start(bf16[128,2048]{1,0:T(8,128)(2,1)} %get-tuple-element.60.refs_1_), channel_id=1, source_target_pairs={{0,2},{2,4},{4,6},{1,3},{3,5},{5,7},{8,10},{10,12},{12,14},{9,11},... | collective-permute-start | bytes 1572872 | tf_op jit(solution)/shard_map/ppermute | solution.py:491
  20.9 36.2 %collective-permute-start.6 = (bf16[128,2048]{1,0:T(8,128)(2,1)S(1)}, bf16[128,2048]{1,0:T(8,128)(2,1)S(1)}, u32[]{:S(2)}, u32[]{:S(2)}) collective-permute-start(bf16[128,2048]{1,0:T(8,128)(2,1)S(1)} %get-tuple-element.61.refs_0_), channel_id=1, source_target_pairs={{2,0},{4,2},{6,4},{3,1},{5,3},{7,5},{10,8},{12,10},{14,12},{11,9},... | collective-permute-start | bytes 1572872 | tf_op jit(solution)/shard_map/ppermute | solution.py:491
  22.2 12.8 %copy-start.14 = (bf16[256,512]{1,0:T(8,128)(2,1)S(1)}, bf16[256,512]{1,0:T(8,128)(2,1)}, u32[]{:S(2)}) copy-start(bf16[256,512]{1,0:T(8,128)(2,1)} %constant.65.clone.refs_7_) | copy-start | bytes 786436
  29.9 20.5 %copy-start.3 = (bf16[257,128,128]{2,1,0:T(8,128)(2,1)}, bf16[257,128,128]{2,1,0:T(8,128)(2,1)S(1)}, u32[]{:S(2)}) copy-start(bf16[257,128,128]{2,1,0:T(8,128)(2,1)S(1)} %get-tuple-element.57.refs_2_.hk_ref) | copy-start | bytes 25264132
  30.0 20.5 %copy-start.8 = (bf16[256,2048]{1,0:T(8,128)(2,1)}, bf16[256,2048]{1,0:T(8,128)(2,1)S(1)}, u32[]{:S(2)}) copy-start(bf16[256,2048]{1,0:T(8,128)(2,1)S(1)} %get-tuple-element.46.refs_0_.rows_ref) | copy-start | bytes 3145732
  30.0 27.1 %copy-start = (bf16[257,128,128]{2,1,0:T(8,128)(2,1)}, bf16[257,128,128]{2,1,0:T(8,128)(2,1)S(1)}, u32[]{:S(2)}) copy-start(bf16[257,128,128]{2,1,0:T(8,128)(2,1)S(1)} %get-tuple-element.50.refs_8_.kern_ref) | copy-start | bytes 25264132
  41.2 22.0 %copy-start.12 = (bf16[256,2048]{1,0:T(8,128)(2,1)}, bf16[256,2048]{1,0:T(8,128)(2,1)S(1)}, u32[]{:S(2)}) copy-start(bf16[256,2048]{1,0:T(8,128)(2,1)S(1)} %get-tuple-element.69.act_ref) | copy-start | bytes 3145732
  41.2 27.0 %collective-permute-start.3 = (bf16[2064,128]{1,0:T(8,128)(2,1)}, bf16[2064,128]{1,0:T(8,128)(2,1)S(1)}, u32[]{:S(2)}, u32[]{:S(2)}) collective-permute-start(bf16[2064,128]{1,0:T(8,128)(2,1)} %get-tuple-element.51.q0_ref), channel_id=1, source_target_pairs={{0,8},{8,16},{16,24},{24,0},{1,9},{9,17},{17,25},{25,1},{2,10},{10... | collective-permute-start | bytes 1585160 | tf_op jit(solution)/shard_map/ppermute | solution.py:565
  42.8 25.4 %collective-permute-start.4 = (bf16[2064,128]{1,0:T(8,128)(2,1)}, bf16[2064,128]{1,0:T(8,128)(2,1)S(1)}, u32[]{:S(2)}, u32[]{:S(2)}) collective-permute-start(bf16[2064,128]{1,0:T(8,128)(2,1)} %get-tuple-element.52.q1_ref), channel_id=1, source_target_pairs={{0,24},{8,0},{16,8},{24,16},{1,25},{9,1},{17,9},{25,17},{2,26},{10... | collective-permute-start | bytes 1585160 | tf_op jit(solution)/shard_map/ppermute | solution.py:566
  63.2 1.0 copy-start.10
  64.2 26.2 %collective-permute-start.7 = (bf16[2064,128]{1,0:T(8,128)(2,1)}, bf16[2064,128]{1,0:T(8,128)(2,1)S(1)}, u32[]{:S(2)}, u32[]{:S(2)}) collective-permute-start(bf16[2064,128]{1,0:T(8,128)(2,1)} %get-tuple-element.63.q0_ref), channel_id=1, source_target_pairs={{0,8},{8,16},{16,24},{24,0},{1,9},{9,17},{17,25},{25,1},{2,10},{10... | collective-permute-start | bytes 1585160 | tf_op jit(solution)/shard_map/ppermute | solution.py:565
  65.8 27.0 %collective-permute-start.8 = (bf16[2064,128]{1,0:T(8,128)(2,1)}, bf16[2064,128]{1,0:T(8,128)(2,1)S(1)}, u32[]{:S(2)}, u32[]{:S(2)}) collective-permute-start(bf16[2064,128]{1,0:T(8,128)(2,1)} %get-tuple-element.64.q1_ref), channel_id=1, source_target_pairs={{0,24},{8,0},{16,8},{24,16},{1,25},{9,1},{17,9},{25,17},{2,26},{10... | collective-permute-start | bytes 1585160 | tf_op jit(solution)/shard_map/ppermute | solution.py:566
  70.5 44.5 %collective-permute-start.9 = (bf16[2048,128]{1,0:T(8,128)(2,1)S(1)}, bf16[2048,128]{1,0:T(8,128)(2,1)S(1)}, u32[]{:S(2)}, u32[]{:S(2)}) collective-permute-start(bf16[2048,128]{1,0:T(8,128)(2,1)S(1)} %get-tuple-element.67), channel_id=1, source_target_pairs={{0,8},{8,16},{16,24},{24,0},{1,9},{9,17},{17,25},{25,1},{2,10},{10... | collective-permute-start | bytes 1572872 | tf_op jit(solution)/shard_map/ppermute | solution.py:572
  70.8 44.3 %collective-permute-start.10 = (bf16[2048,128]{1,0:T(8,128)(2,1)S(1)}, bf16[2048,128]{1,0:T(8,128)(2,1)S(1)}, u32[]{:S(2)}, u32[]{:S(2)}) collective-permute-start(bf16[2048,128]{1,0:T(8,128)(2,1)S(1)} %get-tuple-element.73), channel_id=1, source_target_pairs={{0,24},{8,0},{16,8},{24,16},{1,25},{9,1},{17,9},{25,17},{2,26},{10... | collective-permute-start | bytes 1572872 | tf_op jit(solution)/shard_map/ppermute | solution.py:573
  74.4 3.4 %copy-start.1 = (bf16[257,128,128]{2,1,0:T(8,128)(2,1)S(1)}, bf16[257,128,128]{2,1,0:T(8,128)(2,1)}, u32[]{:S(2)}) copy-start(bf16[257,128,128]{2,1,0:T(8,128)(2,1)} %copy-done) | copy-start | bytes 25264132
  77.8 3.4 %copy-start.4 = (bf16[257,128,128]{2,1,0:T(8,128)(2,1)S(1)}, bf16[257,128,128]{2,1,0:T(8,128)(2,1)}, u32[]{:S(2)}) copy-start(bf16[257,128,128]{2,1,0:T(8,128)(2,1)} %copy-done.3) | copy-start | bytes 25264132
  81.2 1.2 copy-start.9
  82.4 1.2 copy-start.13
  83.6 31.4 %copy-start.2 = (bf16[257,128,128]{2,1,0:T(8,128)(2,1)S(1)}, bf16[257,128,128]{2,1,0:T(8,128)(2,1)}, u32[]{:S(2)}) copy-start(bf16[257,128,128]{2,1,0:T(8,128)(2,1)} %copy-done) | copy-start | bytes 25264132
  83.6 31.4 %copy-start.5 = (bf16[257,128,128]{2,1,0:T(8,128)(2,1)S(1)}, bf16[257,128,128]{2,1,0:T(8,128)(2,1)}, u32[]{:S(2)}) copy-start(bf16[257,128,128]{2,1,0:T(8,128)(2,1)} %copy-done.3) | copy-start | bytes 25264132
  83.6 31.4 %copy-start.11 = (bf16[256,2048]{1,0:T(8,128)(2,1)S(1)}, bf16[256,2048]{1,0:T(8,128)(2,1)}, u32[]{:S(2)}) copy-start(bf16[256,2048]{1,0:T(8,128)(2,1)} %copy-done.10) | copy-start | bytes 3145732
  90.3 31.6 %copy-start.6 = (bf16[4096,128]{1,0:T(8,128)(2,1)}, bf16[4096,128]{1,0:T(8,128)(2,1)S(1)}, u32[]{:S(2)}) copy-start(bf16[4096,128]{1,0:T(8,128)(2,1)S(1)} %local_columns.2.refs_0_) | copy-start | bytes 3145732
  95.1 31.2 %collective-permute-start.11 = (bf16[2048,128]{1,0:T(8,128)(2,1)S(1)}, bf16[2048,128]{1,0:T(8,128)(2,1)S(1)}, u32[]{:S(2)}, u32[]{:S(2)}) collective-permute-start(bf16[2048,128]{1,0:T(8,128)(2,1)S(1)} %get-tuple-element.72), channel_id=1, source_target_pairs={{0,8},{8,16},{16,24},{24,0},{1,9},{9,17},{17,25},{25,1},{2,10},{10... | collective-permute-start | bytes 1572872 | tf_op jit(solution)/shard_map/ppermute | solution.py:572
  95.5 40.1 %collective-permute-start.12 = (bf16[2048,128]{1,0:T(8,128)(2,1)S(1)}, bf16[2048,128]{1,0:T(8,128)(2,1)S(1)}, u32[]{:S(2)}, u32[]{:S(2)}) collective-permute-start(bf16[2048,128]{1,0:T(8,128)(2,1)S(1)} %get-tuple-element.76), channel_id=1, source_target_pairs={{0,24},{8,0},{16,8},{24,16},{1,25},{9,1},{17,9},{25,17},{2,26},{10... | collective-permute-start | bytes 1572872 | tf_op jit(solution)/shard_map/ppermute | solution.py:573
  115.1 6.9 %copy-start.16 = (bf16[2048,128]{1,0:T(8,128)(2,1)}, bf16[2048,128]{1,0:T(8,128)(2,1)S(1)}, u32[]{:S(2)}) copy-start(bf16[2048,128]{1,0:T(8,128)(2,1)S(1)} %collective-permute-done.10.refs_4_) | copy-start | bytes 1572868
  115.1 6.9 %copy-start.15 = (bf16[2048,128]{1,0:T(8,128)(2,1)}, bf16[2048,128]{1,0:T(8,128)(2,1)S(1)}, u32[]{:S(2)}) copy-start(bf16[2048,128]{1,0:T(8,128)(2,1)S(1)} %collective-permute-done.9.refs_2_) | copy-start | bytes 1572868
  122.0 1.0 copy-start.7
  126.3 9.4 %copy-start.17 = (bf16[2048,128]{1,0:T(8,128)(2,1)}, bf16[2048,128]{1,0:T(8,128)(2,1)S(1)}, u32[]{:S(2)}) copy-start(bf16[2048,128]{1,0:T(8,128)(2,1)S(1)} %collective-permute-done.11.refs_3_) | copy-start | bytes 1572868
  135.6 0.8 copy-start.18

commit v3 on v2

--- a/solution.py
+++ b/solution.py
@@ -8,11 +8,15 @@
 from jax.experimental.pallas import tpu as pltpu
 from jax.sharding import PartitionSpec as P
 
-CUTS = (0, 128, 256)
+CUTS = (0, 96, 176, 256)
 RIGHT, ACROSS, LEFT = 1, 2, 3
 LANES = 128
-SCOPED = 14 << 20
+SCOPED = 8 << 20
 VMEM = pl.BlockSpec(memory_space=pltpu.VMEM)
+
+
+def hinted(flops):
+    return flops // 4
 
 
 def in_hbm(*arrays):
@@ -183,7 +187,7 @@
         out_shape=out_shape,
         compiler_params=pltpu.CompilerParams(vmem_limit_bytes=SCOPED),
         cost_estimate=pl.CostEstimate(
-            flops=4 * n * width * pairs * block, transcendentals=0, bytes_accessed=2 * n * width
+            flops=hinted(4 * n * width * pairs * block), transcendentals=0, bytes_accessed=2 * n * width
         ),
         name="phi_part",
     )(which, *fields, *(in_hbm(kern, kern_hk) if loads else [kern_hk]))
@@ -274,7 +278,7 @@
         + [pltpu.VMEM((rows_out, block), jnp.bfloat16) for rows_out in out_rows],
         compiler_params=pltpu.CompilerParams(vmem_limit_bytes=SCOPED),
         cost_estimate=pl.CostEstimate(
-            flops=2 * n * width * cols * block, transcendentals=0, bytes_accessed=2 * n * width
+            flops=hinted(2 * n * width * cols * block), transcendentals=0, bytes_accessed=2 * n * width
         ),
         name="action_part",
     )(which, rows, partial, prev, below, low, high, pot, stencil_matrix(zc, rows_y), kern)
@@ -356,7 +360,7 @@
         out_shape=jax.ShapeDtypeStruct((cols * n, block), jnp.bfloat16),
         compiler_params=pltpu.CompilerParams(vmem_limit_bytes=SCOPED),
         cost_estimate=pl.CostEstimate(
-            flops=4 * n * width * cols * block, transcendentals=0, bytes_accessed=2 * n * width
+            flops=hinted(4 * n * width * cols * block), transcendentals=0, bytes_accessed=2 * n * width
         ),
         name="local_columns",
     )(which, act, rows, kern, kern_hk, left1, left1, right1, right1)
@@ -389,63 +393,53 @@
             )
 
 
-def final_kernel(per_step, chunks, rows_y, tiles, mix_ref, *refs):
-    own, rest, out_ref = refs[:chunks], refs[chunks:-1], refs[-1]
-    step = pl.program_id(0)
-    half = pl.num_programs(0) // 2
-
-    def emit(added):
-        columns = []
-        for col in range(per_step):
-            values = []
-            for chunk, mine in enumerate(own):
-                n = mine.shape[0] // per_step
-                at = slice(col * n, (col + 1) * n)
-                value = mine[at, :].astype(jnp.float32)
-                values.append(value + added[chunk][at, :].astype(jnp.float32) if added else value)
-            columns.append(values)
-        write_columns(rows_y, tiles, columns, mix_ref, out_ref)
-
-    if not rest:
-        emit(())
-        return
-
-    @pl.when(step < half)
-    def _():
-        emit(rest[:chunks])
-
-    @pl.when(step >= half)
-    def _():
-        emit(rest[chunks:])
-
-
-def finish(own, low, high, cols, rows_y, rows_z):
-    chunks = len(own)
-    block = own[0].shape[1]
+def final_kernel(per_step, counts, rows_y, tiles, mix_ref, *refs):
+    out_ref = refs[-1]
+    columns = []
+    for col in range(per_step):
+        values, first = [], 0
+        for count in counts:
+            n = refs[first].shape[0] // per_step
+            at = slice(col * n, (col + 1) * n)
+            values.append(sum(ref[at, :].astype(jnp.float32) for ref in refs[first : first + count]))
+            first += count
+        columns.append(values)
+    write_columns(rows_y, tiles, columns, mix_ref, out_ref)
+
+
+def finish(parts, firsts, cols, all_cols, rows_y, rows_z, before=None):
+    arrays = [array for part in parts for array in part]
+    block = arrays[0].shape[1]
     tiles = rows_z // LANES
     rows = block * tiles * rows_y
     per_step = 4
-    steps = cols // per_step
-    half = steps // 2
-
-    def specs(place):
-        return [pl.BlockSpec((part.shape[0] // steps, block), lambda s: (place(s), 0)) for part in own]
-
-    in_specs = [pl.BlockSpec((rows, rows), lambda s: (0, 0))] + specs(lambda s: s)
-    arrays = list(own)
-    if low is not None:
-        in_specs += specs(lambda s: jnp.minimum(s, half - 1)) + specs(lambda s: jnp.maximum(s - half, 0))
-        arrays += [*low, *high]
-    flat = pl.pallas_call(
-        functools.partial(final_kernel, per_step, chunks, rows_y, tiles),
-        grid=(steps,),
+    start = firsts[0] // per_step
+    in_specs = [pl.BlockSpec((rows, rows), lambda s: (0, 0))]
+    for part in parts:
+        n = part[0].shape[0] // all_cols
+        for first, _ in zip(firsts, part):
+            in_specs.append(
+                pl.BlockSpec((per_step * n, block), functools.partial(lambda at, s: (s + at, 0), first // per_step))
+            )
+    arrays = in_hbm(regroup_matrix(block, tiles * rows_y), *arrays)
+    counts = [len(part) for part in parts]
+    kernel = functools.partial(final_kernel, per_step, counts, rows_y, tiles)
+    aliases = {}
+    if before is not None:
+        aliases = {len(arrays): 0}
+        arrays.append(before)
+        in_specs.append(pl.BlockSpec(memory_space=pl.ANY))
+        kernel = lambda *refs: final_kernel(per_step, counts, rows_y, tiles, *refs[:-2], refs[-1])
+    return pl.pallas_call(
+        kernel,
+        grid=(cols // per_step,),
         in_specs=in_specs,
-        out_specs=pl.BlockSpec((per_step * rows, LANES), lambda s: (s, 0)),
-        out_shape=jax.ShapeDtypeStruct((cols * rows, LANES), jnp.bfloat16),
+        out_specs=pl.BlockSpec((per_step * rows, LANES), lambda s: (s + start, 0)),
+        out_shape=jax.ShapeDtypeStruct((all_cols * rows, LANES), jnp.bfloat16),
+        input_output_aliases=aliases,
         compiler_params=pltpu.CompilerParams(vmem_limit_bytes=SCOPED),
         name="finish",
-    )(*in_hbm(regroup_matrix(block, tiles * rows_y), *arrays))
-    return unflatten(flat, cols, block, rows_y, tiles)
+    )(*arrays)
 
 
 def unflatten(flat, cols, block, rows_y, tiles):
@@ -530,8 +524,9 @@
             _, sums = all_columns(c, *phi_columns(c, which), table, listed, 1)
             spread = jnp.where(named[:, None, None], sums.reshape(listed, -1, block)[source], 0)
             total = lax.psum_scatter(spread, "gx", scatter_dimension=0, tiled=True)
-            parts.append(total.reshape(-1, block))
-        return finish(parts, None, None, groups, rows_y, rows_z)
+            parts.append([total.reshape(-1, block)])
+        flat = finish(parts, (0,), groups, groups, rows_y, rows_z)
+        return unflatten(flat, groups, block, rows_y, rows_z // LANES)
 
     me = lax.axis_index("gx")
     owners = req_cols // groups
@@ -551,8 +546,7 @@
     far, near = which[: groups * groups], which[groups * groups :]
     table = jnp.concatenate([far, jnp.stack([*marks, away]).astype(jnp.int32)])
     away = away.reshape(1)
-    for c in range(1, chunks):
-        send_halo(c, table)
+    send_halo(1, table)
 
     rows, acts, sent, own, right1, left1, right2, left2 = [], [], [], [], [], [], [], []
 
@@ -577,10 +571,15 @@
 
     send_first(0)
     for c in range(1, chunks):
+        if c + 1 < chunks:
+            send_halo(c + 1, sent[c - 1][1])
         send_first(c, *sent[c - 1])
         send_second(c - 1, *sent[c])
     send_second(chunks - 1, own[-1])
-    return finish(own, right2, left2, groups, rows_y, rows_z)
+    flat = finish(list(zip(own, right2)), (0, 0), half, groups, rows_y, rows_z)
+    left2 = lax.optimization_barrier((*left2, flat))
+    flat = finish(list(zip(own, left2)), (half, 0), half, groups, rows_y, rows_z, left2[-1])
+    return unflatten(flat, groups, block, rows_y, rows_z // LANES)
 
 
 def solution(mesh):

time: 143 us -> 135 us (0.944); the launches traced: 142 us -> 132 us
  waiting for transfers between devices: 42.8 us -> 16.4 us
  starting transfers between devices: 27.4 us -> 37.5 us
  Pallas kernels: 54 us -> 63.6 us
  other arithmetic: 2.52 us -> 0.51 us
    ppermute x2 -> x3, waiting for transfers between devices: 25.5 us -> 0.56 us  [send_second(): left2.append(lax.ppermute(to_left, 'gx', behind))]
    ppermute x2 -> x3, waiting for transfers between devices: 2.38 us -> 13.9 us  [send_first(): left1.append(lax.ppermute(q1, 'gx', behind))]
    ppermute x2 -> x3, waiting for transfers between devices: 11.6 us -> 1.97 us  [send_halo(): lax.ppermute(down, 'gy', shifts('gy', -1))]
    ppermute x2 -> x3, starting transfers between devices: 4.46 us -> 9.88 us  [send_first(): left1.append(lax.ppermute(q1, 'gx', behind))]
    ppermute x2 -> x3, starting transfers between devices: 8.97 us -> 12.8 us  [send_halo(): lax.ppermute(up, 'gy', shifts('gy', 1))]
    ppermute x2 -> x3, waiting for transfers between devices: 3.29 us -> 0.01 us  [send_second(): right2.append(lax.ppermute(to_right, 'gx', ahead))]
    pallas_call x2 -> x3, Pallas kernels: 13.5 us -> 16 us  [local_columns(): pl.pallas_call(functools.partial(local_kernel, groups), grid_spec=pltpu.P...]
    pallas_call x2 -> x3, Pallas kernels: 13.2 us -> 15.4 us  [phi_part(): pl.pallas_call(functools.partial(phi_kernel, groups, len(fields), loads),...]
  transfers between devices with their start and end apart: 13 -> 19, of which waited for: 6 -> 4; matrix products, arithmetic and copies ran while one was open for 2% -> 1% of each run, Pallas kernels for 31% -> 42%
where the time goes in v3:
time: 135 us; the launch traced here: 132 us
  Pallas kernels  63.6 us (47%)
  starting transfers between devices  37.5 us (28%)
  waiting for transfers between devices  16.4 us (12%)
  local copies, waits for them, and re-layouts  11.9 us (9%)
  between operations  2.39 us (2%)
    pallas_call x3, Pallas kernels, local_columns(): pl.pallas_call(functools.partial(local_kernel, groups), grid_spec=pltpu.P...  16 us
    pallas_call x3, Pallas kernels, phi_part(): pl.pallas_call(functools.partial(phi_kernel, groups, len(fields), loads),...  15.4 us
    pallas_call x3, Pallas kernels, action_part(): pl.pallas_call(functools.partial(action_kernel, groups, rows_y, cols, low...  14.4 us
    ppermute x3, waiting for transfers between devices, send_first(): left1.append(lax.ppermute(q1, 'gx', behind))  13.9 us
    ppermute x3, starting transfers between devices, send_halo(): lax.ppermute(up, 'gy', shifts('gy', 1))  12.8 us
    unnamed x52, local copies, waits for them, and re-layouts  10.9 us
    ppermute x3, starting transfers between devices, send_first(): left1.append(lax.ppermute(q1, 'gx', behind))  9.88 us
    pallas_call x2, Pallas kernels, finish(): pl.pallas_call(kernel, grid=(cols // per_step,), in_specs=in_specs, out_s...  6.9 us
  transfers between devices with their start and end apart: 19, of which 4 were waited for; matrix products, arithmetic and copies ran while one was open for 1% of the time, Pallas kernels for 42%

profile of v3, /device:TPU:0, one launch (start us, length us, event | category | flops | bytes accessed | tf_op | source)
XLA Modules:
  0.0 132.3 jit_solution(16635930934577189243)
XLA Ops:
  0.0 4.8 %prepare.1 = (bf16[96,2048]{1,0:T(8,128)(2,1)S(1)}, bf16[96,2048]{1,0:T(8,128)(2,1)S(1)}, bf16[80,2048]{1,0:T(8,128)(2,1)S(1)}, bf16[80,2048]{1,0:T(8,128)(2,1)S...) custom-call(bf16[8192,128]{1,0:T(8,128)(2,1)} %bitcast.19, ...), custom_call_target="tpu_custom_call" | custom-call | tf_op jit(solution)/shard_map/prepare/pallas_call | solution.py:101
  4.8 4.9 %collective-permute-start = (bf16[96,2048]{1,0:T(8,128)(2,1)S(1)}, bf16[96,2048]{1,0:T(8,128)(2,1)S(1)}, u32[]{:S(2)}, u32[]{:S(2)}) collective-permute-start(bf16[96,2048]{1,0:T(8,128)(2,1)S(1)} %get-tuple-element.66.refs_1_), channel_id=1, source_target_pairs={{0,2},{2,4},{4,6},{1,3},{3,5},{5,7},{8,10},{10,12},{12,14},{9,11},... | collective-permute-start | bytes 1179656 | tf_op jit(solution)/shard_map/ppermute | solution.py:485
  9.7 1.3 collective-permute-start.1
  11.1 0.6 fusion.3
  13.6 0.1 pad_add_fusion.1
  13.6 0.2 select_reduce_fusion.1
  13.8 0.1 select_reduce_fusion
  14.0 0.1 fusion.2
  14.2 0.1 slice.24.which_ref
  14.2 0.1 pad_add_fusion.which_ref
  14.3 4.6 %collective-permute-start.5 = (bf16[80,2048]{1,0:T(8,128)(2,1)S(1)}, bf16[80,2048]{1,0:T(8,128)(2,1)S(1)}, u32[]{:S(2)}, u32[]{:S(2)}) collective-permute-start(bf16[80,2048]{1,0:T(8,128)(2,1)S(1)} %get-tuple-element.81.refs_1_), channel_id=1, source_target_pairs={{0,2},{2,4},{4,6},{1,3},{3,5},{5,7},{8,10},{10,12},{12,14},{9,11},... | collective-permute-start | bytes 983048 | tf_op jit(solution)/shard_map/ppermute | solution.py:485
  18.9 1.3 collective-permute-start.6
  20.3 7.3 %phi_part.3 = (bf16[192,2048]{1,0:T(8,128)(2,1)S(1)}, f32[8,192,256]{2,1,0:T(8,128)S(1)}, bf16[257,128,128]{2,1,0:T(8,128)(2,1)S(1)}, bf16[257,128,128]{2,1,0:T(8,128)(2,1)S(1)}) custom-call(s32[256]{0:T(256)S(1)} %slice.24.which_ref, bf16[96,2048]{1,0:T(8,128)(2,1)S(1)} %get-tuple-element.65.refs_0_, bf16[96,2048]{1,0:T(8,128)(2,1)S(1)} %get-tuple-element.66.refs_1_, ...), custom_call_target="tpu_custom_call" | custom-call | flops 402653184 | bytes 786432 | tf_op jit(solution)/shard_map/phi_part/pallas_call | solution.py:178
  27.6 2.0 %collective-permute-done.1.refs_3_ = bf16[96,2048]{1,0:T(8,128)(2,1)S(1)} collective-permute-done((bf16[96,2048]{1,0:T(8,128)(2,1)S(1)}, bf16[96,2048]{1,0:T(8,128)(2,1)S(1)}, u32[]{:S(2)}, u32[]{:S(2)}) %collective-permute-start.1) | collective-permute-done | bytes 393248 | tf_op jit(solution)/shard_map/ppermute | solution.py:485
  29.6 4.5 %action_part.3 = (bf16[192,2048]{1,0:T(8,128)(2,1)S(1)}, bf16[1552,128]{1,0:T(8,128)(2,1)S(1)}, bf16[1552,128]{1,0:T(8,128)(2,1)S(1)}) custom-call(s32[259]{0:T(512)S(1)} %pad_add_fusion.which_ref, bf16[192,2048]{1,0:T(8,128)(2,1)S(1)} %get-tuple-element.67.refs_0_.rows_ref, f32[8,192,256]{2,1,0:T(8,128)S(1)} %get-tuple-element.68.refs_1_, ...), custom_call_target="tpu_custom_call" | custom-call | flops 402653184 | bytes 786432 | tf_op jit(solution)/shard_map/action_part/pallas_call | solution.py:269
  34.0 1.6 %collective-permute-start.3 = (bf16[1552,128]{1,0:T(8,128)(2,1)S(1)}, bf16[1552,128]{1,0:T(8,128)(2,1)S(1)}, u32[]{:S(2)}, u32[]{:S(2)}) collective-permute-start(bf16[1552,128]{1,0:T(8,128)(2,1)S(1)} %get-tuple-element.72.q0_ref), channel_id=1, source_target_pairs={{0,8},{8,16},{16,24},{24,0},{1,9},{9,17},{17,25},{25,1},{2,10},{10... | collective-permute-start | bytes 1191944 | tf_op jit(solution)/shard_map/ppermute | solution.py:559
  35.7 2.2 %collective-permute-start.4 = (bf16[1552,128]{1,0:T(8,128)(2,1)S(1)}, bf16[1552,128]{1,0:T(8,128)(2,1)S(1)}, u32[]{:S(2)}, u32[]{:S(2)}) collective-permute-start(bf16[1552,128]{1,0:T(8,128)(2,1)S(1)} %get-tuple-element.73.q1_ref), channel_id=1, source_target_pairs={{0,24},{8,0},{16,8},{24,16},{1,25},{9,1},{17,9},{25,17},{2,26},{10... | collective-permute-start | bytes 1191944 | tf_op jit(solution)/shard_map/ppermute | solution.py:560
  37.9 3.4 %collective-permute-start.10 = (bf16[80,2048]{1,0:T(8,128)(2,1)}, bf16[80,2048]{1,0:T(8,128)(2,1)S(1)}, u32[]{:S(2)}, u32[]{:S(2)}) collective-permute-start(bf16[80,2048]{1,0:T(8,128)(2,1)} %get-tuple-element.98.refs_1_), channel_id=1, source_target_pairs={{0,2},{2,4},{4,6},{1,3},{3,5},{5,7},{8,10},{10,12},{12,14},{9,11},... | collective-permute-start | bytes 983048 | tf_op jit(solution)/shard_map/ppermute | solution.py:485
  41.3 3.5 %phi_part.4 = (bf16[160,2048]{1,0:T(8,128)(2,1)S(1)}, f32[8,160,256]{2,1,0:T(8,128)S(1)}) custom-call(s32[256]{0:T(256)S(1)} %slice.24.which_ref, bf16[80,2048]{1,0:T(8,128)(2,1)S(1)} %get-tuple-element.82.refs_0_, bf16[80,2048]{1,0:T(8,128)(2,1)S(1)} %get-tuple-element.81.refs_1_, bf16[257,128,128]{2,1,0:T(8,128)(2,1)S(1)} %get-tuple-element.78.refs_2_.hk_ref), custom_call_target="tpu_custom_call" | custom-call | flops 335544320 | bytes 655360 | tf_op jit(solution)/shard_map/phi_part/pallas_call | solution.py:178
  44.9 1.3 collective-permute-start.11
  46.2 4.9 %action_part.4 = (bf16[160,2048]{1,0:T(8,128)(2,1)S(1)}, bf16[1296,128]{1,0:T(8,128)(2,1)S(1)}, bf16[1296,128]{1,0:T(8,128)(2,1)}) custom-call(s32[259]{0:T(512)S(1)} %pad_add_fusion.which_ref, bf16[160,2048]{1,0:T(8,128)(2,1)S(1)} %get-tuple-element.79.refs_0_.rows_ref, f32[8,160,256]{2,1,0:T(8,128)S(1)} %get-tuple-element.80.refs_1_, ...), custom_call_target="tpu_custom_call" | custom-call | flops 335544320 | bytes 655360 | tf_op jit(solution)/shard_map/action_part/pallas_call | solution.py:269
  51.1 2.4 %collective-permute-done.4.left_ref.left_code = bf16[1552,128]{1,0:T(8,128)(2,1)S(1)} collective-permute-done((bf16[1552,128]{1,0:T(8,128)(2,1)S(1)}, bf16[1552,128]{1,0:T(8,128)(2,1)S(1)}, u32[]{:S(2)}, u32[]{:S(2)}) %collective-permute-start.4) | collective-permute-done | bytes 397344 | tf_op jit(solution)/shard_map/ppermute | solution.py:560
  53.5 1.6 %send_onward.3 = (bf16[1536,128]{1,0:T(8,128)(2,1)}, bf16[1536,128]{1,0:T(8,128)(2,1)}) custom-call(s32[1]{0:T(128)} %bitcast.5.away_ref, bf16[1552,128]{1,0:T(8,128)(2,1)S(1)} %get-tuple-element.72.q0_ref, bf16[1552,128]{1,0:T(8,128)(2,1)S(1)} %get-tuple-element.73.q1_ref, bf16[1552,128]{1,0:T(8,128)(2,1)S(1)} %collective-permute-done.3.right_ref.right_code, ...), custom_call_target="tpu_custom_call" | custom-call | bytes 2383872 | tf_op jit(solution)/shard_map/send_onward/pallas_call | solution.py:303
  55.1 2.7 %collective-permute-start.7 = (bf16[1536,128]{1,0:T(8,128)(2,1)}, bf16[1536,128]{1,0:T(8,128)(2,1)}, u32[]{:S(2)}, u32[]{:S(2)}) collective-permute-start(bf16[1536,128]{1,0:T(8,128)(2,1)} %get-tuple-element.91), channel_id=1, source_target_pairs={{0,24},{8,0},{16,8},{24,16},{1,25},{9,1},{17,9},{25,17},{2,26},{10... | collective-permute-start | bytes 1179656 | tf_op jit(solution)/shard_map/ppermute | solution.py:567
  57.8 3.8 %collective-permute-start.9 = (bf16[1296,128]{1,0:T(8,128)(2,1)}, bf16[1296,128]{1,0:T(8,128)(2,1)S(1)}, u32[]{:S(2)}, u32[]{:S(2)}) collective-permute-start(bf16[1296,128]{1,0:T(8,128)(2,1)} %get-tuple-element.85.q1_ref), channel_id=1, source_target_pairs={{0,24},{8,0},{16,8},{24,16},{1,25},{9,1},{17,9},{25,17},{2,26},{10... | collective-permute-start | bytes 995336 | tf_op jit(solution)/shard_map/ppermute | solution.py:560
  61.6 4.7 %phi_part.5 = (bf16[160,2048]{1,0:T(8,128)(2,1)S(1)}, f32[8,160,256]{2,1,0:T(8,128)S(1)}) custom-call(s32[256]{0:T(256)S(1)} %slice.24.which_ref, bf16[80,2048]{1,0:T(8,128)(2,1)} %get-tuple-element.99.refs_0_, bf16[80,2048]{1,0:T(8,128)(2,1)} %get-tuple-element.98.refs_1_, bf16[257,128,128]{2,1,0:T(8,128)(2,1)S(1)} %get-tuple-element.78.refs_2_.hk_ref), custom_call_target="tpu_custom_call" | custom-call | flops 335544320 | bytes 655360 | tf_op jit(solution)/shard_map/phi_part/pallas_call | solution.py:178
  66.4 5.1 %action_part.5 = (bf16[160,2048]{1,0:T(8,128)(2,1)S(1)}, bf16[1296,128]{1,0:T(8,128)(2,1)}, bf16[1296,128]{1,0:T(8,128)(2,1)}) custom-call(s32[259]{0:T(512)S(1)} %pad_add_fusion.which_ref, bf16[160,2048]{1,0:T(8,128)(2,1)S(1)} %get-tuple-element.96.refs_0_.rows_ref, f32[8,160,256]{2,1,0:T(8,128)S(1)} %get-tuple-element.97.refs_1_, ...), custom_call_target="tpu_custom_call" | custom-call | flops 335544320 | bytes 655360 | tf_op jit(solution)/shard_map/action_part/pallas_call | solution.py:269
  71.4 0.9 copy-done.16
  72.3 3.8 %collective-permute-start.14 = (bf16[1296,128]{1,0:T(8,128)(2,1)}, bf16[1296,128]{1,0:T(8,128)(2,1)S(1)}, u32[]{:S(2)}, u32[]{:S(2)}) collective-permute-start(bf16[1296,128]{1,0:T(8,128)(2,1)} %get-tuple-element.102.q1_ref), channel_id=1, source_target_pairs={{0,24},{8,0},{16,8},{24,16},{1,25},{9,1},{17,9},{25,17},{2,26},{10... | collective-permute-start | bytes 995336 | tf_op jit(solution)/shard_map/ppermute | solution.py:560
  76.2 0.1 slice.22.which_ref
  76.3 11.4 %collective-permute-done.9.left_ref.left_code = bf16[1296,128]{1,0:T(8,128)(2,1)S(1)} collective-permute-done((bf16[1296,128]{1,0:T(8,128)(2,1)}, bf16[1296,128]{1,0:T(8,128)(2,1)S(1)}, u32[]{:S(2)}, u32[]{:S(2)}) %collective-permute-start.9) | collective-permute-done | bytes 331808 | tf_op jit(solution)/shard_map/ppermute | solution.py:560
  87.7 2.0 %send_onward.4 = (bf16[1280,128]{1,0:T(8,128)(2,1)S(1)}, bf16[1280,128]{1,0:T(8,128)(2,1)S(1)}) custom-call(s32[1]{0:T(128)} %bitcast.5.away_ref, bf16[1296,128]{1,0:T(8,128)(2,1)S(1)} %get-tuple-element.84.q0_ref, bf16[1296,128]{1,0:T(8,128)(2,1)} %get-tuple-element.85.q1_ref, bf16[1296,128]{1,0:T(8,128)(2,1)S(1)} %collective-permute-done.8.right_ref.right_code, ...), custom_call_target="tpu_custom_call" | custom-call | bytes 1990656 | tf_op jit(solution)/shard_map/send_onward/pallas_call | solution.py:303
  89.8 2.0 %collective-permute-start.17 = (bf16[1280,128]{1,0:T(8,128)(2,1)S(1)}, bf16[1280,128]{1,0:T(8,128)(2,1)S(1)}, u32[]{:S(2)}, u32[]{:S(2)}) collective-permute-start(bf16[1280,128]{1,0:T(8,128)(2,1)S(1)} %get-tuple-element.106), channel_id=1, source_target_pairs={{0,8},{8,16},{16,24},{24,0},{1,9},{9,17},{17,25},{25,1},{2,10},{10... | collective-permute-start | bytes 983048 | tf_op jit(solution)/shard_map/ppermute | solution.py:566
  91.8 3.4 %copy-done.1 = bf16[257,128,128]{2,1,0:T(8,128)(2,1)S(1)} copy-done((bf16[257,128,128]{2,1,0:T(8,128)(2,1)S(1)}, bf16[257,128,128]{2,1,0:T(8,128)(2,1)}, u32[]{:S(2)}) %copy-start.1) | copy-done | bytes 8421400
  95.2 3.4 %copy-done.4 = bf16[257,128,128]{2,1,0:T(8,128)(2,1)S(1)} copy-done((bf16[257,128,128]{2,1,0:T(8,128)(2,1)S(1)}, bf16[257,128,128]{2,1,0:T(8,128)(2,1)}, u32[]{:S(2)}) %copy-start.4) | copy-done | bytes 8421400
  98.6 5.1 %local_columns.4.refs_2_.refs_3_ = bf16[2560,128]{1,0:T(8,128)(2,1)S(1)} custom-call(s32[256]{0:T(256)S(1)} %slice.22.which_ref, bf16[160,2048]{1,0:T(8,128)(2,1)S(1)} %copy-done.15, bf16[160,2048]{1,0:T(8,128)(2,1)S(1)} %copy-done.9, bf16[257,128,128]{2,1,0:T(8,128)(2,1)S(1)} %copy-done.1, bf16[257,128,128]{2,1,0:T(8,128)(2,1)S(1)} %copy-done.4, ...), custom_call_target="tpu_custom_call" | custom-call | flops 671088640 | bytes 655360 | tf_op jit(solution)/shard_map/local_columns/pallas_call | solution.py:350
  103.8 2.4 %send_onward.5 = (bf16[1280,128]{1,0:T(8,128)(2,1)S(1)}, bf16[1280,128]{1,0:T(8,128)(2,1)S(1)}) custom-call(s32[1]{0:T(128)} %bitcast.5.away_ref, bf16[1296,128]{1,0:T(8,128)(2,1)} %get-tuple-element.101.q0_ref, bf16[1296,128]{1,0:T(8,128)(2,1)} %get-tuple-element.102.q1_ref, bf16[1296,128]{1,0:T(8,128)(2,1)S(1)} %collective-permute-done.13.right_ref.right_code, ...), custom_call_target="tpu_custom_call" | custom-call | bytes 1990656 | tf_op jit(solution)/shard_map/send_onward/pallas_call | solution.py:303
  106.2 0.6 collective-permute-start.18
  106.8 3.8 %collective-permute-start.16 = (bf16[1280,128]{1,0:T(8,128)(2,1)S(1)}, bf16[1280,128]{1,0:T(8,128)(2,1)S(1)}, u32[]{:S(2)}, u32[]{:S(2)}) collective-permute-start(bf16[1280,128]{1,0:T(8,128)(2,1)S(1)} %get-tuple-element.111), channel_id=1, source_target_pairs={{0,24},{8,0},{16,8},{24,16},{1,25},{9,1},{17,9},{25,17},{2,26},{10... | collective-permute-start | bytes 983048 | tf_op jit(solution)/shard_map/ppermute | solution.py:567
  110.7 5.8 %local_columns.3.refs_0_.refs_1_ = bf16[3072,128]{1,0:T(8,128)(2,1)S(1)} custom-call(s32[256]{0:T(256)S(1)} %slice.22.which_ref, bf16[192,2048]{1,0:T(8,128)(2,1)S(1)} %copy-done.13, bf16[192,2048]{1,0:T(8,128)(2,1)S(1)} %get-tuple-element.67.refs_0_.rows_ref, bf16[257,128,128]{2,1,0:T(8,128)(2,1)S(1)} %copy-done.2, bf16[257,128,128]{2,1,0:T(8,128)(2,1)S(1)} %copy-done.4, ...), custom_call_target="tpu_custom_call" | custom-call | flops 805306368 | bytes 786432 | tf_op jit(solution)/shard_map/local_columns/pallas_call | solution.py:350
  116.4 0.9 copy-done.5
  117.4 5.1 %local_columns.5.refs_4_.refs_5_ = bf16[2560,128]{1,0:T(8,128)(2,1)S(1)} custom-call(s32[256]{0:T(256)S(1)} %slice.22.which_ref, bf16[160,2048]{1,0:T(8,128)(2,1)S(1)} %copy-done.17, bf16[160,2048]{1,0:T(8,128)(2,1)S(1)} %copy-done.11, bf16[257,128,128]{2,1,0:T(8,128)(2,1)S(1)} %copy-done.2, bf16[257,128,128]{2,1,0:T(8,128)(2,1)S(1)} %copy-done.4, ...), custom_call_target="tpu_custom_call" | custom-call | flops 671088640 | bytes 655360 | tf_op jit(solution)/shard_map/local_columns/pallas_call | solution.py:350
  122.5 0.8 copy-done.7
  123.4 0.7 copy-done.21
  124.1 3.5 %finish.2.refs_7_ = bf16[8192,128]{1,0:T(8,128)(2,1)} custom-call(bf16[512,512]{1,0:T(8,128)(2,1)} %constant.66.clone.mix_ref.refs_0_, bf16[3072,128]{1,0:T(8,128)(2,1)} %copy-done.5, bf16[1536,128]{1,0:T(8,128)(2,1)} %collective-permute-done.15.refs_1_, bf16[2560,128]{1,0:T(8,128)(2,1)} %copy-done.6, bf16[1280,128]{1,0:T(8,128)(2,1)} %copy-done.20, ...), custom_call_target="tpu_custom_call" | custom-call | tf_op jit(solution)/shard_map/finish/pallas_call | solution.py:433
  127.6 0.6 collective-permute-done.16.refs_6_
  128.1 0.7 copy-done.23
  128.8 3.4 %finish.3 = bf16[8192,128]{1,0:T(8,128)(2,1)} custom-call(bf16[512,512]{1,0:T(8,128)(2,1)} %constant.66.clone.mix_ref.refs_0_, bf16[3072,128]{1,0:T(8,128)(2,1)} %copy-done.5, bf16[1536,128]{1,0:T(8,128)(2,1)} %collective-permute-done.7.refs_2_, bf16[2560,128]{1,0:T(8,128)(2,1)} %copy-done.6, ...), custom_call_target="tpu_custom_call", output_to_operand_aliasing={{}: (7, {})} | custom-call | tf_op jit(solution)/shard_map/finish/pallas_call | solution.py:433
  (71 shorter events, 0.4 us)
Async XLA Ops:
  0.0 11.0 %copy-start.25 = (s32[32]{0:T(128)S(1)}, s32[32]{0:T(128)}, u32[]{:S(2)}) copy-start(s32[32]{0:T(128)} %param.17) | copy-start | bytes 388
  0.0 13.8 %copy-start.24 = (s32[16,16]{1,0:T(8,128)S(1)}, s32[16,16]{1,0:T(8,128)}, u32[]{:S(2)}) copy-start(s32[16,16]{1,0:T(8,128)} %param.16) | copy-start | bytes 3076
  4.8 22.7 %collective-permute-start = (bf16[96,2048]{1,0:T(8,128)(2,1)S(1)}, bf16[96,2048]{1,0:T(8,128)(2,1)S(1)}, u32[]{:S(2)}, u32[]{:S(2)}) collective-permute-start(bf16[96,2048]{1,0:T(8,128)(2,1)S(1)} %get-tuple-element.66.refs_1_), channel_id=1, source_target_pairs={{0,2},{2,4},{4,6},{1,3},{3,5},{5,7},{8,10},{10,12},{12,14},{9,11},... | collective-permute-start | bytes 1179656 | tf_op jit(solution)/shard_map/ppermute | solution.py:485
  9.7 19.8 %collective-permute-start.1 = (bf16[96,2048]{1,0:T(8,128)(2,1)S(1)}, bf16[96,2048]{1,0:T(8,128)(2,1)S(1)}, u32[]{:S(2)}, u32[]{:S(2)}) collective-permute-start(bf16[96,2048]{1,0:T(8,128)(2,1)S(1)} %get-tuple-element.65.refs_0_), channel_id=1, source_target_pairs={{2,0},{4,2},{6,4},{3,1},{5,3},{7,5},{10,8},{12,10},{14,12},{11,9},... | collective-permute-start | bytes 1179656 | tf_op jit(solution)/shard_map/ppermute | solution.py:485
  14.3 30.5 %collective-permute-start.5 = (bf16[80,2048]{1,0:T(8,128)(2,1)S(1)}, bf16[80,2048]{1,0:T(8,128)(2,1)S(1)}, u32[]{:S(2)}, u32[]{:S(2)}) collective-permute-start(bf16[80,2048]{1,0:T(8,128)(2,1)S(1)} %get-tuple-element.81.refs_1_), channel_id=1, source_target_pairs={{0,2},{2,4},{4,6},{1,3},{3,5},{5,7},{8,10},{10,12},{12,14},{9,11},... | collective-permute-start | bytes 983048 | tf_op jit(solution)/shard_map/ppermute | solution.py:485
  18.9 27.3 %collective-permute-start.6 = (bf16[80,2048]{1,0:T(8,128)(2,1)S(1)}, bf16[80,2048]{1,0:T(8,128)(2,1)S(1)}, u32[]{:S(2)}, u32[]{:S(2)}) collective-permute-start(bf16[80,2048]{1,0:T(8,128)(2,1)S(1)} %get-tuple-element.82.refs_0_), channel_id=1, source_target_pairs={{2,0},{4,2},{6,4},{3,1},{5,3},{7,5},{10,8},{12,10},{14,12},{11,9},... | collective-permute-start | bytes 983048 | tf_op jit(solution)/shard_map/ppermute | solution.py:485
  20.2 7.4 %collective-permute-start.2 = (bf16[4,2048]{1,0:T(4,128)(2,1)S(1)}, bf16[4,2048]{1,0:T(4,128)(2,1)S(1)}, u32[]{:S(2)}, u32[]{:S(2)}) collective-permute-start(bf16[4,2048]{1,0:T(4,128)(2,1)S(1)} %get-tuple-element.62), channel_id=1, source_target_pairs={{0,1},{1,0},{2,3},{3,2},{4,5},{5,4},{6,7},{7,6},{8,9},{9,8},{10,11... | collective-permute-start | bytes 49160 | tf_op jit(solution)/shard_map/ppermute | solution.py:467
  20.3 9.3 %copy-start.19 = (bf16[192,384]{1,0:T(8,128)(2,1)S(1)}, bf16[192,384]{1,0:T(8,128)(2,1)}, u32[]{:S(2)}) copy-start(bf16[192,384]{1,0:T(8,128)(2,1)} %constant.67.clone.refs_7_) | copy-start | bytes 442372
  27.5 34.1 %copy-start.3 = (bf16[257,128,128]{2,1,0:T(8,128)(2,1)}, bf16[257,128,128]{2,1,0:T(8,128)(2,1)S(1)}, u32[]{:S(2)}) copy-start(bf16[257,128,128]{2,1,0:T(8,128)(2,1)S(1)} %get-tuple-element.78.refs_2_.hk_ref) | copy-start | bytes 25264132
  27.6 38.8 %copy-start = (bf16[257,128,128]{2,1,0:T(8,128)(2,1)}, bf16[257,128,128]{2,1,0:T(8,128)(2,1)S(1)}, u32[]{:S(2)}) copy-start(bf16[257,128,128]{2,1,0:T(8,128)(2,1)S(1)} %get-tuple-element.71.refs_8_.kern_ref) | copy-start | bytes 25264132
  34.0 10.8 %copy-start.12 = (bf16[192,2048]{1,0:T(8,128)(2,1)}, bf16[192,2048]{1,0:T(8,128)(2,1)S(1)}, u32[]{:S(2)}) copy-start(bf16[192,2048]{1,0:T(8,128)(2,1)S(1)} %get-tuple-element.90.act_ref) | copy-start | bytes 2359300
  34.0 17.1 %collective-permute-start.3 = (bf16[1552,128]{1,0:T(8,128)(2,1)S(1)}, bf16[1552,128]{1,0:T(8,128)(2,1)S(1)}, u32[]{:S(2)}, u32[]{:S(2)}) collective-permute-start(bf16[1552,128]{1,0:T(8,128)(2,1)S(1)} %get-tuple-element.72.q0_ref), channel_id=1, source_target_pairs={{0,8},{8,16},{16,24},{24,0},{1,9},{9,17},{17,25},{25,1},{2,10},{10... | collective-permute-start | bytes 1191944 | tf_op jit(solution)/shard_map/ppermute | solution.py:559
  35.7 17.9 %collective-permute-start.4 = (bf16[1552,128]{1,0:T(8,128)(2,1)S(1)}, bf16[1552,128]{1,0:T(8,128)(2,1)S(1)}, u32[]{:S(2)}, u32[]{:S(2)}) collective-permute-start(bf16[1552,128]{1,0:T(8,128)(2,1)S(1)} %get-tuple-element.73.q1_ref), channel_id=1, source_target_pairs={{0,24},{8,0},{16,8},{24,16},{1,25},{9,1},{17,9},{25,17},{2,26},{10... | collective-permute-start | bytes 1191944 | tf_op jit(solution)/shard_map/ppermute | solution.py:560
  37.9 19.9 %collective-permute-start.10 = (bf16[80,2048]{1,0:T(8,128)(2,1)}, bf16[80,2048]{1,0:T(8,128)(2,1)S(1)}, u32[]{:S(2)}, u32[]{:S(2)}) collective-permute-start(bf16[80,2048]{1,0:T(8,128)(2,1)} %get-tuple-element.98.refs_1_), channel_id=1, source_target_pairs={{0,2},{2,4},{4,6},{1,3},{3,5},{5,7},{8,10},{10,12},{12,14},{9,11},... | collective-permute-start | bytes 983048 | tf_op jit(solution)/shard_map/ppermute | solution.py:485
  41.3 4.8 %copy-start.18 = (bf16[160,320]{1,0:T(8,128)(2,1)S(1)}, bf16[160,320]{1,0:T(8,128)(2,1)}, u32[]{:S(2)}) copy-start(bf16[160,320]{1,0:T(8,128)(2,1)} %constant.68.clone.refs_7_) | copy-start | bytes 307204
  44.8 6.3 %copy-start.8 = (bf16[160,2048]{1,0:T(8,128)(2,1)}, bf16[160,2048]{1,0:T(8,128)(2,1)S(1)}, u32[]{:S(2)}) copy-start(bf16[160,2048]{1,0:T(8,128)(2,1)S(1)} %get-tuple-element.79.refs_0_.rows_ref) | copy-start | bytes 1966084
  44.9 21.5 %collective-permute-start.11 = (bf16[80,2048]{1,0:T(8,128)(2,1)}, bf16[80,2048]{1,0:T(8,128)(2,1)S(1)}, u32[]{:S(2)}, u32[]{:S(2)}) collective-permute-start(bf16[80,2048]{1,0:T(8,128)(2,1)} %get-tuple-element.99.refs_0_), channel_id=1, source_target_pairs={{2,0},{4,2},{6,4},{3,1},{5,3},{7,5},{10,8},{12,10},{14,12},{11,9},... | collective-permute-start | bytes 983048 | tf_op jit(solution)/shard_map/ppermute | solution.py:485
  51.1 15.2 %copy-start.14 = (bf16[160,2048]{1,0:T(8,128)(2,1)}, bf16[160,2048]{1,0:T(8,128)(2,1)S(1)}, u32[]{:S(2)}) copy-start(bf16[160,2048]{1,0:T(8,128)(2,1)S(1)} %get-tuple-element.108.act_ref) | copy-start | bytes 1966084
  51.1 21.2 %collective-permute-start.8 = (bf16[1296,128]{1,0:T(8,128)(2,1)S(1)}, bf16[1296,128]{1,0:T(8,128)(2,1)S(1)}, u32[]{:S(2)}, u32[]{:S(2)}) collective-permute-start(bf16[1296,128]{1,0:T(8,128)(2,1)S(1)} %get-tuple-element.84.q0_ref), channel_id=1, source_target_pairs={{0,8},{8,16},{16,24},{24,0},{1,9},{9,17},{17,25},{25,1},{2,10},{10... | collective-permute-start | bytes 995336 | tf_op jit(solution)/shard_map/ppermute | solution.py:559
  55.1 34.7 %collective-permute-start.7 = (bf16[1536,128]{1,0:T(8,128)(2,1)}, bf16[1536,128]{1,0:T(8,128)(2,1)}, u32[]{:S(2)}, u32[]{:S(2)}) collective-permute-start(bf16[1536,128]{1,0:T(8,128)(2,1)} %get-tuple-element.91), channel_id=1, source_target_pairs={{0,24},{8,0},{16,8},{24,16},{1,25},{9,1},{17,9},{25,17},{2,26},{10... | collective-permute-start | bytes 1179656 | tf_op jit(solution)/shard_map/ppermute | solution.py:567
  57.8 34.0 %collective-permute-start.15 = (bf16[1536,128]{1,0:T(8,128)(2,1)}, bf16[1536,128]{1,0:T(8,128)(2,1)}, u32[]{:S(2)}, u32[]{:S(2)}) collective-permute-start(bf16[1536,128]{1,0:T(8,128)(2,1)} %get-tuple-element.88), channel_id=1, source_target_pairs={{0,8},{8,16},{16,24},{24,0},{1,9},{9,17},{17,25},{25,1},{2,10},{10... | collective-permute-start | bytes 1179656 | tf_op jit(solution)/shard_map/ppermute | solution.py:566
  57.8 29.9 %collective-permute-start.9 = (bf16[1296,128]{1,0:T(8,128)(2,1)}, bf16[1296,128]{1,0:T(8,128)(2,1)S(1)}, u32[]{:S(2)}, u32[]{:S(2)}) collective-permute-start(bf16[1296,128]{1,0:T(8,128)(2,1)} %get-tuple-element.85.q1_ref), channel_id=1, source_target_pairs={{0,24},{8,0},{16,8},{24,16},{1,25},{9,1},{17,9},{25,17},{2,26},{10... | collective-permute-start | bytes 995336 | tf_op jit(solution)/shard_map/ppermute | solution.py:560
  66.3 5.1 %copy-start.10 = (bf16[160,2048]{1,0:T(8,128)(2,1)}, bf16[160,2048]{1,0:T(8,128)(2,1)S(1)}, u32[]{:S(2)}) copy-start(bf16[160,2048]{1,0:T(8,128)(2,1)S(1)} %get-tuple-element.96.refs_0_.rows_ref) | copy-start | bytes 1966084
  71.4 0.9 copy-start.16
  72.3 31.5 %collective-permute-start.13 = (bf16[1296,128]{1,0:T(8,128)(2,1)}, bf16[1296,128]{1,0:T(8,128)(2,1)S(1)}, u32[]{:S(2)}, u32[]{:S(2)}) collective-permute-start(bf16[1296,128]{1,0:T(8,128)(2,1)} %get-tuple-element.101.q0_ref), channel_id=1, source_target_pairs={{0,8},{8,16},{16,24},{24,0},{1,9},{9,17},{17,25},{25,1},{2,10},{10... | collective-permute-start | bytes 995336 | tf_op jit(solution)/shard_map/ppermute | solution.py:559
  72.3 31.5 %collective-permute-start.14 = (bf16[1296,128]{1,0:T(8,128)(2,1)}, bf16[1296,128]{1,0:T(8,128)(2,1)S(1)}, u32[]{:S(2)}, u32[]{:S(2)}) collective-permute-start(bf16[1296,128]{1,0:T(8,128)(2,1)} %get-tuple-element.102.q1_ref), channel_id=1, source_target_pairs={{0,24},{8,0},{16,8},{24,16},{1,25},{9,1},{17,9},{25,17},{2,26},{10... | collective-permute-start | bytes 995336 | tf_op jit(solution)/shard_map/ppermute | solution.py:560
  76.3 15.6 %copy-start.9 = (bf16[160,2048]{1,0:T(8,128)(2,1)S(1)}, bf16[160,2048]{1,0:T(8,128)(2,1)}, u32[]{:S(2)}) copy-start(bf16[160,2048]{1,0:T(8,128)(2,1)} %copy-done.8) | copy-start | bytes 1966084
  76.3 15.6 %copy-start.15 = (bf16[160,2048]{1,0:T(8,128)(2,1)S(1)}, bf16[160,2048]{1,0:T(8,128)(2,1)}, u32[]{:S(2)}) copy-start(bf16[160,2048]{1,0:T(8,128)(2,1)} %copy-done.14) | copy-start | bytes 1966084
  89.7 27.6 %collective-permute-start.12 = (bf16[1280,128]{1,0:T(8,128)(2,1)S(1)}, bf16[1280,128]{1,0:T(8,128)(2,1)S(1)}, u32[]{:S(2)}, u32[]{:S(2)}) collective-permute-start(bf16[1280,128]{1,0:T(8,128)(2,1)S(1)} %get-tuple-element.105), channel_id=1, source_target_pairs={{0,24},{8,0},{16,8},{24,16},{1,25},{9,1},{17,9},{25,17},{2,26},{10... | collective-permute-start | bytes 983048 | tf_op jit(solution)/shard_map/ppermute | solution.py:567
  89.8 27.5 %collective-permute-start.17 = (bf16[1280,128]{1,0:T(8,128)(2,1)S(1)}, bf16[1280,128]{1,0:T(8,128)(2,1)S(1)}, u32[]{:S(2)}, u32[]{:S(2)}) collective-permute-start(bf16[1280,128]{1,0:T(8,128)(2,1)S(1)} %get-tuple-element.106), channel_id=1, source_target_pairs={{0,8},{8,16},{16,24},{24,0},{1,9},{9,17},{17,25},{25,1},{2,10},{10... | collective-permute-start | bytes 983048 | tf_op jit(solution)/shard_map/ppermute | solution.py:566
  91.8 3.4 %copy-start.1 = (bf16[257,128,128]{2,1,0:T(8,128)(2,1)S(1)}, bf16[257,128,128]{2,1,0:T(8,128)(2,1)}, u32[]{:S(2)}) copy-start(bf16[257,128,128]{2,1,0:T(8,128)(2,1)} %copy-done) | copy-start | bytes 25264132
  95.2 3.4 %copy-start.4 = (bf16[257,128,128]{2,1,0:T(8,128)(2,1)S(1)}, bf16[257,128,128]{2,1,0:T(8,128)(2,1)}, u32[]{:S(2)}) copy-start(bf16[257,128,128]{2,1,0:T(8,128)(2,1)} %copy-done.3) | copy-start | bytes 25264132
  98.6 12.0 %copy-start.2 = (bf16[257,128,128]{2,1,0:T(8,128)(2,1)S(1)}, bf16[257,128,128]{2,1,0:T(8,128)(2,1)}, u32[]{:S(2)}) copy-start(bf16[257,128,128]{2,1,0:T(8,128)(2,1)} %copy-done) | copy-start | bytes 25264132
  103.8 12.7 %copy-start.6 = (bf16[2560,128]{1,0:T(8,128)(2,1)}, bf16[2560,128]{1,0:T(8,128)(2,1)S(1)}, u32[]{:S(2)}) copy-start(bf16[2560,128]{1,0:T(8,128)(2,1)S(1)} %local_columns.4.refs_2_.refs_3_) | copy-start | bytes 1966084
  103.8 6.9 %copy-start.13 = (bf16[192,2048]{1,0:T(8,128)(2,1)S(1)}, bf16[192,2048]{1,0:T(8,128)(2,1)}, u32[]{:S(2)}) copy-start(bf16[192,2048]{1,0:T(8,128)(2,1)} %copy-done.12) | copy-start | bytes 2359300
  106.2 17.1 %collective-permute-start.18 = (bf16[1280,128]{1,0:T(8,128)(2,1)S(1)}, bf16[1280,128]{1,0:T(8,128)(2,1)S(1)}, u32[]{:S(2)}, u32[]{:S(2)}) collective-permute-start(bf16[1280,128]{1,0:T(8,128)(2,1)S(1)} %get-tuple-element.112), channel_id=1, source_target_pairs={{0,8},{8,16},{16,24},{24,0},{1,9},{9,17},{17,25},{25,1},{2,10},{10... | collective-permute-start | bytes 983048 | tf_op jit(solution)/shard_map/ppermute | solution.py:566
  106.8 21.3 %collective-permute-start.16 = (bf16[1280,128]{1,0:T(8,128)(2,1)S(1)}, bf16[1280,128]{1,0:T(8,128)(2,1)S(1)}, u32[]{:S(2)}, u32[]{:S(2)}) collective-permute-start(bf16[1280,128]{1,0:T(8,128)(2,1)S(1)} %get-tuple-element.111), channel_id=1, source_target_pairs={{0,24},{8,0},{16,8},{24,16},{1,25},{9,1},{17,9},{25,17},{2,26},{10... | collective-permute-start | bytes 983048 | tf_op jit(solution)/shard_map/ppermute | solution.py:567
  110.6 6.7 %copy-start.11 = (bf16[160,2048]{1,0:T(8,128)(2,1)S(1)}, bf16[160,2048]{1,0:T(8,128)(2,1)}, u32[]{:S(2)}) copy-start(bf16[160,2048]{1,0:T(8,128)(2,1)} %copy-done.10) | copy-start | bytes 1966084
  110.6 6.7 %copy-start.17 = (bf16[160,2048]{1,0:T(8,128)(2,1)S(1)}, bf16[160,2048]{1,0:T(8,128)(2,1)}, u32[]{:S(2)}) copy-start(bf16[160,2048]{1,0:T(8,128)(2,1)} %copy-done.16) | copy-start | bytes 1966084
  116.4 0.9 copy-start.5
  117.3 5.2 %copy-start.22 = (bf16[1280,128]{1,0:T(8,128)(2,1)}, bf16[1280,128]{1,0:T(8,128)(2,1)S(1)}, u32[]{:S(2)}) copy-start(bf16[1280,128]{1,0:T(8,128)(2,1)S(1)} %collective-permute-done.12.refs_4_) | copy-start | bytes 983044
  117.3 5.2 %copy-start.20 = (bf16[1280,128]{1,0:T(8,128)(2,1)}, bf16[1280,128]{1,0:T(8,128)(2,1)S(1)}, u32[]{:S(2)}) copy-start(bf16[1280,128]{1,0:T(8,128)(2,1)S(1)} %collective-permute-done.17.refs_3_) | copy-start | bytes 983044
  122.5 0.8 copy-start.7
  123.4 0.7 copy-start.21
  128.1 0.7 copy-start.23

commit v4 on v3

--- a/solution.py
+++ b/solution.py
@@ -93,7 +93,7 @@
         .reshape(groups * block * tiles * rows_y, LANES)
     )
     parts = tiles * rows_y
-    per_step = 4
+    per_step = 8
     width = per_step * block
     chunks = len(cuts) - 1
     spans = [last - first for first, last in zip(cuts, cuts[1:])]
@@ -110,7 +110,7 @@
         + [pl.BlockSpec((rows_y * span, groups), lambda s: (0, 0)) for span in spans],
         out_shape=[jax.ShapeDtypeStruct((size, groups * block), jnp.bfloat16) for size in sizes]
         + [jax.ShapeDtypeStruct((rows_y * span, groups), jnp.float32) for span in spans],
-        compiler_params=pltpu.CompilerParams(vmem_limit_bytes=SCOPED),
+        compiler_params=pltpu.CompilerParams(vmem_limit_bytes=2 * SCOPED),
         name="prepare",
     )(*in_hbm(flat, regroup_matrix(block, parts), pot))
     fields = [[outs[c * rows_y + y] for y in range(rows_y)] for c in range(chunks)]
@@ -421,7 +421,7 @@
             in_specs.append(
                 pl.BlockSpec((per_step * n, block), functools.partial(lambda at, s: (s + at, 0), first // per_step))
             )
-    arrays = in_hbm(regroup_matrix(block, tiles * rows_y), *arrays)
+    arrays = [*in_hbm(regroup_matrix(block, tiles * rows_y)), *arrays]
     counts = [len(part) for part in parts]
     kernel = functools.partial(final_kernel, per_step, counts, rows_y, tiles)
     aliases = {}
@@ -529,24 +529,26 @@
         return unflatten(flat, groups, block, rows_y, rows_z // LANES)
 
     me = lax.axis_index("gx")
-    owners = req_cols // groups
-    other = jnp.where(owners[0] == me, owners[listed - 1], owners[0])
-    away = (other - me) % ring
+    toward = (req_cols // groups - me) % ring
+    away = jnp.max(toward)
     ahead = [(i, (i + 1) % ring) for i in range(ring)]
     behind = [(i, (i - 1) % ring) for i in range(ring)]
 
     half = groups // 2
-    column = jnp.arange(groups, dtype=jnp.int32)
-    swapped = jnp.where(away == ACROSS, column, (column + half) % groups)
-    wanted = jnp.concatenate([other * groups + swapped, me * groups + column])
+    column = req_cols % groups
+    first = jnp.where(toward == ACROSS, column, (column + half) % groups)
+    order = jnp.where(toward == 0, groups + column, first)
     slots = jnp.sum(
-        jnp.where(wanted[:, None] == req_cols[None, :], jnp.arange(listed, dtype=jnp.int32), 0), axis=1
+        jnp.where(
+            jnp.arange(2 * groups, dtype=jnp.int32)[:, None] == order[None, :], jnp.arange(listed, dtype=jnp.int32), 0
+        ),
+        axis=1,
     )
     which = block_of_column(slot_of, slots).reshape(-1)
     far, near = which[: groups * groups], which[groups * groups :]
     table = jnp.concatenate([far, jnp.stack([*marks, away]).astype(jnp.int32)])
     away = away.reshape(1)
-    send_halo(1, table)
+    send_halo(1, far)
 
     rows, acts, sent, own, right1, left1, right2, left2 = [], [], [], [], [], [], [], []
 

time: 135 us -> 132 us (0.978)
  local copies, waits for them, and re-layouts: 11.9 us -> 9.05 us
  between operations: 2.39 us -> 0.43 us
    unnamed x52 -> x42, local copies, waits for them, and re-layouts: 10.9 us -> 8.67 us
    pallas_call x3, Pallas kernels: 5.99 us -> 7.52 us  [send_onward(): pl.pallas_call(onward_kernel, grid_spec=pltpu.PrefetchScalarGridSpec(num_...]
  transfers between devices with their start and end apart: 19 -> 19, of which waited for: 4 -> 3; matrix products, arithmetic and copies ran while one was open for 1% -> 2% of each run, Pallas kernels for 42% -> 44%
where the time goes in v4:
time: 132 us; the launch traced here: 130 us
  Pallas kernels  64.5 us (49%)
  starting transfers between devices  38.2 us (29%)
  waiting for transfers between devices  16.6 us (13%)
  local copies, waits for them, and re-layouts  9.05 us (7%)
  other arithmetic  1.58 us (1%)
    pallas_call x3, Pallas kernels, local_columns(): pl.pallas_call(functools.partial(local_kernel, groups), grid_spec=pltpu.P...  16.1 us
    pallas_call x3, Pallas kernels, action_part(): pl.pallas_call(functools.partial(action_kernel, groups, rows_y, cols, low...  15.6 us
    pallas_call x3, Pallas kernels, phi_part(): pl.pallas_call(functools.partial(phi_kernel, groups, len(fields), loads),...  15.3 us
    ppermute x3, waiting for transfers between devices, send_first(): left1.append(lax.ppermute(q1, 'gx', behind))  13.8 us
    ppermute x3, starting transfers between devices, send_halo(): lax.ppermute(up, 'gy', shifts('gy', 1))  13.5 us
    ppermute x3, starting transfers between devices, send_first(): left1.append(lax.ppermute(q1, 'gx', behind))  9.92 us
    unnamed x42, local copies, waits for them, and re-layouts  8.67 us
    pallas_call x3, Pallas kernels, send_onward(): pl.pallas_call(onward_kernel, grid_spec=pltpu.PrefetchScalarGridSpec(num_...  7.52 us
  transfers between devices with their start and end apart: 19, of which 3 were waited for; matrix products, arithmetic and copies ran while one was open for 2% of the time, Pallas kernels for 44%

profile of v4, /device:TPU:0, one launch (start us, length us, event | category | flops | bytes accessed | tf_op | source)
XLA Modules:
  0.0 130.4 jit_solution(15077175078920698356)
XLA Ops:
  0.0 4.1 %prepare.1 = (bf16[96,2048]{1,0:T(8,128)(2,1)S(1)}, bf16[96,2048]{1,0:T(8,128)(2,1)S(1)}, bf16[80,2048]{1,0:T(8,128)(2,1)S(1)}, bf16[80,2048]{1,0:T(8,128)(2,1)S...) custom-call(bf16[8192,128]{1,0:T(8,128)(2,1)} %bitcast.17, ...), custom_call_target="tpu_custom_call" | custom-call | tf_op jit(solution)/shard_map/prepare/pallas_call | solution.py:101
  4.1 4.9 %collective-permute-start = (bf16[96,2048]{1,0:T(8,128)(2,1)S(1)}, bf16[96,2048]{1,0:T(8,128)(2,1)S(1)}, u32[]{:S(2)}, u32[]{:S(2)}) collective-permute-start(bf16[96,2048]{1,0:T(8,128)(2,1)S(1)} %get-tuple-element.66.refs_1_), channel_id=1, source_target_pairs={{0,2},{2,4},{4,6},{1,3},{3,5},{5,7},{8,10},{10,12},{12,14},{9,11},... | collective-permute-start | bytes 1179656 | tf_op jit(solution)/shard_map/ppermute | solution.py:485
  9.0 1.3 collective-permute-start.1
  10.3 0.1 collective-permute-start.2
  10.4 0.6 fusion.2
  11.1 0.1 select_reduce_fusion.1
  11.2 0.1 select_reduce_fusion
  11.3 0.1 fusion.3
  11.4 0.1 copy.20
  11.5 0.1 slice.15.which_ref
  11.6 5.3 %collective-permute-start.5 = (bf16[80,2048]{1,0:T(8,128)(2,1)S(1)}, bf16[80,2048]{1,0:T(8,128)(2,1)}, u32[]{:S(2)}, u32[]{:S(2)}) collective-permute-start(bf16[80,2048]{1,0:T(8,128)(2,1)S(1)} %get-tuple-element.81.refs_1_), channel_id=1, source_target_pairs={{0,2},{2,4},{4,6},{1,3},{3,5},{5,7},{8,10},{10,12},{12,14},{9,11},... | collective-permute-start | bytes 983048 | tf_op jit(solution)/shard_map/ppermute | solution.py:485
  16.8 1.3 collective-permute-start.6
  18.1 0.6 pad_add_fusion.which_ref
  18.8 7.2 %phi_part.3 = (bf16[192,2048]{1,0:T(8,128)(2,1)S(1)}, f32[8,192,256]{2,1,0:T(8,128)S(1)}, bf16[257,128,128]{2,1,0:T(8,128)(2,1)S(1)}, bf16[257,128,128]{2,1,0:T(8,128)(2,1)S(1)}) custom-call(s32[256]{0:T(256)S(1)} %slice.15.which_ref, bf16[96,2048]{1,0:T(8,128)(2,1)S(1)} %get-tuple-element.65.refs_0_, bf16[96,2048]{1,0:T(8,128)(2,1)S(1)} %get-tuple-element.66.refs_1_, ...), custom_call_target="tpu_custom_call" | custom-call | flops 402653184 | bytes 786432 | tf_op jit(solution)/shard_map/phi_part/pallas_call | solution.py:178
  26.0 2.8 %collective-permute-done.1.refs_3_ = bf16[96,2048]{1,0:T(8,128)(2,1)S(1)} collective-permute-done((bf16[96,2048]{1,0:T(8,128)(2,1)S(1)}, bf16[96,2048]{1,0:T(8,128)(2,1)S(1)}, u32[]{:S(2)}, u32[]{:S(2)}) %collective-permute-start.1) | collective-permute-done | bytes 393248 | tf_op jit(solution)/shard_map/ppermute | solution.py:485
  28.8 4.5 %action_part.3 = (bf16[192,2048]{1,0:T(8,128)(2,1)S(1)}, bf16[1552,128]{1,0:T(8,128)(2,1)S(1)}, bf16[1552,128]{1,0:T(8,128)(2,1)S(1)}) custom-call(s32[259]{0:T(512)S(1)} %pad_add_fusion.which_ref, bf16[192,2048]{1,0:T(8,128)(2,1)S(1)} %get-tuple-element.67.refs_0_.rows_ref, f32[8,192,256]{2,1,0:T(8,128)S(1)} %get-tuple-element.68.refs_1_, ...), custom_call_target="tpu_custom_call" | custom-call | flops 402653184 | bytes 786432 | tf_op jit(solution)/shard_map/action_part/pallas_call | solution.py:269
  33.3 1.6 %collective-permute-start.3 = (bf16[1552,128]{1,0:T(8,128)(2,1)S(1)}, bf16[1552,128]{1,0:T(8,128)(2,1)S(1)}, u32[]{:S(2)}, u32[]{:S(2)}) collective-permute-start(bf16[1552,128]{1,0:T(8,128)(2,1)S(1)} %get-tuple-element.72.q0_ref), channel_id=1, source_target_pairs={{0,8},{8,16},{16,24},{24,0},{1,9},{9,17},{17,25},{25,1},{2,10},{10... | collective-permute-start | bytes 1191944 | tf_op jit(solution)/shard_map/ppermute | solution.py:561
  34.9 2.3 %collective-permute-start.4 = (bf16[1552,128]{1,0:T(8,128)(2,1)S(1)}, bf16[1552,128]{1,0:T(8,128)(2,1)S(1)}, u32[]{:S(2)}, u32[]{:S(2)}) collective-permute-start(bf16[1552,128]{1,0:T(8,128)(2,1)S(1)} %get-tuple-element.73.q1_ref), channel_id=1, source_target_pairs={{0,24},{8,0},{16,8},{24,16},{1,25},{9,1},{17,9},{25,17},{2,26},{10... | collective-permute-start | bytes 1191944 | tf_op jit(solution)/shard_map/ppermute | solution.py:562
  37.2 3.4 %collective-permute-start.10 = (bf16[80,2048]{1,0:T(8,128)(2,1)}, bf16[80,2048]{1,0:T(8,128)(2,1)S(1)}, u32[]{:S(2)}, u32[]{:S(2)}) collective-permute-start(bf16[80,2048]{1,0:T(8,128)(2,1)} %get-tuple-element.98.refs_1_), channel_id=1, source_target_pairs={{0,2},{2,4},{4,6},{1,3},{3,5},{5,7},{8,10},{10,12},{12,14},{9,11},... | collective-permute-start | bytes 983048 | tf_op jit(solution)/shard_map/ppermute | solution.py:485
  40.6 3.5 %phi_part.4 = (bf16[160,2048]{1,0:T(8,128)(2,1)S(1)}, f32[8,160,256]{2,1,0:T(8,128)S(1)}) custom-call(s32[256]{0:T(256)S(1)} %slice.15.which_ref, bf16[80,2048]{1,0:T(8,128)(2,1)S(1)} %get-tuple-element.82.refs_0_, bf16[80,2048]{1,0:T(8,128)(2,1)S(1)} %get-tuple-element.81.refs_1_, bf16[257,128,128]{2,1,0:T(8,128)(2,1)S(1)} %get-tuple-element.78.refs_2_.hk_ref), custom_call_target="tpu_custom_call" | custom-call | flops 335544320 | bytes 655360 | tf_op jit(solution)/shard_map/phi_part/pallas_call | solution.py:178
  44.1 1.3 collective-permute-start.11
  45.4 6.0 %action_part.4 = (bf16[160,2048]{1,0:T(8,128)(2,1)S(1)}, bf16[1296,128]{1,0:T(8,128)(2,1)S(1)}, bf16[1296,128]{1,0:T(8,128)(2,1)}) custom-call(s32[259]{0:T(512)S(1)} %pad_add_fusion.which_ref, bf16[160,2048]{1,0:T(8,128)(2,1)S(1)} %get-tuple-element.79.refs_0_.rows_ref, f32[8,160,256]{2,1,0:T(8,128)S(1)} %get-tuple-element.80.refs_1_, ...), custom_call_target="tpu_custom_call" | custom-call | flops 335544320 | bytes 655360 | tf_op jit(solution)/shard_map/action_part/pallas_call | solution.py:269
  51.5 0.1 collective-permute-start.8
  51.6 0.6 collective-permute-done.4.left_ref.left_code
  52.1 2.1 %send_onward.3 = (bf16[1536,128]{1,0:T(8,128)(2,1)}, bf16[1536,128]{1,0:T(8,128)(2,1)}) custom-call(s32[1]{0:T(128)} %bitcast.3.away_ref, bf16[1552,128]{1,0:T(8,128)(2,1)S(1)} %get-tuple-element.72.q0_ref, bf16[1552,128]{1,0:T(8,128)(2,1)S(1)} %get-tuple-element.73.q1_ref, bf16[1552,128]{1,0:T(8,128)(2,1)S(1)} %collective-permute-done.3.right_ref.right_code, ...), custom_call_target="tpu_custom_call" | custom-call | bytes 2383872 | tf_op jit(solution)/shard_map/send_onward/pallas_call | solution.py:303
  54.2 3.2 %collective-permute-start.7 = (bf16[1536,128]{1,0:T(8,128)(2,1)}, bf16[1536,128]{1,0:T(8,128)(2,1)}, u32[]{:S(2)}, u32[]{:S(2)}) collective-permute-start(bf16[1536,128]{1,0:T(8,128)(2,1)} %get-tuple-element.91), channel_id=1, source_target_pairs={{0,24},{8,0},{16,8},{24,16},{1,25},{9,1},{17,9},{25,17},{2,26},{10... | collective-permute-start | bytes 1179656 | tf_op jit(solution)/shard_map/ppermute | solution.py:569
  57.5 3.8 %collective-permute-start.9 = (bf16[1296,128]{1,0:T(8,128)(2,1)}, bf16[1296,128]{1,0:T(8,128)(2,1)S(1)}, u32[]{:S(2)}, u32[]{:S(2)}) collective-permute-start(bf16[1296,128]{1,0:T(8,128)(2,1)} %get-tuple-element.85.q1_ref), channel_id=1, source_target_pairs={{0,24},{8,0},{16,8},{24,16},{1,25},{9,1},{17,9},{25,17},{2,26},{10... | collective-permute-start | bytes 995336 | tf_op jit(solution)/shard_map/ppermute | solution.py:562
  61.3 4.7 %phi_part.5 = (bf16[160,2048]{1,0:T(8,128)(2,1)S(1)}, f32[8,160,256]{2,1,0:T(8,128)S(1)}) custom-call(s32[256]{0:T(256)S(1)} %slice.15.which_ref, bf16[80,2048]{1,0:T(8,128)(2,1)} %get-tuple-element.99.refs_0_, bf16[80,2048]{1,0:T(8,128)(2,1)} %get-tuple-element.98.refs_1_, bf16[257,128,128]{2,1,0:T(8,128)(2,1)S(1)} %get-tuple-element.78.refs_2_.hk_ref), custom_call_target="tpu_custom_call" | custom-call | flops 335544320 | bytes 655360 | tf_op jit(solution)/shard_map/phi_part/pallas_call | solution.py:178
  66.0 5.1 %action_part.5 = (bf16[160,2048]{1,0:T(8,128)(2,1)S(1)}, bf16[1296,128]{1,0:T(8,128)(2,1)}, bf16[1296,128]{1,0:T(8,128)(2,1)}) custom-call(s32[259]{0:T(512)S(1)} %pad_add_fusion.which_ref, bf16[160,2048]{1,0:T(8,128)(2,1)S(1)} %get-tuple-element.96.refs_0_.rows_ref, f32[8,160,256]{2,1,0:T(8,128)S(1)} %get-tuple-element.97.refs_1_, ...), custom_call_target="tpu_custom_call" | custom-call | flops 335544320 | bytes 655360 | tf_op jit(solution)/shard_map/action_part/pallas_call | solution.py:269
  71.1 0.9 copy-done.13
  72.0 3.8 %collective-permute-start.14 = (bf16[1296,128]{1,0:T(8,128)(2,1)}, bf16[1296,128]{1,0:T(8,128)(2,1)S(1)}, u32[]{:S(2)}, u32[]{:S(2)}) collective-permute-start(bf16[1296,128]{1,0:T(8,128)(2,1)} %get-tuple-element.102.q1_ref), channel_id=1, source_target_pairs={{0,24},{8,0},{16,8},{24,16},{1,25},{9,1},{17,9},{25,17},{2,26},{10... | collective-permute-start | bytes 995336 | tf_op jit(solution)/shard_map/ppermute | solution.py:562
  75.8 0.1 copy.19
  75.9 0.1 slice.13.which_ref
  75.9 13.2 %collective-permute-done.9.left_ref.left_code = bf16[1296,128]{1,0:T(8,128)(2,1)S(1)} collective-permute-done((bf16[1296,128]{1,0:T(8,128)(2,1)}, bf16[1296,128]{1,0:T(8,128)(2,1)S(1)}, u32[]{:S(2)}, u32[]{:S(2)}) %collective-permute-start.9) | collective-permute-done | bytes 331808 | tf_op jit(solution)/shard_map/ppermute | solution.py:562
  89.2 1.0 copy-done.17
  90.1 2.6 %send_onward.4 = (bf16[1280,128]{1,0:T(8,128)(2,1)S(1)}, bf16[1280,128]{1,0:T(8,128)(2,1)S(1)}) custom-call(s32[1]{0:T(128)} %bitcast.3.away_ref, bf16[1296,128]{1,0:T(8,128)(2,1)S(1)} %copy-done.17, bf16[1296,128]{1,0:T(8,128)(2,1)} %get-tuple-element.85.q1_ref, bf16[1296,128]{1,0:T(8,128)(2,1)S(1)} %collective-permute-done.8.right_ref.right_code, ...), custom_call_target="tpu_custom_call" | custom-call | bytes 1990656 | tf_op jit(solution)/shard_map/send_onward/pallas_call | solution.py:303
  92.8 0.1 collective-permute-start.12
  92.8 2.0 %collective-permute-start.17 = (bf16[1280,128]{1,0:T(8,128)(2,1)S(1)}, bf16[1280,128]{1,0:T(8,128)(2,1)S(1)}, u32[]{:S(2)}, u32[]{:S(2)}) collective-permute-start(bf16[1280,128]{1,0:T(8,128)(2,1)S(1)} %get-tuple-element.106), channel_id=1, source_target_pairs={{0,8},{8,16},{16,24},{24,0},{1,9},{9,17},{17,25},{25,1},{2,10},{10... | collective-permute-start | bytes 983048 | tf_op jit(solution)/shard_map/ppermute | solution.py:568
  94.9 3.4 %copy-done.1 = bf16[257,128,128]{2,1,0:T(8,128)(2,1)S(1)} copy-done((bf16[257,128,128]{2,1,0:T(8,128)(2,1)S(1)}, bf16[257,128,128]{2,1,0:T(8,128)(2,1)}, u32[]{:S(2)}) %copy-start.1) | copy-done | bytes 8421400
  98.2 3.4 %copy-done.4 = bf16[257,128,128]{2,1,0:T(8,128)(2,1)S(1)} copy-done((bf16[257,128,128]{2,1,0:T(8,128)(2,1)S(1)}, bf16[257,128,128]{2,1,0:T(8,128)(2,1)}, u32[]{:S(2)}) %copy-start.4) | copy-done | bytes 8421400
  101.6 5.1 %local_columns.4.refs_2_.refs_3_ = bf16[2560,128]{1,0:T(8,128)(2,1)S(1)} custom-call(s32[256]{0:T(256)S(1)} %slice.13.which_ref, bf16[160,2048]{1,0:T(8,128)(2,1)S(1)} %copy-done.12, bf16[160,2048]{1,0:T(8,128)(2,1)S(1)} %copy-done.6, bf16[257,128,128]{2,1,0:T(8,128)(2,1)S(1)} %copy-done.1, bf16[257,128,128]{2,1,0:T(8,128)(2,1)S(1)} %copy-done.4, ...), custom_call_target="tpu_custom_call" | custom-call | flops 671088640 | bytes 655360 | tf_op jit(solution)/shard_map/local_columns/pallas_call | solution.py:350
  106.8 2.8 %send_onward.5 = (bf16[1280,128]{1,0:T(8,128)(2,1)S(1)}, bf16[1280,128]{1,0:T(8,128)(2,1)S(1)}) custom-call(s32[1]{0:T(128)} %bitcast.3.away_ref, bf16[1296,128]{1,0:T(8,128)(2,1)} %get-tuple-element.101.q0_ref, bf16[1296,128]{1,0:T(8,128)(2,1)} %get-tuple-element.102.q1_ref, bf16[1296,128]{1,0:T(8,128)(2,1)S(1)} %collective-permute-done.13.right_ref.right_code, ...), custom_call_target="tpu_custom_call" | custom-call | bytes 1990656 | tf_op jit(solution)/shard_map/send_onward/pallas_call | solution.py:303
  109.6 1.0 collective-permute-start.18
  110.6 2.9 %collective-permute-start.16 = (bf16[1280,128]{1,0:T(8,128)(2,1)S(1)}, bf16[1280,128]{1,0:T(8,128)(2,1)S(1)}, u32[]{:S(2)}, u32[]{:S(2)}) collective-permute-start(bf16[1280,128]{1,0:T(8,128)(2,1)S(1)} %get-tuple-element.111), channel_id=1, source_target_pairs={{0,24},{8,0},{16,8},{24,16},{1,25},{9,1},{17,9},{25,17},{2,26},{10... | collective-permute-start | bytes 983048 | tf_op jit(solution)/shard_map/ppermute | solution.py:569
  113.5 5.8 %local_columns.3.refs_0_.refs_1_ = bf16[3072,128]{1,0:T(8,128)(2,1)S(1)} custom-call(s32[256]{0:T(256)S(1)} %slice.13.which_ref, bf16[192,2048]{1,0:T(8,128)(2,1)S(1)} %copy-done.10, bf16[192,2048]{1,0:T(8,128)(2,1)S(1)} %get-tuple-element.67.refs_0_.rows_ref, bf16[257,128,128]{2,1,0:T(8,128)(2,1)S(1)} %copy-done.2, bf16[257,128,128]{2,1,0:T(8,128)(2,1)S(1)} %copy-done.4, ...), custom_call_target="tpu_custom_call" | custom-call | flops 805306368 | bytes 786432 | tf_op jit(solution)/shard_map/local_columns/pallas_call | solution.py:350
  119.4 5.2 %local_columns.5.refs_4_.refs_5_ = bf16[2560,128]{1,0:T(8,128)(2,1)S(1)} custom-call(s32[256]{0:T(256)S(1)} %slice.13.which_ref, bf16[160,2048]{1,0:T(8,128)(2,1)S(1)} %copy-done.14, bf16[160,2048]{1,0:T(8,128)(2,1)S(1)} %copy-done.8, bf16[257,128,128]{2,1,0:T(8,128)(2,1)S(1)} %copy-done.2, bf16[257,128,128]{2,1,0:T(8,128)(2,1)S(1)} %copy-done.4, ...), custom_call_target="tpu_custom_call" | custom-call | flops 671088640 | bytes 655360 | tf_op jit(solution)/shard_map/local_columns/pallas_call | solution.py:350
  124.6 2.9 %finish.2.refs_7_ = bf16[8192,128]{1,0:T(8,128)(2,1)} custom-call(bf16[512,512]{1,0:T(8,128)(2,1)} %constant.74.clone.mix_ref.refs_0_, bf16[3072,128]{1,0:T(8,128)(2,1)S(1)} %local_columns.3.refs_0_.refs_1_, bf16[1536,128]{1,0:T(8,128)(2,1)S(1)} %collective-permute-done.15.refs_1_, bf16[2560,128]{1,0:T(8,128)(2,1)S(1)} %local_columns.4.refs_2_.refs_3_, ...), custom_call_target="tpu_custom_call" | custom-call | tf_op jit(solution)/shard_map/finish/pallas_call | solution.py:433
  127.4 3.0 %finish.3 = bf16[8192,128]{1,0:T(8,128)(2,1)} custom-call(bf16[512,512]{1,0:T(8,128)(2,1)} %constant.74.clone.mix_ref.refs_0_, bf16[3072,128]{1,0:T(8,128)(2,1)S(1)} %local_columns.3.refs_0_.refs_1_, bf16[1536,128]{1,0:T(8,128)(2,1)} %collective-permute-done.7.refs_2_, ...), custom_call_target="tpu_custom_call", output_to_operand_aliasing={{}: (7, {})} | custom-call | tf_op jit(solution)/shard_map/finish/pallas_call | solution.py:433
  (59 shorter events, 0.2 us)
Async XLA Ops:
  0.0 10.4 %copy-start.20 = (s32[32]{0:T(128)S(1)}, s32[32]{0:T(128)}, u32[]{:S(2)}) copy-start(s32[32]{0:T(128)} %param.17) | copy-start | bytes 388
  0.0 11.2 %copy-start.19 = (s32[16,16]{1,0:T(8,128)S(1)}, s32[16,16]{1,0:T(8,128)}, u32[]{:S(2)}) copy-start(s32[16,16]{1,0:T(8,128)} %param.16) | copy-start | bytes 3076
  4.1 21.9 %collective-permute-start = (bf16[96,2048]{1,0:T(8,128)(2,1)S(1)}, bf16[96,2048]{1,0:T(8,128)(2,1)S(1)}, u32[]{:S(2)}, u32[]{:S(2)}) collective-permute-start(bf16[96,2048]{1,0:T(8,128)(2,1)S(1)} %get-tuple-element.66.refs_1_), channel_id=1, source_target_pairs={{0,2},{2,4},{4,6},{1,3},{3,5},{5,7},{8,10},{10,12},{12,14},{9,11},... | collective-permute-start | bytes 1179656 | tf_op jit(solution)/shard_map/ppermute | solution.py:485
  9.0 19.9 %collective-permute-start.1 = (bf16[96,2048]{1,0:T(8,128)(2,1)S(1)}, bf16[96,2048]{1,0:T(8,128)(2,1)S(1)}, u32[]{:S(2)}, u32[]{:S(2)}) collective-permute-start(bf16[96,2048]{1,0:T(8,128)(2,1)S(1)} %get-tuple-element.65.refs_0_), channel_id=1, source_target_pairs={{2,0},{4,2},{6,4},{3,1},{5,3},{7,5},{10,8},{12,10},{14,12},{11,9},... | collective-permute-start | bytes 1179656 | tf_op jit(solution)/shard_map/ppermute | solution.py:485
  10.3 15.7 %collective-permute-start.2 = (bf16[4,2048]{1,0:T(4,128)(2,1)S(1)}, bf16[4,2048]{1,0:T(4,128)(2,1)S(1)}, u32[]{:S(2)}, u32[]{:S(2)}) collective-permute-start(bf16[4,2048]{1,0:T(4,128)(2,1)S(1)} %get-tuple-element.62), channel_id=1, source_target_pairs={{0,1},{1,0},{2,3},{3,2},{4,5},{5,4},{6,7},{7,6},{8,9},{9,8},{10,11... | collective-permute-start | bytes 49160 | tf_op jit(solution)/shard_map/ppermute | solution.py:467
  11.6 32.5 %collective-permute-start.5 = (bf16[80,2048]{1,0:T(8,128)(2,1)S(1)}, bf16[80,2048]{1,0:T(8,128)(2,1)}, u32[]{:S(2)}, u32[]{:S(2)}) collective-permute-start(bf16[80,2048]{1,0:T(8,128)(2,1)S(1)} %get-tuple-element.81.refs_1_), channel_id=1, source_target_pairs={{0,2},{2,4},{4,6},{1,3},{3,5},{5,7},{8,10},{10,12},{12,14},{9,11},... | collective-permute-start | bytes 983048 | tf_op jit(solution)/shard_map/ppermute | solution.py:485
  16.8 28.6 %collective-permute-start.6 = (bf16[80,2048]{1,0:T(8,128)(2,1)S(1)}, bf16[80,2048]{1,0:T(8,128)(2,1)}, u32[]{:S(2)}, u32[]{:S(2)}) collective-permute-start(bf16[80,2048]{1,0:T(8,128)(2,1)S(1)} %get-tuple-element.82.refs_0_), channel_id=1, source_target_pairs={{2,0},{4,2},{6,4},{3,1},{5,3},{7,5},{10,8},{12,10},{14,12},{11,9},... | collective-permute-start | bytes 983048 | tf_op jit(solution)/shard_map/ppermute | solution.py:485
  18.8 10.0 %copy-start.18 = (bf16[192,384]{1,0:T(8,128)(2,1)S(1)}, bf16[192,384]{1,0:T(8,128)(2,1)}, u32[]{:S(2)}) copy-start(bf16[192,384]{1,0:T(8,128)(2,1)} %constant.75.clone.refs_7_) | copy-start | bytes 442372
  26.0 35.3 %copy-start.3 = (bf16[257,128,128]{2,1,0:T(8,128)(2,1)}, bf16[257,128,128]{2,1,0:T(8,128)(2,1)S(1)}, u32[]{:S(2)}) copy-start(bf16[257,128,128]{2,1,0:T(8,128)(2,1)S(1)} %get-tuple-element.78.refs_2_.hk_ref) | copy-start | bytes 25264132
  26.0 40.0 %copy-start = (bf16[257,128,128]{2,1,0:T(8,128)(2,1)}, bf16[257,128,128]{2,1,0:T(8,128)(2,1)S(1)}, u32[]{:S(2)}) copy-start(bf16[257,128,128]{2,1,0:T(8,128)(2,1)S(1)} %get-tuple-element.71.refs_8_.kern_ref) | copy-start | bytes 25264132
  33.3 10.8 %copy-start.9 = (bf16[192,2048]{1,0:T(8,128)(2,1)}, bf16[192,2048]{1,0:T(8,128)(2,1)S(1)}, u32[]{:S(2)}) copy-start(bf16[192,2048]{1,0:T(8,128)(2,1)S(1)} %get-tuple-element.90.act_ref) | copy-start | bytes 2359300
  33.3 18.2 %collective-permute-start.3 = (bf16[1552,128]{1,0:T(8,128)(2,1)S(1)}, bf16[1552,128]{1,0:T(8,128)(2,1)S(1)}, u32[]{:S(2)}, u32[]{:S(2)}) collective-permute-start(bf16[1552,128]{1,0:T(8,128)(2,1)S(1)} %get-tuple-element.72.q0_ref), channel_id=1, source_target_pairs={{0,8},{8,16},{16,24},{24,0},{1,9},{9,17},{17,25},{25,1},{2,10},{10... | collective-permute-start | bytes 1191944 | tf_op jit(solution)/shard_map/ppermute | solution.py:561
  34.9 17.2 %collective-permute-start.4 = (bf16[1552,128]{1,0:T(8,128)(2,1)S(1)}, bf16[1552,128]{1,0:T(8,128)(2,1)S(1)}, u32[]{:S(2)}, u32[]{:S(2)}) collective-permute-start(bf16[1552,128]{1,0:T(8,128)(2,1)S(1)} %get-tuple-element.73.q1_ref), channel_id=1, source_target_pairs={{0,24},{8,0},{16,8},{24,16},{1,25},{9,1},{17,9},{25,17},{2,26},{10... | collective-permute-start | bytes 1191944 | tf_op jit(solution)/shard_map/ppermute | solution.py:562
  37.2 20.3 %collective-permute-start.10 = (bf16[80,2048]{1,0:T(8,128)(2,1)}, bf16[80,2048]{1,0:T(8,128)(2,1)S(1)}, u32[]{:S(2)}, u32[]{:S(2)}) collective-permute-start(bf16[80,2048]{1,0:T(8,128)(2,1)} %get-tuple-element.98.refs_1_), channel_id=1, source_target_pairs={{0,2},{2,4},{4,6},{1,3},{3,5},{5,7},{8,10},{10,12},{12,14},{9,11},... | collective-permute-start | bytes 983048 | tf_op jit(solution)/shard_map/ppermute | solution.py:485
  40.6 4.8 %copy-start.15 = (bf16[160,320]{1,0:T(8,128)(2,1)S(1)}, bf16[160,320]{1,0:T(8,128)(2,1)}, u32[]{:S(2)}) copy-start(bf16[160,320]{1,0:T(8,128)(2,1)} %constant.76.clone.refs_7_) | copy-start | bytes 307204
  44.1 7.4 %copy-start.5 = (bf16[160,2048]{1,0:T(8,128)(2,1)}, bf16[160,2048]{1,0:T(8,128)(2,1)S(1)}, u32[]{:S(2)}) copy-start(bf16[160,2048]{1,0:T(8,128)(2,1)S(1)} %get-tuple-element.79.refs_0_.rows_ref) | copy-start | bytes 1966084
  44.1 21.9 %collective-permute-start.11 = (bf16[80,2048]{1,0:T(8,128)(2,1)}, bf16[80,2048]{1,0:T(8,128)(2,1)S(1)}, u32[]{:S(2)}, u32[]{:S(2)}) collective-permute-start(bf16[80,2048]{1,0:T(8,128)(2,1)} %get-tuple-element.99.refs_0_), channel_id=1, source_target_pairs={{2,0},{4,2},{6,4},{3,1},{5,3},{7,5},{10,8},{12,10},{14,12},{11,9},... | collective-permute-start | bytes 983048 | tf_op jit(solution)/shard_map/ppermute | solution.py:485
  51.5 14.5 %copy-start.11 = (bf16[160,2048]{1,0:T(8,128)(2,1)}, bf16[160,2048]{1,0:T(8,128)(2,1)S(1)}, u32[]{:S(2)}) copy-start(bf16[160,2048]{1,0:T(8,128)(2,1)S(1)} %get-tuple-element.108.act_ref) | copy-start | bytes 1966084
  51.5 14.5 %copy-start.16 = (bf16[1296,128]{1,0:T(8,128)(2,1)}, bf16[1296,128]{1,0:T(8,128)(2,1)S(1)}, u32[]{:S(2)}) copy-start(bf16[1296,128]{1,0:T(8,128)(2,1)S(1)} %get-tuple-element.84.q0_ref) | copy-start | bytes 995332
  51.5 20.5 %collective-permute-start.8 = (bf16[1296,128]{1,0:T(8,128)(2,1)S(1)}, bf16[1296,128]{1,0:T(8,128)(2,1)S(1)}, u32[]{:S(2)}, u32[]{:S(2)}) collective-permute-start(bf16[1296,128]{1,0:T(8,128)(2,1)S(1)} %get-tuple-element.84.q0_ref), channel_id=1, source_target_pairs={{0,8},{8,16},{16,24},{24,0},{1,9},{9,17},{17,25},{25,1},{2,10},{10... | collective-permute-start | bytes 995336 | tf_op jit(solution)/shard_map/ppermute | solution.py:561
  54.2 38.6 %collective-permute-start.7 = (bf16[1536,128]{1,0:T(8,128)(2,1)}, bf16[1536,128]{1,0:T(8,128)(2,1)}, u32[]{:S(2)}, u32[]{:S(2)}) collective-permute-start(bf16[1536,128]{1,0:T(8,128)(2,1)} %get-tuple-element.91), channel_id=1, source_target_pairs={{0,24},{8,0},{16,8},{24,16},{1,25},{9,1},{17,9},{25,17},{2,26},{10... | collective-permute-start | bytes 1179656 | tf_op jit(solution)/shard_map/ppermute | solution.py:569
  57.5 37.4 %collective-permute-start.15 = (bf16[1536,128]{1,0:T(8,128)(2,1)}, bf16[1536,128]{1,0:T(8,128)(2,1)S(1)}, u32[]{:S(2)}, u32[]{:S(2)}) collective-permute-start(bf16[1536,128]{1,0:T(8,128)(2,1)} %get-tuple-element.88), channel_id=1, source_target_pairs={{0,8},{8,16},{16,24},{24,0},{1,9},{9,17},{17,25},{25,1},{2,10},{10... | collective-permute-start | bytes 1179656 | tf_op jit(solution)/shard_map/ppermute | solution.py:568
  57.5 31.7 %collective-permute-start.9 = (bf16[1296,128]{1,0:T(8,128)(2,1)}, bf16[1296,128]{1,0:T(8,128)(2,1)S(1)}, u32[]{:S(2)}, u32[]{:S(2)}) collective-permute-start(bf16[1296,128]{1,0:T(8,128)(2,1)} %get-tuple-element.85.q1_ref), channel_id=1, source_target_pairs={{0,24},{8,0},{16,8},{24,16},{1,25},{9,1},{17,9},{25,17},{2,26},{10... | collective-permute-start | bytes 995336 | tf_op jit(solution)/shard_map/ppermute | solution.py:562
  66.0 5.1 %copy-start.7 = (bf16[160,2048]{1,0:T(8,128)(2,1)}, bf16[160,2048]{1,0:T(8,128)(2,1)S(1)}, u32[]{:S(2)}) copy-start(bf16[160,2048]{1,0:T(8,128)(2,1)S(1)} %get-tuple-element.96.refs_0_.rows_ref) | copy-start | bytes 1966084
  71.1 0.9 copy-start.13
  72.0 34.8 %collective-permute-start.13 = (bf16[1296,128]{1,0:T(8,128)(2,1)}, bf16[1296,128]{1,0:T(8,128)(2,1)S(1)}, u32[]{:S(2)}, u32[]{:S(2)}) collective-permute-start(bf16[1296,128]{1,0:T(8,128)(2,1)} %get-tuple-element.101.q0_ref), channel_id=1, source_target_pairs={{0,8},{8,16},{16,24},{24,0},{1,9},{9,17},{17,25},{25,1},{2,10},{10... | collective-permute-start | bytes 995336 | tf_op jit(solution)/shard_map/ppermute | solution.py:561
  72.0 34.9 %collective-permute-start.14 = (bf16[1296,128]{1,0:T(8,128)(2,1)}, bf16[1296,128]{1,0:T(8,128)(2,1)S(1)}, u32[]{:S(2)}, u32[]{:S(2)}) collective-permute-start(bf16[1296,128]{1,0:T(8,128)(2,1)} %get-tuple-element.102.q1_ref), channel_id=1, source_target_pairs={{0,24},{8,0},{16,8},{24,16},{1,25},{9,1},{17,9},{25,17},{2,26},{10... | collective-permute-start | bytes 995336 | tf_op jit(solution)/shard_map/ppermute | solution.py:562
  75.9 18.9 %copy-start.6 = (bf16[160,2048]{1,0:T(8,128)(2,1)S(1)}, bf16[160,2048]{1,0:T(8,128)(2,1)}, u32[]{:S(2)}) copy-start(bf16[160,2048]{1,0:T(8,128)(2,1)} %copy-done.5) | copy-start | bytes 1966084
  75.9 18.9 %copy-start.12 = (bf16[160,2048]{1,0:T(8,128)(2,1)S(1)}, bf16[160,2048]{1,0:T(8,128)(2,1)}, u32[]{:S(2)}) copy-start(bf16[160,2048]{1,0:T(8,128)(2,1)} %copy-done.11) | copy-start | bytes 1966084
  89.2 1.0 copy-start.17
  92.8 26.6 %collective-permute-start.12 = (bf16[1280,128]{1,0:T(8,128)(2,1)S(1)}, bf16[1280,128]{1,0:T(8,128)(2,1)S(1)}, u32[]{:S(2)}, u32[]{:S(2)}) collective-permute-start(bf16[1280,128]{1,0:T(8,128)(2,1)S(1)} %get-tuple-element.105), channel_id=1, source_target_pairs={{0,24},{8,0},{16,8},{24,16},{1,25},{9,1},{17,9},{25,17},{2,26},{10... | collective-permute-start | bytes 983048 | tf_op jit(solution)/shard_map/ppermute | solution.py:569
  92.8 26.5 %collective-permute-start.17 = (bf16[1280,128]{1,0:T(8,128)(2,1)S(1)}, bf16[1280,128]{1,0:T(8,128)(2,1)S(1)}, u32[]{:S(2)}, u32[]{:S(2)}) collective-permute-start(bf16[1280,128]{1,0:T(8,128)(2,1)S(1)} %get-tuple-element.106), channel_id=1, source_target_pairs={{0,8},{8,16},{16,24},{24,0},{1,9},{9,17},{17,25},{25,1},{2,10},{10... | collective-permute-start | bytes 983048 | tf_op jit(solution)/shard_map/ppermute | solution.py:568
  94.9 3.4 %copy-start.1 = (bf16[257,128,128]{2,1,0:T(8,128)(2,1)S(1)}, bf16[257,128,128]{2,1,0:T(8,128)(2,1)}, u32[]{:S(2)}) copy-start(bf16[257,128,128]{2,1,0:T(8,128)(2,1)} %copy-done) | copy-start | bytes 25264132
  98.2 3.4 %copy-start.4 = (bf16[257,128,128]{2,1,0:T(8,128)(2,1)S(1)}, bf16[257,128,128]{2,1,0:T(8,128)(2,1)}, u32[]{:S(2)}) copy-start(bf16[257,128,128]{2,1,0:T(8,128)(2,1)} %copy-done.3) | copy-start | bytes 25264132
  101.6 11.8 %copy-start.2 = (bf16[257,128,128]{2,1,0:T(8,128)(2,1)S(1)}, bf16[257,128,128]{2,1,0:T(8,128)(2,1)}, u32[]{:S(2)}) copy-start(bf16[257,128,128]{2,1,0:T(8,128)(2,1)} %copy-done) | copy-start | bytes 25264132
  106.8 6.7 %copy-start.10 = (bf16[192,2048]{1,0:T(8,128)(2,1)S(1)}, bf16[192,2048]{1,0:T(8,128)(2,1)}, u32[]{:S(2)}) copy-start(bf16[192,2048]{1,0:T(8,128)(2,1)} %copy-done.9) | copy-start | bytes 2359300
  109.6 14.9 %collective-permute-start.18 = (bf16[1280,128]{1,0:T(8,128)(2,1)S(1)}, bf16[1280,128]{1,0:T(8,128)(2,1)S(1)}, u32[]{:S(2)}, u32[]{:S(2)}) collective-permute-start(bf16[1280,128]{1,0:T(8,128)(2,1)S(1)} %get-tuple-element.112), channel_id=1, source_target_pairs={{0,8},{8,16},{16,24},{24,0},{1,9},{9,17},{17,25},{25,1},{2,10},{10... | collective-permute-start | bytes 983048 | tf_op jit(solution)/shard_map/ppermute | solution.py:568
  110.6 16.8 %collective-permute-start.16 = (bf16[1280,128]{1,0:T(8,128)(2,1)S(1)}, bf16[1280,128]{1,0:T(8,128)(2,1)S(1)}, u32[]{:S(2)}, u32[]{:S(2)}) collective-permute-start(bf16[1280,128]{1,0:T(8,128)(2,1)S(1)} %get-tuple-element.111), channel_id=1, source_target_pairs={{0,24},{8,0},{16,8},{24,16},{1,25},{9,1},{17,9},{25,17},{2,26},{10... | collective-permute-start | bytes 983048 | tf_op jit(solution)/shard_map/ppermute | solution.py:569
  113.5 5.9 %copy-start.8 = (bf16[160,2048]{1,0:T(8,128)(2,1)S(1)}, bf16[160,2048]{1,0:T(8,128)(2,1)}, u32[]{:S(2)}) copy-start(bf16[160,2048]{1,0:T(8,128)(2,1)} %copy-done.7) | copy-start | bytes 1966084
  113.5 5.9 %copy-start.14 = (bf16[160,2048]{1,0:T(8,128)(2,1)S(1)}, bf16[160,2048]{1,0:T(8,128)(2,1)}, u32[]{:S(2)}) copy-start(bf16[160,2048]{1,0:T(8,128)(2,1)} %copy-done.13) | copy-start | bytes 1966084

commit v5 on v4

--- a/solution.py
+++ b/solution.py
@@ -296,7 +296,7 @@
 
 def send_onward(away, q0, q1, right1, left1):
     rows, block = q0.shape
-    steps = 4
+    steps = 2
     size = (rows - 16) // steps
     part = pl.BlockSpec((size, block), lambda s, a: (s, 0))
     code = pl.BlockSpec((16, block), lambda s, a: ((rows - 16) // 16, 0))

time: 132 us -> 132 us (level)
  Pallas kernels: 64.5 us -> 62.3 us
  waiting for transfers between devices: 16.6 us -> 18.3 us
    pallas_call x3, Pallas kernels: 7.52 us -> 5.35 us  [send_onward(): pl.pallas_call(onward_kernel, grid_spec=pltpu.PrefetchScalarGridSpec(num_...]
    ppermute x3, waiting for transfers between devices: 0.01 us -> 1.7 us  [send_second(): left2.append(lax.ppermute(to_left, 'gx', behind))]
  transfers between devices with their start and end apart: 19 -> 19, of which waited for: 3 -> 5; matrix products, arithmetic and copies ran while one was open for 2% -> 2% of each run, Pallas kernels for 44% -> 43%
where the time goes in v5:
time: 132 us; the launch traced here: 130 us
  Pallas kernels  62.3 us (47%)
  starting transfers between devices  38.2 us (29%)
  waiting for transfers between devices  18.3 us (14%)
  local copies, waits for them, and re-layouts  9.05 us (7%)
  other arithmetic  1.58 us (1%)
    pallas_call x3, Pallas kernels, local_columns(): pl.pallas_call(functools.partial(local_kernel, groups), grid_spec=pltpu.P...  16.1 us
    pallas_call x3, Pallas kernels, action_part(): pl.pallas_call(functools.partial(action_kernel, groups, rows_y, cols, low...  15.6 us
    pallas_call x3, Pallas kernels, phi_part(): pl.pallas_call(functools.partial(phi_kernel, groups, len(fields), loads),...  15.3 us
    ppermute x3, waiting for transfers between devices, send_first(): left1.append(lax.ppermute(q1, 'gx', behind))  13.7 us
    ppermute x3, starting transfers between devices, send_halo(): lax.ppermute(up, 'gy', shifts('gy', 1))  13.5 us
    ppermute x3, starting transfers between devices, send_first(): left1.append(lax.ppermute(q1, 'gx', behind))  9.92 us
    unnamed x42, local copies, waits for them, and re-layouts  8.67 us
    ppermute x3, starting transfers between devices, send_second(): left2.append(lax.ppermute(to_left, 'gx', behind))  6.07 us
  transfers between devices with their start and end apart: 19, of which 5 were waited for; matrix products, arithmetic and copies ran while one was open for 2% of the time, Pallas kernels for 43%

profile of v5, /device:TPU:0, one launch (start us, length us, event | category | flops | bytes accessed | tf_op | source)
XLA Modules:
  0.0 129.9 jit_solution(8651042034849155226)
XLA Ops:
  0.0 4.1 %prepare.1 = (bf16[96,2048]{1,0:T(8,128)(2,1)S(1)}, bf16[96,2048]{1,0:T(8,128)(2,1)S(1)}, bf16[80,2048]{1,0:T(8,128)(2,1)S(1)}, bf16[80,2048]{1,0:T(8,128)(2,1)S...) custom-call(bf16[8192,128]{1,0:T(8,128)(2,1)} %bitcast.17, ...), custom_call_target="tpu_custom_call" | custom-call | tf_op jit(solution)/shard_map/prepare/pallas_call | solution.py:101
  4.1 4.9 %collective-permute-start = (bf16[96,2048]{1,0:T(8,128)(2,1)S(1)}, bf16[96,2048]{1,0:T(8,128)(2,1)S(1)}, u32[]{:S(2)}, u32[]{:S(2)}) collective-permute-start(bf16[96,2048]{1,0:T(8,128)(2,1)S(1)} %get-tuple-element.66.refs_1_), channel_id=1, source_target_pairs={{0,2},{2,4},{4,6},{1,3},{3,5},{5,7},{8,10},{10,12},{12,14},{9,11},... | collective-permute-start | bytes 1179656 | tf_op jit(solution)/shard_map/ppermute | solution.py:485
  9.0 1.3 collective-permute-start.1
  10.3 0.1 collective-permute-start.2
  10.4 0.6 fusion.2
  11.1 0.1 select_reduce_fusion.1
  11.2 0.1 select_reduce_fusion
  11.3 0.1 fusion.3
  11.4 0.1 copy.20
  11.5 0.1 slice.15.which_ref
  11.6 5.3 %collective-permute-start.5 = (bf16[80,2048]{1,0:T(8,128)(2,1)S(1)}, bf16[80,2048]{1,0:T(8,128)(2,1)}, u32[]{:S(2)}, u32[]{:S(2)}) collective-permute-start(bf16[80,2048]{1,0:T(8,128)(2,1)S(1)} %get-tuple-element.81.refs_1_), channel_id=1, source_target_pairs={{0,2},{2,4},{4,6},{1,3},{3,5},{5,7},{8,10},{10,12},{12,14},{9,11},... | collective-permute-start | bytes 983048 | tf_op jit(solution)/shard_map/ppermute | solution.py:485
  16.8 1.3 collective-permute-start.6
  18.1 0.6 pad_add_fusion.which_ref
  18.8 7.2 %phi_part.3 = (bf16[192,2048]{1,0:T(8,128)(2,1)S(1)}, f32[8,192,256]{2,1,0:T(8,128)S(1)}, bf16[257,128,128]{2,1,0:T(8,128)(2,1)S(1)}, bf16[257,128,128]{2,1,0:T(8,128)(2,1)S(1)}) custom-call(s32[256]{0:T(256)S(1)} %slice.15.which_ref, bf16[96,2048]{1,0:T(8,128)(2,1)S(1)} %get-tuple-element.65.refs_0_, bf16[96,2048]{1,0:T(8,128)(2,1)S(1)} %get-tuple-element.66.refs_1_, ...), custom_call_target="tpu_custom_call" | custom-call | flops 402653184 | bytes 786432 | tf_op jit(solution)/shard_map/phi_part/pallas_call | solution.py:178
  26.0 2.8 %collective-permute-done.1.refs_3_ = bf16[96,2048]{1,0:T(8,128)(2,1)S(1)} collective-permute-done((bf16[96,2048]{1,0:T(8,128)(2,1)S(1)}, bf16[96,2048]{1,0:T(8,128)(2,1)S(1)}, u32[]{:S(2)}, u32[]{:S(2)}) %collective-permute-start.1) | collective-permute-done | bytes 393248 | tf_op jit(solution)/shard_map/ppermute | solution.py:485
  28.8 4.5 %action_part.3 = (bf16[192,2048]{1,0:T(8,128)(2,1)S(1)}, bf16[1552,128]{1,0:T(8,128)(2,1)S(1)}, bf16[1552,128]{1,0:T(8,128)(2,1)S(1)}) custom-call(s32[259]{0:T(512)S(1)} %pad_add_fusion.which_ref, bf16[192,2048]{1,0:T(8,128)(2,1)S(1)} %get-tuple-element.67.refs_0_.rows_ref, f32[8,192,256]{2,1,0:T(8,128)S(1)} %get-tuple-element.68.refs_1_, ...), custom_call_target="tpu_custom_call" | custom-call | flops 402653184 | bytes 786432 | tf_op jit(solution)/shard_map/action_part/pallas_call | solution.py:269
  33.3 1.6 %collective-permute-start.3 = (bf16[1552,128]{1,0:T(8,128)(2,1)S(1)}, bf16[1552,128]{1,0:T(8,128)(2,1)S(1)}, u32[]{:S(2)}, u32[]{:S(2)}) collective-permute-start(bf16[1552,128]{1,0:T(8,128)(2,1)S(1)} %get-tuple-element.72.q0_ref), channel_id=1, source_target_pairs={{0,8},{8,16},{16,24},{24,0},{1,9},{9,17},{17,25},{25,1},{2,10},{10... | collective-permute-start | bytes 1191944 | tf_op jit(solution)/shard_map/ppermute | solution.py:561
  34.9 2.3 %collective-permute-start.4 = (bf16[1552,128]{1,0:T(8,128)(2,1)S(1)}, bf16[1552,128]{1,0:T(8,128)(2,1)S(1)}, u32[]{:S(2)}, u32[]{:S(2)}) collective-permute-start(bf16[1552,128]{1,0:T(8,128)(2,1)S(1)} %get-tuple-element.73.q1_ref), channel_id=1, source_target_pairs={{0,24},{8,0},{16,8},{24,16},{1,25},{9,1},{17,9},{25,17},{2,26},{10... | collective-permute-start | bytes 1191944 | tf_op jit(solution)/shard_map/ppermute | solution.py:562
  37.2 3.4 %collective-permute-start.10 = (bf16[80,2048]{1,0:T(8,128)(2,1)}, bf16[80,2048]{1,0:T(8,128)(2,1)S(1)}, u32[]{:S(2)}, u32[]{:S(2)}) collective-permute-start(bf16[80,2048]{1,0:T(8,128)(2,1)} %get-tuple-element.98.refs_1_), channel_id=1, source_target_pairs={{0,2},{2,4},{4,6},{1,3},{3,5},{5,7},{8,10},{10,12},{12,14},{9,11},... | collective-permute-start | bytes 983048 | tf_op jit(solution)/shard_map/ppermute | solution.py:485
  40.6 3.5 %phi_part.4 = (bf16[160,2048]{1,0:T(8,128)(2,1)S(1)}, f32[8,160,256]{2,1,0:T(8,128)S(1)}) custom-call(s32[256]{0:T(256)S(1)} %slice.15.which_ref, bf16[80,2048]{1,0:T(8,128)(2,1)S(1)} %get-tuple-element.82.refs_0_, bf16[80,2048]{1,0:T(8,128)(2,1)S(1)} %get-tuple-element.81.refs_1_, bf16[257,128,128]{2,1,0:T(8,128)(2,1)S(1)} %get-tuple-element.78.refs_2_.hk_ref), custom_call_target="tpu_custom_call" | custom-call | flops 335544320 | bytes 655360 | tf_op jit(solution)/shard_map/phi_part/pallas_call | solution.py:178
  44.1 1.3 collective-permute-start.11
  45.4 6.0 %action_part.4 = (bf16[160,2048]{1,0:T(8,128)(2,1)S(1)}, bf16[1296,128]{1,0:T(8,128)(2,1)S(1)}, bf16[1296,128]{1,0:T(8,128)(2,1)}) custom-call(s32[259]{0:T(512)S(1)} %pad_add_fusion.which_ref, bf16[160,2048]{1,0:T(8,128)(2,1)S(1)} %get-tuple-element.79.refs_0_.rows_ref, f32[8,160,256]{2,1,0:T(8,128)S(1)} %get-tuple-element.80.refs_1_, ...), custom_call_target="tpu_custom_call" | custom-call | flops 335544320 | bytes 655360 | tf_op jit(solution)/shard_map/action_part/pallas_call | solution.py:269
  51.6 0.6 collective-permute-done.4.left_ref.left_code
  52.1 1.6 %send_onward.3 = (bf16[1536,128]{1,0:T(8,128)(2,1)}, bf16[1536,128]{1,0:T(8,128)(2,1)}) custom-call(s32[1]{0:T(128)} %bitcast.3.away_ref, bf16[1552,128]{1,0:T(8,128)(2,1)S(1)} %get-tuple-element.72.q0_ref, bf16[1552,128]{1,0:T(8,128)(2,1)S(1)} %get-tuple-element.73.q1_ref, bf16[1552,128]{1,0:T(8,128)(2,1)S(1)} %collective-permute-done.3.right_ref.right_code, ...), custom_call_target="tpu_custom_call" | custom-call | bytes 2383872 | tf_op jit(solution)/shard_map/send_onward/pallas_call | solution.py:303
  53.7 3.2 %collective-permute-start.7 = (bf16[1536,128]{1,0:T(8,128)(2,1)}, bf16[1536,128]{1,0:T(8,128)(2,1)}, u32[]{:S(2)}, u32[]{:S(2)}) collective-permute-start(bf16[1536,128]{1,0:T(8,128)(2,1)} %get-tuple-element.91), channel_id=1, source_target_pairs={{0,24},{8,0},{16,8},{24,16},{1,25},{9,1},{17,9},{25,17},{2,26},{10... | collective-permute-start | bytes 1179656 | tf_op jit(solution)/shard_map/ppermute | solution.py:569
  57.0 3.8 %collective-permute-start.9 = (bf16[1296,128]{1,0:T(8,128)(2,1)}, bf16[1296,128]{1,0:T(8,128)(2,1)S(1)}, u32[]{:S(2)}, u32[]{:S(2)}) collective-permute-start(bf16[1296,128]{1,0:T(8,128)(2,1)} %get-tuple-element.85.q1_ref), channel_id=1, source_target_pairs={{0,24},{8,0},{16,8},{24,16},{1,25},{9,1},{17,9},{25,17},{2,26},{10... | collective-permute-start | bytes 995336 | tf_op jit(solution)/shard_map/ppermute | solution.py:562
  60.8 4.7 %phi_part.5 = (bf16[160,2048]{1,0:T(8,128)(2,1)S(1)}, f32[8,160,256]{2,1,0:T(8,128)S(1)}) custom-call(s32[256]{0:T(256)S(1)} %slice.15.which_ref, bf16[80,2048]{1,0:T(8,128)(2,1)} %get-tuple-element.99.refs_0_, bf16[80,2048]{1,0:T(8,128)(2,1)} %get-tuple-element.98.refs_1_, bf16[257,128,128]{2,1,0:T(8,128)(2,1)S(1)} %get-tuple-element.78.refs_2_.hk_ref), custom_call_target="tpu_custom_call" | custom-call | flops 335544320 | bytes 655360 | tf_op jit(solution)/shard_map/phi_part/pallas_call | solution.py:178
  65.5 5.1 %action_part.5 = (bf16[160,2048]{1,0:T(8,128)(2,1)S(1)}, bf16[1296,128]{1,0:T(8,128)(2,1)}, bf16[1296,128]{1,0:T(8,128)(2,1)}) custom-call(s32[259]{0:T(512)S(1)} %pad_add_fusion.which_ref, bf16[160,2048]{1,0:T(8,128)(2,1)S(1)} %get-tuple-element.96.refs_0_.rows_ref, f32[8,160,256]{2,1,0:T(8,128)S(1)} %get-tuple-element.97.refs_1_, ...), custom_call_target="tpu_custom_call" | custom-call | flops 335544320 | bytes 655360 | tf_op jit(solution)/shard_map/action_part/pallas_call | solution.py:269
  70.6 0.9 copy-done.13
  71.5 3.8 %collective-permute-start.14 = (bf16[1296,128]{1,0:T(8,128)(2,1)}, bf16[1296,128]{1,0:T(8,128)(2,1)S(1)}, u32[]{:S(2)}, u32[]{:S(2)}) collective-permute-start(bf16[1296,128]{1,0:T(8,128)(2,1)} %get-tuple-element.102.q1_ref), channel_id=1, source_target_pairs={{0,24},{8,0},{16,8},{24,16},{1,25},{9,1},{17,9},{25,17},{2,26},{10... | collective-permute-start | bytes 995336 | tf_op jit(solution)/shard_map/ppermute | solution.py:562
  75.3 0.1 copy.19
  75.3 0.1 slice.13.which_ref
  75.4 13.1 %collective-permute-done.9.left_ref.left_code = bf16[1296,128]{1,0:T(8,128)(2,1)S(1)} collective-permute-done((bf16[1296,128]{1,0:T(8,128)(2,1)}, bf16[1296,128]{1,0:T(8,128)(2,1)S(1)}, u32[]{:S(2)}, u32[]{:S(2)}) %collective-permute-start.9) | collective-permute-done | bytes 331808 | tf_op jit(solution)/shard_map/ppermute | solution.py:562
  88.5 1.0 copy-done.17
  89.5 1.8 %send_onward.4 = (bf16[1280,128]{1,0:T(8,128)(2,1)S(1)}, bf16[1280,128]{1,0:T(8,128)(2,1)S(1)}) custom-call(s32[1]{0:T(128)} %bitcast.3.away_ref, bf16[1296,128]{1,0:T(8,128)(2,1)S(1)} %copy-done.17, bf16[1296,128]{1,0:T(8,128)(2,1)} %get-tuple-element.85.q1_ref, bf16[1296,128]{1,0:T(8,128)(2,1)S(1)} %collective-permute-done.8.right_ref.right_code, ...), custom_call_target="tpu_custom_call" | custom-call | bytes 1990656 | tf_op jit(solution)/shard_map/send_onward/pallas_call | solution.py:303
  91.4 2.0 %collective-permute-start.17 = (bf16[1280,128]{1,0:T(8,128)(2,1)S(1)}, bf16[1280,128]{1,0:T(8,128)(2,1)S(1)}, u32[]{:S(2)}, u32[]{:S(2)}) collective-permute-start(bf16[1280,128]{1,0:T(8,128)(2,1)S(1)} %get-tuple-element.106), channel_id=1, source_target_pairs={{0,8},{8,16},{16,24},{24,0},{1,9},{9,17},{17,25},{25,1},{2,10},{10... | collective-permute-start | bytes 983048 | tf_op jit(solution)/shard_map/ppermute | solution.py:568
  93.4 3.4 %copy-done.1 = bf16[257,128,128]{2,1,0:T(8,128)(2,1)S(1)} copy-done((bf16[257,128,128]{2,1,0:T(8,128)(2,1)S(1)}, bf16[257,128,128]{2,1,0:T(8,128)(2,1)}, u32[]{:S(2)}) %copy-start.1) | copy-done | bytes 8421400
  96.8 3.4 %copy-done.4 = bf16[257,128,128]{2,1,0:T(8,128)(2,1)S(1)} copy-done((bf16[257,128,128]{2,1,0:T(8,128)(2,1)S(1)}, bf16[257,128,128]{2,1,0:T(8,128)(2,1)}, u32[]{:S(2)}) %copy-start.4) | copy-done | bytes 8421400
  100.2 5.1 %local_columns.4.refs_2_.refs_3_ = bf16[2560,128]{1,0:T(8,128)(2,1)S(1)} custom-call(s32[256]{0:T(256)S(1)} %slice.13.which_ref, bf16[160,2048]{1,0:T(8,128)(2,1)S(1)} %copy-done.12, bf16[160,2048]{1,0:T(8,128)(2,1)S(1)} %copy-done.6, bf16[257,128,128]{2,1,0:T(8,128)(2,1)S(1)} %copy-done.1, bf16[257,128,128]{2,1,0:T(8,128)(2,1)S(1)} %copy-done.4, ...), custom_call_target="tpu_custom_call" | custom-call | flops 671088640 | bytes 655360 | tf_op jit(solution)/shard_map/local_columns/pallas_call | solution.py:350
  105.3 2.0 %send_onward.5 = (bf16[1280,128]{1,0:T(8,128)(2,1)S(1)}, bf16[1280,128]{1,0:T(8,128)(2,1)S(1)}) custom-call(s32[1]{0:T(128)} %bitcast.3.away_ref, bf16[1296,128]{1,0:T(8,128)(2,1)} %get-tuple-element.101.q0_ref, bf16[1296,128]{1,0:T(8,128)(2,1)} %get-tuple-element.102.q1_ref, bf16[1296,128]{1,0:T(8,128)(2,1)S(1)} %collective-permute-done.13.right_ref.right_code, ...), custom_call_target="tpu_custom_call" | custom-call | bytes 1990656 | tf_op jit(solution)/shard_map/send_onward/pallas_call | solution.py:303
  107.3 1.1 collective-permute-start.18
  108.4 2.8 %collective-permute-start.16 = (bf16[1280,128]{1,0:T(8,128)(2,1)S(1)}, bf16[1280,128]{1,0:T(8,128)(2,1)S(1)}, u32[]{:S(2)}, u32[]{:S(2)}) collective-permute-start(bf16[1280,128]{1,0:T(8,128)(2,1)S(1)} %get-tuple-element.111), channel_id=1, source_target_pairs={{0,24},{8,0},{16,8},{24,16},{1,25},{9,1},{17,9},{25,17},{2,26},{10... | collective-permute-start | bytes 983048 | tf_op jit(solution)/shard_map/ppermute | solution.py:569
  111.2 5.8 %local_columns.3.refs_0_.refs_1_ = bf16[3072,128]{1,0:T(8,128)(2,1)S(1)} custom-call(s32[256]{0:T(256)S(1)} %slice.13.which_ref, bf16[192,2048]{1,0:T(8,128)(2,1)S(1)} %copy-done.10, bf16[192,2048]{1,0:T(8,128)(2,1)S(1)} %get-tuple-element.67.refs_0_.rows_ref, bf16[257,128,128]{2,1,0:T(8,128)(2,1)S(1)} %copy-done.2, bf16[257,128,128]{2,1,0:T(8,128)(2,1)S(1)} %copy-done.4, ...), custom_call_target="tpu_custom_call" | custom-call | flops 805306368 | bytes 786432 | tf_op jit(solution)/shard_map/local_columns/pallas_call | solution.py:350
  117.1 5.2 %local_columns.5.refs_4_.refs_5_ = bf16[2560,128]{1,0:T(8,128)(2,1)S(1)} custom-call(s32[256]{0:T(256)S(1)} %slice.13.which_ref, bf16[160,2048]{1,0:T(8,128)(2,1)S(1)} %copy-done.14, bf16[160,2048]{1,0:T(8,128)(2,1)S(1)} %copy-done.8, bf16[257,128,128]{2,1,0:T(8,128)(2,1)S(1)} %copy-done.2, bf16[257,128,128]{2,1,0:T(8,128)(2,1)S(1)} %copy-done.4, ...), custom_call_target="tpu_custom_call" | custom-call | flops 671088640 | bytes 655360 | tf_op jit(solution)/shard_map/local_columns/pallas_call | solution.py:350
  122.3 0.1 collective-permute-done.18.refs_5_
  122.4 2.8 %finish.2.refs_7_ = bf16[8192,128]{1,0:T(8,128)(2,1)} custom-call(bf16[512,512]{1,0:T(8,128)(2,1)} %constant.74.clone.mix_ref.refs_0_, bf16[3072,128]{1,0:T(8,128)(2,1)S(1)} %local_columns.3.refs_0_.refs_1_, bf16[1536,128]{1,0:T(8,128)(2,1)S(1)} %collective-permute-done.15.refs_1_, bf16[2560,128]{1,0:T(8,128)(2,1)S(1)} %local_columns.4.refs_2_.refs_3_, ...), custom_call_target="tpu_custom_call" | custom-call | tf_op jit(solution)/shard_map/finish/pallas_call | solution.py:433
  125.2 1.7 %collective-permute-done.16.refs_6_ = bf16[1280,128]{1,0:T(8,128)(2,1)S(1)} collective-permute-done((bf16[1280,128]{1,0:T(8,128)(2,1)S(1)}, bf16[1280,128]{1,0:T(8,128)(2,1)S(1)}, u32[]{:S(2)}, u32[]{:S(2)}) %collective-permute-start.16) | collective-permute-done | bytes 327712 | tf_op jit(solution)/shard_map/ppermute | solution.py:569
  126.9 3.0 %finish.3 = bf16[8192,128]{1,0:T(8,128)(2,1)} custom-call(bf16[512,512]{1,0:T(8,128)(2,1)} %constant.74.clone.mix_ref.refs_0_, bf16[3072,128]{1,0:T(8,128)(2,1)S(1)} %local_columns.3.refs_0_.refs_1_, bf16[1536,128]{1,0:T(8,128)(2,1)} %collective-permute-done.7.refs_2_, ...), custom_call_target="tpu_custom_call", output_to_operand_aliasing={{}: (7, {})} | custom-call | tf_op jit(solution)/shard_map/finish/pallas_call | solution.py:433
  (59 shorter events, 0.3 us)
Async XLA Ops:
  0.0 10.4 %copy-start.20 = (s32[32]{0:T(128)S(1)}, s32[32]{0:T(128)}, u32[]{:S(2)}) copy-start(s32[32]{0:T(128)} %param.17) | copy-start | bytes 388
  0.0 11.2 %copy-start.19 = (s32[16,16]{1,0:T(8,128)S(1)}, s32[16,16]{1,0:T(8,128)}, u32[]{:S(2)}) copy-start(s32[16,16]{1,0:T(8,128)} %param.16) | copy-start | bytes 3076
  4.1 21.9 %collective-permute-start = (bf16[96,2048]{1,0:T(8,128)(2,1)S(1)}, bf16[96,2048]{1,0:T(8,128)(2,1)S(1)}, u32[]{:S(2)}, u32[]{:S(2)}) collective-permute-start(bf16[96,2048]{1,0:T(8,128)(2,1)S(1)} %get-tuple-element.66.refs_1_), channel_id=1, source_target_pairs={{0,2},{2,4},{4,6},{1,3},{3,5},{5,7},{8,10},{10,12},{12,14},{9,11},... | collective-permute-start | bytes 1179656 | tf_op jit(solution)/shard_map/ppermute | solution.py:485
  9.0 19.9 %collective-permute-start.1 = (bf16[96,2048]{1,0:T(8,128)(2,1)S(1)}, bf16[96,2048]{1,0:T(8,128)(2,1)S(1)}, u32[]{:S(2)}, u32[]{:S(2)}) collective-permute-start(bf16[96,2048]{1,0:T(8,128)(2,1)S(1)} %get-tuple-element.65.refs_0_), channel_id=1, source_target_pairs={{2,0},{4,2},{6,4},{3,1},{5,3},{7,5},{10,8},{12,10},{14,12},{11,9},... | collective-permute-start | bytes 1179656 | tf_op jit(solution)/shard_map/ppermute | solution.py:485
  10.3 15.7 %collective-permute-start.2 = (bf16[4,2048]{1,0:T(4,128)(2,1)S(1)}, bf16[4,2048]{1,0:T(4,128)(2,1)S(1)}, u32[]{:S(2)}, u32[]{:S(2)}) collective-permute-start(bf16[4,2048]{1,0:T(4,128)(2,1)S(1)} %get-tuple-element.62), channel_id=1, source_target_pairs={{0,1},{1,0},{2,3},{3,2},{4,5},{5,4},{6,7},{7,6},{8,9},{9,8},{10,11... | collective-permute-start | bytes 49160 | tf_op jit(solution)/shard_map/ppermute | solution.py:467
  11.6 32.5 %collective-permute-start.5 = (bf16[80,2048]{1,0:T(8,128)(2,1)S(1)}, bf16[80,2048]{1,0:T(8,128)(2,1)}, u32[]{:S(2)}, u32[]{:S(2)}) collective-permute-start(bf16[80,2048]{1,0:T(8,128)(2,1)S(1)} %get-tuple-element.81.refs_1_), channel_id=1, source_target_pairs={{0,2},{2,4},{4,6},{1,3},{3,5},{5,7},{8,10},{10,12},{12,14},{9,11},... | collective-permute-start | bytes 983048 | tf_op jit(solution)/shard_map/ppermute | solution.py:485
  16.8 28.6 %collective-permute-start.6 = (bf16[80,2048]{1,0:T(8,128)(2,1)S(1)}, bf16[80,2048]{1,0:T(8,128)(2,1)}, u32[]{:S(2)}, u32[]{:S(2)}) collective-permute-start(bf16[80,2048]{1,0:T(8,128)(2,1)S(1)} %get-tuple-element.82.refs_0_), channel_id=1, source_target_pairs={{2,0},{4,2},{6,4},{3,1},{5,3},{7,5},{10,8},{12,10},{14,12},{11,9},... | collective-permute-start | bytes 983048 | tf_op jit(solution)/shard_map/ppermute | solution.py:485
  18.8 10.0 %copy-start.18 = (bf16[192,384]{1,0:T(8,128)(2,1)S(1)}, bf16[192,384]{1,0:T(8,128)(2,1)}, u32[]{:S(2)}) copy-start(bf16[192,384]{1,0:T(8,128)(2,1)} %constant.75.clone.refs_7_) | copy-start | bytes 442372
  26.0 34.8 %copy-start.3 = (bf16[257,128,128]{2,1,0:T(8,128)(2,1)}, bf16[257,128,128]{2,1,0:T(8,128)(2,1)S(1)}, u32[]{:S(2)}) copy-start(bf16[257,128,128]{2,1,0:T(8,128)(2,1)S(1)} %get-tuple-element.78.refs_2_.hk_ref) | copy-start | bytes 25264132
  26.0 39.5 %copy-start = (bf16[257,128,128]{2,1,0:T(8,128)(2,1)}, bf16[257,128,128]{2,1,0:T(8,128)(2,1)S(1)}, u32[]{:S(2)}) copy-start(bf16[257,128,128]{2,1,0:T(8,128)(2,1)S(1)} %get-tuple-element.71.refs_8_.kern_ref) | copy-start | bytes 25264132
  33.3 10.8 %copy-start.9 = (bf16[192,2048]{1,0:T(8,128)(2,1)}, bf16[192,2048]{1,0:T(8,128)(2,1)S(1)}, u32[]{:S(2)}) copy-start(bf16[192,2048]{1,0:T(8,128)(2,1)S(1)} %get-tuple-element.90.act_ref) | copy-start | bytes 2359300
  33.3 18.2 %collective-permute-start.3 = (bf16[1552,128]{1,0:T(8,128)(2,1)S(1)}, bf16[1552,128]{1,0:T(8,128)(2,1)S(1)}, u32[]{:S(2)}, u32[]{:S(2)}) collective-permute-start(bf16[1552,128]{1,0:T(8,128)(2,1)S(1)} %get-tuple-element.72.q0_ref), channel_id=1, source_target_pairs={{0,8},{8,16},{16,24},{24,0},{1,9},{9,17},{17,25},{25,1},{2,10},{10... | collective-permute-start | bytes 1191944 | tf_op jit(solution)/shard_map/ppermute | solution.py:561
  34.9 17.2 %collective-permute-start.4 = (bf16[1552,128]{1,0:T(8,128)(2,1)S(1)}, bf16[1552,128]{1,0:T(8,128)(2,1)S(1)}, u32[]{:S(2)}, u32[]{:S(2)}) collective-permute-start(bf16[1552,128]{1,0:T(8,128)(2,1)S(1)} %get-tuple-element.73.q1_ref), channel_id=1, source_target_pairs={{0,24},{8,0},{16,8},{24,16},{1,25},{9,1},{17,9},{25,17},{2,26},{10... | collective-permute-start | bytes 1191944 | tf_op jit(solution)/shard_map/ppermute | solution.py:562
  37.2 19.8 %collective-permute-start.10 = (bf16[80,2048]{1,0:T(8,128)(2,1)}, bf16[80,2048]{1,0:T(8,128)(2,1)S(1)}, u32[]{:S(2)}, u32[]{:S(2)}) collective-permute-start(bf16[80,2048]{1,0:T(8,128)(2,1)} %get-tuple-element.98.refs_1_), channel_id=1, source_target_pairs={{0,2},{2,4},{4,6},{1,3},{3,5},{5,7},{8,10},{10,12},{12,14},{9,11},... | collective-permute-start | bytes 983048 | tf_op jit(solution)/shard_map/ppermute | solution.py:485
  40.6 4.8 %copy-start.15 = (bf16[160,320]{1,0:T(8,128)(2,1)S(1)}, bf16[160,320]{1,0:T(8,128)(2,1)}, u32[]{:S(2)}) copy-start(bf16[160,320]{1,0:T(8,128)(2,1)} %constant.76.clone.refs_7_) | copy-start | bytes 307204
  44.1 7.4 %copy-start.5 = (bf16[160,2048]{1,0:T(8,128)(2,1)}, bf16[160,2048]{1,0:T(8,128)(2,1)S(1)}, u32[]{:S(2)}) copy-start(bf16[160,2048]{1,0:T(8,128)(2,1)S(1)} %get-tuple-element.79.refs_0_.rows_ref) | copy-start | bytes 1966084
  44.1 21.4 %collective-permute-start.11 = (bf16[80,2048]{1,0:T(8,128)(2,1)}, bf16[80,2048]{1,0:T(8,128)(2,1)S(1)}, u32[]{:S(2)}, u32[]{:S(2)}) collective-permute-start(bf16[80,2048]{1,0:T(8,128)(2,1)} %get-tuple-element.99.refs_0_), channel_id=1, source_target_pairs={{2,0},{4,2},{6,4},{3,1},{5,3},{7,5},{10,8},{12,10},{14,12},{11,9},... | collective-permute-start | bytes 983048 | tf_op jit(solution)/shard_map/ppermute | solution.py:485
  51.5 14.0 %copy-start.11 = (bf16[160,2048]{1,0:T(8,128)(2,1)}, bf16[160,2048]{1,0:T(8,128)(2,1)S(1)}, u32[]{:S(2)}) copy-start(bf16[160,2048]{1,0:T(8,128)(2,1)S(1)} %get-tuple-element.108.act_ref) | copy-start | bytes 1966084
  51.5 14.0 %copy-start.16 = (bf16[1296,128]{1,0:T(8,128)(2,1)}, bf16[1296,128]{1,0:T(8,128)(2,1)S(1)}, u32[]{:S(2)}) copy-start(bf16[1296,128]{1,0:T(8,128)(2,1)S(1)} %get-tuple-element.84.q0_ref) | copy-start | bytes 995332
  51.5 20.0 %collective-permute-start.8 = (bf16[1296,128]{1,0:T(8,128)(2,1)S(1)}, bf16[1296,128]{1,0:T(8,128)(2,1)S(1)}, u32[]{:S(2)}, u32[]{:S(2)}) collective-permute-start(bf16[1296,128]{1,0:T(8,128)(2,1)S(1)} %get-tuple-element.84.q0_ref), channel_id=1, source_target_pairs={{0,8},{8,16},{16,24},{24,0},{1,9},{9,17},{17,25},{25,1},{2,10},{10... | collective-permute-start | bytes 995336 | tf_op jit(solution)/shard_map/ppermute | solution.py:561
  53.7 37.6 %collective-permute-start.7 = (bf16[1536,128]{1,0:T(8,128)(2,1)}, bf16[1536,128]{1,0:T(8,128)(2,1)}, u32[]{:S(2)}, u32[]{:S(2)}) collective-permute-start(bf16[1536,128]{1,0:T(8,128)(2,1)} %get-tuple-element.91), channel_id=1, source_target_pairs={{0,24},{8,0},{16,8},{24,16},{1,25},{9,1},{17,9},{25,17},{2,26},{10... | collective-permute-start | bytes 1179656 | tf_op jit(solution)/shard_map/ppermute | solution.py:569
  57.0 36.4 %collective-permute-start.15 = (bf16[1536,128]{1,0:T(8,128)(2,1)}, bf16[1536,128]{1,0:T(8,128)(2,1)S(1)}, u32[]{:S(2)}, u32[]{:S(2)}) collective-permute-start(bf16[1536,128]{1,0:T(8,128)(2,1)} %get-tuple-element.88), channel_id=1, source_target_pairs={{0,8},{8,16},{16,24},{24,0},{1,9},{9,17},{17,25},{25,1},{2,10},{10... | collective-permute-start | bytes 1179656 | tf_op jit(solution)/shard_map/ppermute | solution.py:568
  57.0 31.5 %collective-permute-start.9 = (bf16[1296,128]{1,0:T(8,128)(2,1)}, bf16[1296,128]{1,0:T(8,128)(2,1)S(1)}, u32[]{:S(2)}, u32[]{:S(2)}) collective-permute-start(bf16[1296,128]{1,0:T(8,128)(2,1)} %get-tuple-element.85.q1_ref), channel_id=1, source_target_pairs={{0,24},{8,0},{16,8},{24,16},{1,25},{9,1},{17,9},{25,17},{2,26},{10... | collective-permute-start | bytes 995336 | tf_op jit(solution)/shard_map/ppermute | solution.py:562
  65.5 5.1 %copy-start.7 = (bf16[160,2048]{1,0:T(8,128)(2,1)}, bf16[160,2048]{1,0:T(8,128)(2,1)S(1)}, u32[]{:S(2)}) copy-start(bf16[160,2048]{1,0:T(8,128)(2,1)S(1)} %get-tuple-element.96.refs_0_.rows_ref) | copy-start | bytes 1966084
  70.6 0.9 copy-start.13
  71.4 33.9 %collective-permute-start.13 = (bf16[1296,128]{1,0:T(8,128)(2,1)}, bf16[1296,128]{1,0:T(8,128)(2,1)S(1)}, u32[]{:S(2)}, u32[]{:S(2)}) collective-permute-start(bf16[1296,128]{1,0:T(8,128)(2,1)} %get-tuple-element.101.q0_ref), channel_id=1, source_target_pairs={{0,8},{8,16},{16,24},{24,0},{1,9},{9,17},{17,25},{25,1},{2,10},{10... | collective-permute-start | bytes 995336 | tf_op jit(solution)/shard_map/ppermute | solution.py:561
  71.5 33.9 %collective-permute-start.14 = (bf16[1296,128]{1,0:T(8,128)(2,1)}, bf16[1296,128]{1,0:T(8,128)(2,1)S(1)}, u32[]{:S(2)}, u32[]{:S(2)}) collective-permute-start(bf16[1296,128]{1,0:T(8,128)(2,1)} %get-tuple-element.102.q1_ref), channel_id=1, source_target_pairs={{0,24},{8,0},{16,8},{24,16},{1,25},{9,1},{17,9},{25,17},{2,26},{10... | collective-permute-start | bytes 995336 | tf_op jit(solution)/shard_map/ppermute | solution.py:562
  75.4 18.0 %copy-start.6 = (bf16[160,2048]{1,0:T(8,128)(2,1)S(1)}, bf16[160,2048]{1,0:T(8,128)(2,1)}, u32[]{:S(2)}) copy-start(bf16[160,2048]{1,0:T(8,128)(2,1)} %copy-done.5) | copy-start | bytes 1966084
  75.4 18.0 %copy-start.12 = (bf16[160,2048]{1,0:T(8,128)(2,1)S(1)}, bf16[160,2048]{1,0:T(8,128)(2,1)}, u32[]{:S(2)}) copy-start(bf16[160,2048]{1,0:T(8,128)(2,1)} %copy-done.11) | copy-start | bytes 1966084
  88.5 1.0 copy-start.17
  91.3 25.8 %collective-permute-start.12 = (bf16[1280,128]{1,0:T(8,128)(2,1)S(1)}, bf16[1280,128]{1,0:T(8,128)(2,1)S(1)}, u32[]{:S(2)}, u32[]{:S(2)}) collective-permute-start(bf16[1280,128]{1,0:T(8,128)(2,1)S(1)} %get-tuple-element.105), channel_id=1, source_target_pairs={{0,24},{8,0},{16,8},{24,16},{1,25},{9,1},{17,9},{25,17},{2,26},{10... | collective-permute-start | bytes 983048 | tf_op jit(solution)/shard_map/ppermute | solution.py:569
  91.4 25.7 %collective-permute-start.17 = (bf16[1280,128]{1,0:T(8,128)(2,1)S(1)}, bf16[1280,128]{1,0:T(8,128)(2,1)S(1)}, u32[]{:S(2)}, u32[]{:S(2)}) collective-permute-start(bf16[1280,128]{1,0:T(8,128)(2,1)S(1)} %get-tuple-element.106), channel_id=1, source_target_pairs={{0,8},{8,16},{16,24},{24,0},{1,9},{9,17},{17,25},{25,1},{2,10},{10... | collective-permute-start | bytes 983048 | tf_op jit(solution)/shard_map/ppermute | solution.py:568
  93.4 3.4 %copy-start.1 = (bf16[257,128,128]{2,1,0:T(8,128)(2,1)S(1)}, bf16[257,128,128]{2,1,0:T(8,128)(2,1)}, u32[]{:S(2)}) copy-start(bf16[257,128,128]{2,1,0:T(8,128)(2,1)} %copy-done) | copy-start | bytes 25264132
  96.8 3.4 %copy-start.4 = (bf16[257,128,128]{2,1,0:T(8,128)(2,1)S(1)}, bf16[257,128,128]{2,1,0:T(8,128)(2,1)}, u32[]{:S(2)}) copy-start(bf16[257,128,128]{2,1,0:T(8,128)(2,1)} %copy-done.3) | copy-start | bytes 25264132
  100.2 11.0 %copy-start.2 = (bf16[257,128,128]{2,1,0:T(8,128)(2,1)S(1)}, bf16[257,128,128]{2,1,0:T(8,128)(2,1)}, u32[]{:S(2)}) copy-start(bf16[257,128,128]{2,1,0:T(8,128)(2,1)} %copy-done) | copy-start | bytes 25264132
  105.3 5.9 %copy-start.10 = (bf16[192,2048]{1,0:T(8,128)(2,1)S(1)}, bf16[192,2048]{1,0:T(8,128)(2,1)}, u32[]{:S(2)}) copy-start(bf16[192,2048]{1,0:T(8,128)(2,1)} %copy-done.9) | copy-start | bytes 2359300
  107.3 15.0 %collective-permute-start.18 = (bf16[1280,128]{1,0:T(8,128)(2,1)S(1)}, bf16[1280,128]{1,0:T(8,128)(2,1)S(1)}, u32[]{:S(2)}, u32[]{:S(2)}) collective-permute-start(bf16[1280,128]{1,0:T(8,128)(2,1)S(1)} %get-tuple-element.112), channel_id=1, source_target_pairs={{0,8},{8,16},{16,24},{24,0},{1,9},{9,17},{17,25},{25,1},{2,10},{10... | collective-permute-start | bytes 983048 | tf_op jit(solution)/shard_map/ppermute | solution.py:568
  108.4 18.5 %collective-permute-start.16 = (bf16[1280,128]{1,0:T(8,128)(2,1)S(1)}, bf16[1280,128]{1,0:T(8,128)(2,1)S(1)}, u32[]{:S(2)}, u32[]{:S(2)}) collective-permute-start(bf16[1280,128]{1,0:T(8,128)(2,1)S(1)} %get-tuple-element.111), channel_id=1, source_target_pairs={{0,24},{8,0},{16,8},{24,16},{1,25},{9,1},{17,9},{25,17},{2,26},{10... | collective-permute-start | bytes 983048 | tf_op jit(solution)/shard_map/ppermute | solution.py:569
  111.2 5.9 %copy-start.8 = (bf16[160,2048]{1,0:T(8,128)(2,1)S(1)}, bf16[160,2048]{1,0:T(8,128)(2,1)}, u32[]{:S(2)}) copy-start(bf16[160,2048]{1,0:T(8,128)(2,1)} %copy-done.7) | copy-start | bytes 1966084
  111.2 5.9 %copy-start.14 = (bf16[160,2048]{1,0:T(8,128)(2,1)S(1)}, bf16[160,2048]{1,0:T(8,128)(2,1)}, u32[]{:S(2)}) copy-start(bf16[160,2048]{1,0:T(8,128)(2,1)} %copy-done.13) | copy-start | bytes 1966084
